TPU v7x, 32 devices: a whole 2x2x4 slice. The times are simulated.
32 devices in a mesh: dp: 8 (over y, x, core), shard: 4 (over z).
Axes of the slice: x: 2, y: 2, z: 4, core: 2. Of those that a mesh axis runs over, the one named last changes fastest.
Arguments:
- x_in: bfloat16 [4096, 1024], P(('dp', 'shard')), may hold values from -6 to 6
- cotangent: float32 [4096, 1024], P(('dp', 'shard')), may hold values from -6 to 6
- params: float32 [12595200], P(('dp', 'shard')), may hold values from -2 to 2
- first_moment: float32 [12595200], P(('dp', 'shard')), may hold values from -6 to 6
- second_moment: float32 [12595200], P(('dp', 'shard')), may hold values from 0.01 to 1
- seq_lengths: int32 [128], replicated, may hold values from 1 to 125, as said below
- seq_device: int32 [128], replicated, may hold values from 0 to 31, as said below
Outputs:
- block_out: float32 [4096, 1024], P(('dp', 'shard'))
- x_grad: float32 [4096, 1024], P(('dp', 'shard'))
- grad_flat: float32 [12595200], P(('dp', 'shard'))
- new_params: float32 [12595200], P(('dp', 'shard'))
- new_first: float32 [12595200], P(('dp', 'shard'))
- new_second: float32 [12595200], P(('dp', 'shard'))
Inputs may be any that keep to these rules, and one draw needn't show every extreme that they name: `seq_lengths`: every device holds exactly 4 sequences of together at most 128 tokens; some device holds exactly 128. `seq_device`: every device index names exactly 4 sequences.
All inputs are finite; a program needn't handle non-finite values.
Results may differ from a plain program's by a relative error of at most 0.024.
The roundings to bfloat16 on the way count: a program that leaves them out, or rounds other values in their place, can miss the bound.
Values may be sent and summed in bfloat16 or wider, within the bound.
No kernel may reach another device: no remote copies, remote signals or barrier semaphores. Data moves between devices by JAX's collectives and lax.ppermute only.
A program may use at most 256 MiB of HBM per device.

v0:
```python
import jax
import jax.numpy as jnp
from jax import lax
from jax.sharding import PartitionSpec as P

D = 1024
HEADS = 16
HEAD_DIM = 64
FF = 4096
STEP = 4


score_scale = 0.125
norm_eps = 1e-05
gelu_coef = 0.7978845608028654
gelu_cubic = 0.044715
learn_rate = 0.01
beta_first = 0.9
beta_second = 0.95
adam_eps = 1e-08
decay_rate = 0.1
neg_large = -1e30


def matmul(left_side, right_side):
    return jnp.dot(left_side, right_side, preferred_element_type=jnp.float32)


def matmul_tn(left_side, right_side):
    return lax.dot_general(
        left_side, right_side, (((0,), (0,)), ((), ())), preferred_element_type=jnp.float32
    )


def matmul_nt(left_side, right_side):
    return lax.dot_general(
        left_side, right_side, (((1,), (1,)), ((), ())), preferred_element_type=jnp.float32
    )


def contract(pattern, left_side, right_side):
    return jnp.einsum(pattern, left_side, right_side, preferred_element_type=jnp.float32)


def normalize(values, norm_gain, norm_shift):
    average = jnp.mean(values, axis=-1, keepdims=True)
    centered = values - average
    inverse = lax.rsqrt(jnp.mean(centered * centered, axis=-1, keepdims=True) + norm_eps)
    scaled = centered * inverse
    return (scaled * norm_gain + norm_shift, scaled, inverse)


def normalize_back(upstream, scaled, inverse, norm_gain):
    grad_scaled = upstream * norm_gain
    term_one = jnp.mean(grad_scaled, axis=-1, keepdims=True)
    term_two = jnp.mean(grad_scaled * scaled, axis=-1, keepdims=True)
    return inverse * (grad_scaled - term_one - scaled * term_two)


def gelu_parts(pre_act):
    inner_arg = gelu_coef * (pre_act + gelu_cubic * pre_act * pre_act * pre_act)
    tanh_val = jnp.tanh(inner_arg)
    act_value = 0.5 * pre_act * (1.0 + tanh_val)
    act_slope = 0.5 * (1.0 + tanh_val) + 0.5 * pre_act * (1.0 - tanh_val * tanh_val) * gelu_coef * (
        1.0 + 3.0 * gelu_cubic * pre_act * pre_act
    )
    return (act_value, act_slope)


def segments(seq_lengths, seq_device, device_ids, row_count):
    owned = seq_device[None, :] == device_ids[:, None]
    own_lengths = jnp.where(owned, seq_lengths[None, :], 0)
    ends = jnp.cumsum(own_lengths, axis=1)
    position = jnp.arange(row_count, dtype=jnp.int32)
    passed = owned[:, None, :] & (ends[:, None, :] <= position[None, :, None])
    seg_ids = jnp.sum(passed.astype(jnp.int32), axis=2)
    live_mask = position[None, :] < ends[:, -1:]
    return (seg_ids, live_mask)


def layer(x_in, cotangent, seg_ids, live_mask, weights):
    qkv_weight, out_weight, up_weight, down_weight, vectors = weights
    vectors = vectors.astype(jnp.float32)
    first_gain = vectors[0]
    first_shift = vectors[1]
    query_bias = vectors[2]
    value_bias = vectors[3]
    out_bias = vectors[4]
    second_gain = vectors[5]
    second_shift = vectors[6]
    up_bias = vectors[7 : 7 + FF // D].reshape(FF)
    down_bias = vectors[7 + FF // D]
    batch_size = x_in.shape[0]
    row_count = x_in.shape[1]
    flat_rows = batch_size * row_count
    head_shape = (batch_size, row_count, HEADS, HEAD_DIM)
    stream = x_in.astype(jnp.float32).reshape(flat_rows, D)
    normed1, scaled1, inverse1 = normalize(stream, first_gain, first_shift)
    normed1 = normed1.astype(jnp.bfloat16)
    mixed_all = matmul(normed1, qkv_weight)
    query_low = (mixed_all[:, :D] + query_bias).astype(jnp.bfloat16).reshape(head_shape)
    key_low = mixed_all[:, D : 2 * D].astype(jnp.bfloat16).reshape(head_shape)
    value_low = (mixed_all[:, 2 * D :] + value_bias).astype(jnp.bfloat16).reshape(head_shape)
    position = jnp.arange(row_count, dtype=jnp.int32)
    allowed = (seg_ids[:, :, None] == seg_ids[:, None, :]) & (
        position[None, :, None] >= position[None, None, :]
    )
    allowed = allowed[:, None, :, :]
    scores = jnp.where(
        allowed, contract("bqhe,bkhe->bhqk", query_low, key_low) * score_scale, neg_large
    )
    row_max = jnp.max(scores, axis=-1, keepdims=True)
    exp_scores = jnp.exp(scores - row_max)
    row_total = jnp.sum(exp_scores, axis=-1, keepdims=True)
    probability = exp_scores / row_total
    log_total = row_max + jnp.log(row_total)
    attended = contract("bhqk,bkhe->bqhe", probability.astype(jnp.bfloat16), value_low)
    attended = attended.astype(jnp.bfloat16).reshape(flat_rows, D)
    residual = stream + matmul(attended, out_weight) + out_bias
    normed2, scaled2, inverse2 = normalize(residual, second_gain, second_shift)
    normed2 = normed2.astype(jnp.bfloat16)
    pre_act = matmul(normed2, up_weight) + up_bias
    act_value, act_slope = gelu_parts(pre_act)
    hidden = act_value.astype(jnp.bfloat16)
    output = residual + matmul(hidden, down_weight) + down_bias
    upstream = cotangent.reshape(flat_rows, D) * live_mask.reshape(flat_rows, 1).astype(jnp.float32)
    up_low = upstream.astype(jnp.bfloat16)
    grad_down = matmul_tn(hidden, up_low)
    grad_pre = matmul_nt(up_low, down_weight) * act_slope
    pre_low = grad_pre.astype(jnp.bfloat16)
    grad_up = matmul_tn(normed2, pre_low)
    grad_normed2 = matmul_nt(pre_low, up_weight)
    grad_residual = upstream + normalize_back(grad_normed2, scaled2, inverse2, second_gain)
    res_low = grad_residual.astype(jnp.bfloat16)
    grad_out = matmul_tn(attended, res_low)
    grad_attended = matmul_nt(res_low, out_weight).astype(jnp.bfloat16).reshape(head_shape)
    scores = jnp.where(
        allowed, contract("bqhe,bkhe->bhqk", query_low, key_low) * score_scale, neg_large
    )
    probability = jnp.where(allowed, jnp.exp(scores - log_total), 0.0)
    grad_prob = contract("bqhe,bkhe->bhqk", grad_attended, value_low)
    grad_values = contract("bhqk,bqhe->bkhe", probability.astype(jnp.bfloat16), grad_attended)
    row_dot = jnp.sum(probability * grad_prob, axis=-1, keepdims=True)
    score_low = (probability * (grad_prob - row_dot)).astype(jnp.bfloat16)
    grad_queries = contract("bhqk,bkhe->bqhe", score_low, key_low) * score_scale
    grad_keys = contract("bhqk,bqhe->bkhe", score_low, query_low) * score_scale
    grad_queries = grad_queries.reshape(flat_rows, D)
    grad_keys = grad_keys.reshape(flat_rows, D)
    grad_values = grad_values.reshape(flat_rows, D)
    mixed_low = jnp.concatenate([grad_queries, grad_keys, grad_values], axis=1).astype(jnp.bfloat16)
    grad_qkv = matmul_tn(normed1, mixed_low)
    grad_normed1 = matmul_nt(mixed_low, qkv_weight)
    grad_input = grad_residual + normalize_back(grad_normed1, scaled1, inverse1, first_gain)
    head_rows = jnp.stack(
        [
            jnp.sum(grad_normed1 * scaled1, axis=0),
            jnp.sum(grad_normed1, axis=0),
            jnp.sum(grad_queries, axis=0),
            jnp.sum(grad_values, axis=0),
            jnp.sum(grad_residual, axis=0),
            jnp.sum(grad_normed2 * scaled2, axis=0),
            jnp.sum(grad_normed2, axis=0),
        ]
    )
    grad_vectors = jnp.concatenate(
        [
            head_rows,
            jnp.sum(grad_pre, axis=0).reshape(FF // D, D),
            jnp.sum(upstream, axis=0)[None, :],
        ],
        axis=0,
    )
    grads = (grad_qkv, grad_out, grad_up, grad_down, grad_vectors)
    return (
        output.reshape(batch_size, row_count, D),
        grad_input.reshape(batch_size, row_count, D),
        grads,
    )


def local_pieces(flat_slice, share):
    vec_rows = 8 + FF // D
    widths = [share * 3 * D, share * D, share * FF, share * FF, vec_rows * share]
    pieces = []
    offset = 0
    for extent in widths:
        pieces.append(lax.slice_in_dim(flat_slice, offset, offset + extent))
        offset = offset + extent
    return (
        pieces[0].reshape(share, 3 * D),
        pieces[1].reshape(share, D),
        pieces[2].reshape(share, FF),
        pieces[3].reshape(share * FF // D, D),
        pieces[4].reshape(vec_rows, share),
    )


def body(x_in, cotangent, params, first_moment, second_moment, seq_lengths, seq_device):
    devices = lax.axis_size("dp") * lax.axis_size("shard")
    share = D // devices
    params_low = params.astype(jnp.bfloat16)
    qkv_part, out_part, up_part, down_part, vec_part = local_pieces(params_low, share)
    weights = (
        lax.all_gather(qkv_part, ("dp", "shard"), axis=0, tiled=True),
        lax.all_gather(out_part, ("dp", "shard"), axis=0, tiled=True),
        lax.all_gather(up_part, ("dp", "shard"), axis=0, tiled=True),
        lax.all_gather(down_part, ("dp", "shard"), axis=0, tiled=True),
        lax.all_gather(vec_part, ("dp", "shard"), axis=1, tiled=True),
    )
    device = lax.axis_index(("dp", "shard"))
    device_ids = jnp.reshape(device, (1,))
    seg_ids, live_mask = segments(seq_lengths, seq_device, device_ids, x_in.shape[0])
    output, grad_input, grads = layer(
        x_in[None], cotangent[None], seg_ids, live_mask, tuple(weights)
    )
    owned_parts = (
        lax.psum_scatter(grads[0], ("dp", "shard"), scatter_dimension=0, tiled=True),
        lax.psum_scatter(grads[1], ("dp", "shard"), scatter_dimension=0, tiled=True),
        lax.psum_scatter(grads[2], ("dp", "shard"), scatter_dimension=0, tiled=True),
        lax.psum_scatter(grads[3], ("dp", "shard"), scatter_dimension=0, tiled=True),
        lax.psum_scatter(grads[4], ("dp", "shard"), scatter_dimension=1, tiled=True),
    )
    owned = jnp.concatenate([piece.reshape(-1) for piece in owned_parts])
    per_device = owned.shape[0]
    local_index = jnp.arange(per_device, dtype=jnp.int32)
    matrix_mask = (local_index < share * (4 * D + 2 * FF)).astype(jnp.float32)
    new_first = beta_first * first_moment + (1.0 - beta_first) * owned
    new_second = beta_second * second_moment + (1.0 - beta_second) * owned * owned
    fix_first = 1.0 - beta_first**STEP
    fix_second = 1.0 - beta_second**STEP
    ratio = new_first / fix_first / (jnp.sqrt(new_second / fix_second) + adam_eps)
    new_params = params - learn_rate * (ratio + decay_rate * matrix_mask * params)
    return (output[0], grad_input[0], owned, new_params, new_first, new_second)


def solution(mesh):
    return jax.shard_map(
        body,
        mesh=mesh,
        in_specs=(
            P(("dp", "shard"), None),
            P(("dp", "shard"), None),
            P(("dp", "shard")),
            P(("dp", "shard")),
            P(("dp", "shard")),
            P(),
            P(),
        ),
        out_specs=(
            P(("dp", "shard"), None),
            P(("dp", "shard"), None),
            P(("dp", "shard")),
            P(("dp", "shard")),
            P(("dp", "shard")),
            P(("dp", "shard")),
        ),
        check_vma=False,
    )
```

profile of v0, /device:TPU:0, one launch (start us, length us, event | category | flops | bytes accessed | tf_op | source)
XLA Modules:
  0.0 1505.2 jit_solution(13113257212016509975)
XLA Ops:
  7.2 1.5 convert_element_type.81
  8.8 0.8 reshape.357
  9.6 0.7 reshape.362
  10.4 0.8 reshape.363
  11.3 0.8 reshape.364
  12.2 0.3 reduce_window_sum.11
  12.5 0.6 slice.83
  13.1 0.1 slice.66
  13.2 72.2 %all-gather = bf16[32,32,12]{1,2,0:T(8,128)(2,1)S(1)} all-gather(bf16[1,32,12]{1,2,0:T(8,128)(2,1)S(1)} %bitcast.132), channel_id=1, replica_groups=mesh['dp'=8,'shard'=4] {'dp','shard'}, dimensions={0}, use_global_device_ids=true | all-gather | bytes 25344 | tf_op jit(solution)/shard_map/all_gather | solution.py:208
  85.4 0.1 reshape.377
  85.6 0.7 compare_convert_fusion
  86.2 0.1 convert_reduce_fusion.1
  86.3 0.1 convert_reduce_fusion
  86.5 0.2 fusion.26
  86.7 0.1 fusion.43
  86.9 3.9 fusion.49
  90.8 0.1 fusion.28
  90.9 0.2 copy.62
  91.1 0.2 copy.63
  91.3 0.2 copy.61
  91.4 0.4 fusion.57
  91.8 0.2 fusion.11
  92.0 0.3 convolution_convert_fusion.1
  92.3 50.0 %all-gather.8.cloned.1.call-done = bf16[1024,1024]{1,0:T(8,128)(2,1)} async-done(((bf16[32,1024]{1,0:T(8,128)(2,1)}), bf16[1024,1024]{1,0:T(8,128)(2,1)}) %all-gather.8.cloned.1.call-update) | async-done | bytes 2097168 | tf_op jit(solution)/shard_map/all_gather | solution.py:205
  142.3 2.1 fusion.58
  144.4 0.2 multiply_reduce_fusion.3
  144.7 77.1 %all-gather.10.cloned.1.call-done = bf16[1024,4096]{1,0:T(8,128)(2,1)} async-done(((bf16[32,4096]{1,0:T(8,128)(2,1)}), bf16[1024,4096]{1,0:T(8,128)(2,1)}) %all-gather.10.cloned.1.call-update) | async-done | bytes 8388624 | tf_op jit(solution)/shard_map/all_gather | solution.py:206
  221.8 6.1 convolution_add_fusion
  227.9 73.0 %all-gather.12.cloned.1.call-done = bf16[4096,1024]{1,0:T(8,128)(2,1)} async-done(((bf16[128,1024]{1,0:T(8,128)(2,1)}), bf16[4096,1024]{1,0:T(8,128)(2,1)}) %all-gather.12.cloned.1.call-update) | async-done | bytes 8388624 | tf_op jit(solution)/shard_map/all_gather | solution.py:207
  300.9 7.7 fusion.59
  308.5 3.0 multiply_reduce_fusion.1
  311.6 0.3 fusion.52
  311.9 1.3 copy-done.3
  313.2 0.8 convolution_convert_fusion
  314.0 0.2 copy.65
  314.2 0.6 fusion.54
  314.8 1.4 multiply_reduce_fusion
  316.1 0.3 multiply_convert_fusion.1
  316.4 0.5 fusion.10
  316.9 0.5 fusion.55
  317.6 5.9 fusion.25
  323.5 0.2 concatenate.11
  323.6 1.0 copy.73
  324.8 2.6 fusion.39
  327.5 6.4 fusion.37
  334.0 1.5 copy-done.2
  335.5 9.2 fusion.47
  344.7 0.3 reduce-scatter.12.cloned.1.call-start
  345.0 9.4 fusion.32
  354.4 2.1 fusion.24
  356.5 5.7 fusion.9
  362.2 97.5 %reduce-scatter.16.cloned.1.call-done = f32[32,12]{1,0:T(8,128)} async-done(((f32[1024,12]{1,0:T(8,128)}), f32[32,12]{1,0:T(8,128)}) %reduce-scatter.16.cloned.1.call-update) | async-done | bytes 1552
  459.7 0.8 copy.74
  460.5 0.1 reshape.374
  460.5 145.8 %reduce-scatter.10.cloned.1.call-done = f32[32,1024]{1,0:T(8,128)} async-done(((f32[1024,1024]{1,0:T(8,128)}), f32[32,1024]{1,0:T(8,128)}) %reduce-scatter.10.cloned.1.call-update) | async-done | bytes 131088 | tf_op jit(solution)/shard_map/reduce_scatter | solution.py:218
  606.4 0.9 copy.77
  607.3 158.6 %reduce-scatter.8.cloned.1.call-done = f32[32,3072]{1,0:T(8,128)} async-done(((f32[1024,3072]{1,0:T(8,128)}), f32[32,3072]{1,0:T(8,128)}) %reduce-scatter.8.cloned.1.call-update) | async-done | bytes 393232 | tf_op jit(solution)/shard_map/reduce_scatter | solution.py:217
  765.9 1.1 copy.76
  767.0 360.7 %reduce-scatter.14.cloned.1.call-done = f32[128,1024]{1,0:T(8,128)} async-done(((f32[4096,1024]{1,0:T(8,128)}), f32[128,1024]{1,0:T(8,128)}) %reduce-scatter.14.cloned.1.call-update) | async-done | bytes 524304 | tf_op jit(solution)/shard_map/reduce_scatter | solution.py:220
  1127.8 2.0 copy.79
  1129.8 362.2 %reduce-scatter.12.cloned.1.call-done = f32[32,4096]{1,0:T(8,128)} async-done(((f32[1024,4096]{1,0:T(8,128)}), f32[32,4096]{1,0:T(8,128)}) %reduce-scatter.12.cloned.1.call-update) | async-done | bytes 524304 | tf_op jit(solution)/shard_map/reduce_scatter | solution.py:219
  1492.0 1.3 copy.78
  1493.4 0.3 copy-done.9
  1493.7 5.0 multiply_subtract_fusion
  (71 shorter events, 1.1 us)
Async XLA Ops:
  7.2 79.7 %all-gather.6.cloned.1.call-start = ((), (), s32[]{:S(2)}) async-start(), calls=%async_computation.5 | async-start | bytes 6488064 | tf_op jit(solution)/shard_map/all_gather | solution.py:204
  8.7 3.5 copy-start.13
  8.7 3.5 copy-start.14
  9.5 76.8 %copy-start.1 = (bf16[128,1024]{1,0:T(8,128)(2,1)S(1)}, bf16[128,1024]{1,0:T(8,128)(2,1)}, u32[]{:S(2)}) copy-start(bf16[128,1024]{1,0:T(8,128)(2,1)} %param.7) | copy-start | bytes 786436
  9.5 132.7 %all-gather.8.cloned.1.call-start = ((), (), s32[]{:S(2)}) async-start(), calls=%async_computation.6 | async-start | bytes 2162688 | tf_op jit(solution)/shard_map/all_gather | solution.py:205
  10.3 211.5 %all-gather.10.cloned.1.call-start = ((), (), s32[]{:S(2)}) async-start(), calls=%async_computation.7 | async-start | bytes 8650752 | tf_op jit(solution)/shard_map/all_gather | solution.py:206
  11.2 289.6 %all-gather.12.cloned.1.call-start = ((), (), s32[]{:S(2)}) async-start(), calls=%async_computation.8 | async-start | bytes 8650752 | tf_op jit(solution)/shard_map/all_gather | solution.py:207
  12.1 447.6 %reduce-scatter.16.cloned.1.call-start = ((), (), s32[]{:S(2)}) async-start(), calls=%async_computation.13 | async-start | bytes 540672
  91.4 0.9 copy-start.12
  92.3 135.6 %copy-start.10 = (bf16[16,64,128]{2,1,0:T(8,128)(2,1)}, bf16[16,64,128]{2,1,0:T(8,128)(2,1)S(1)}, u32[]{:S(2)}) copy-start(bf16[16,64,128]{2,1,0:T(8,128)(2,1)S(1)} %convolution_convert_fusion.1) | copy-start | bytes 786436
  221.8 79.1 %copy-start.7 = (f32[128,1024]{1,0:T(8,128)S(1)}, f32[128,1024]{1,0:T(8,128)}, u32[]{:S(2)}) copy-start(f32[128,1024]{1,0:T(8,128)} %param.8) | copy-start | bytes 1572868
  300.9 7.7 copy-start
  308.5 3.0 copy-start.5
  311.6 1.6 copy-start.3
  317.6 7.1 copy-start.11
  324.7 281.7 %reduce-scatter.10.cloned.1.call-start = ((), (), s32[]{:S(2)}) async-start(), calls=%async_computation.10 | async-start | bytes 4325376 | tf_op jit(solution)/shard_map/reduce_scatter | solution.py:218
  327.4 438.5 %reduce-scatter.8.cloned.1.call-start = ((), (), s32[]{:S(2)}) async-start(), calls=%async_computation.9 | async-start | bytes 12976128 | tf_op jit(solution)/shard_map/reduce_scatter | solution.py:217
  333.9 1.6 copy-start.2
  333.9 793.8 %reduce-scatter.14.cloned.1.call-start = ((), (), s32[]{:S(2)}) async-start(), calls=%async_computation.12 | async-start | bytes 17301504 | tf_op jit(solution)/shard_map/reduce_scatter | solution.py:220
  344.7 1147.3 %reduce-scatter.12.cloned.1.call-start = ((), (), s32[]{:S(2)}) async-start(), calls=%async_computation.11 | async-start | bytes 17301504 | tf_op jit(solution)/shard_map/reduce_scatter | solution.py:219
  1127.8 365.6 %copy-start.4 = (f32[393600]{0:T(1024)S(1)}, f32[393600]{0:T(1024)}, u32[]{:S(2)}) copy-start(f32[393600]{0:T(1024)} %param.9) | copy-start | bytes 4723204
  1492.0 1.3 copy-start.8
  1492.0 1.7 copy-start.9
  1493.7 5.0 copy-start.6
Sparse Core Ops, SparseCore 0:
  11.4 72.1 all-gather.5
  87.2 55.0 all-gather.7
  145.8 75.9 all-gather.9
  225.1 75.6 all-gather.11
  324.8 134.8 reduce-scatter.15
  461.8 144.5 reduce-scatter.9
  612.4 153.4 reduce-scatter.7
  768.2 359.5 reduce-scatter.13
  1130.1 361.8 reduce-scatter.11
where the time goes:
time: 1510 us
  waiting for transfers between devices  1320 us (87%)
  blocking collectives  72.2 us (5%)
  matrix products  66.5 us (4%)
  local copies, waits for them, and re-layouts  15.5 us (1%)
    reduce_scatter x1, waiting for transfers between devices, body(): lax.psum_scatter(grads[2], ('dp', 'shard'), scatter_dimension=0, tiled=True)  362 us
    reduce_scatter x1, waiting for transfers between devices, body(): lax.psum_scatter(grads[3], ('dp', 'shard'), scatter_dimension=0, tiled=True)  361 us
    reduce_scatter x1, waiting for transfers between devices, body(): lax.psum_scatter(grads[0], ('dp', 'shard'), scatter_dimension=0, tiled=True)  159 us
    reduce_scatter x1, waiting for transfers between devices, body(): lax.psum_scatter(grads[1], ('dp', 'shard'), scatter_dimension=0, tiled=True)  146 us
    unnamed x10, waiting for transfers between devices  97.6 us
    all_gather x1, waiting for transfers between devices, body(): lax.all_gather(up_part, ('dp', 'shard'), axis=0, tiled=True)  77.1 us
    all_gather x1, waiting for transfers between devices, body(): lax.all_gather(down_part, ('dp', 'shard'), axis=0, tiled=True)  73 us
    all_gather x1, blocking collectives, body(): lax.all_gather(vec_part, ('dp', 'shard'), axis=1, tiled=True)  72.2 us
  transfers between devices with their start and end apart: 9, of which 8 were waited for; matrix products, arithmetic and copies ran while one was open for 4% of the time, Pallas kernels for 0%

commit v1 on v0

--- a/solution.py
+++ b/solution.py
@@ -1,6 +1,9 @@
 import jax
 import jax.numpy as jnp
 from jax import lax
+from jax.experimental import pallas as pl
+from jax.experimental.pallas import tpu as pltpu
+from jax.sharding import Mesh
 from jax.sharding import PartitionSpec as P
 
 D = 1024
@@ -195,6 +198,18 @@
     )
 
 
+def adam(params, first_moment, second_moment, owned, share):
+    local_index = jnp.arange(owned.shape[0], dtype=jnp.int32)
+    matrix_mask = (local_index < share * (4 * D + 2 * FF)).astype(jnp.float32)
+    new_first = beta_first * first_moment + (1.0 - beta_first) * owned
+    new_second = beta_second * second_moment + (1.0 - beta_second) * owned * owned
+    fix_first = 1.0 - beta_first**STEP
+    fix_second = 1.0 - beta_second**STEP
+    ratio = new_first / fix_first / (jnp.sqrt(new_second / fix_second) + adam_eps)
+    new_params = params - learn_rate * (ratio + decay_rate * matrix_mask * params)
+    return (new_params, new_first, new_second)
+
+
 def body(x_in, cotangent, params, first_moment, second_moment, seq_lengths, seq_device):
     devices = lax.axis_size("dp") * lax.axis_size("shard")
     share = D // devices
@@ -221,38 +236,464 @@
         lax.psum_scatter(grads[4], ("dp", "shard"), scatter_dimension=1, tiled=True),
     )
     owned = jnp.concatenate([piece.reshape(-1) for piece in owned_parts])
-    per_device = owned.shape[0]
-    local_index = jnp.arange(per_device, dtype=jnp.int32)
-    matrix_mask = (local_index < share * (4 * D + 2 * FF)).astype(jnp.float32)
-    new_first = beta_first * first_moment + (1.0 - beta_first) * owned
-    new_second = beta_second * second_moment + (1.0 - beta_second) * owned * owned
-    fix_first = 1.0 - beta_first**STEP
-    fix_second = 1.0 - beta_second**STEP
-    ratio = new_first / fix_first / (jnp.sqrt(new_second / fix_second) + adam_eps)
-    new_params = params - learn_rate * (ratio + decay_rate * matrix_mask * params)
+    new_params, new_first, new_second = adam(params, first_moment, second_moment, owned, share)
     return (output[0], grad_input[0], owned, new_params, new_first, new_second)
 
+SWAP = ((0, 1), (1, 0))
+TEAM = ("x", "c")
+LOW = jnp.bfloat16
+TOK = 512
+ROW = 128
+
+
+def swap(values, axis):
+    return lax.ppermute(values, axis, SWAP)
+
+
+def z_gather(shard):
+    return lax.all_gather(shard, "z", axis=0, tiled=True)
+
+
+def z_reduce(values):
+    return lax.psum_scatter(values, "z", scatter_dimension=0, tiled=True)
+
+
+def team_exchange(values):
+    return lax.all_to_all(values, TEAM, 0, 0, tiled=True)
+
+
+def team_gather(own):
+    near = swap(own, "x")
+    return (own, near, swap(own, "c"), swap(near, "c"))
+
+
+def team_reduce(keep, send):
+    summed = keep + swap(send, "c")
+    return (summed[:ROW], swap(summed[ROW:].astype(LOW), "x"))
+
+
+def sds(shape, dtype=jnp.float32):
+    return jax.ShapeDtypeStruct(shape, dtype)
+
+
+def call(kernel, name, outs, operands, scratch=()):
+    specs = [pl.BlockSpec(memory_space=pltpu.SMEM)] + [
+        pl.BlockSpec(memory_space=pltpu.VMEM) for _ in operands[1:]
+    ]
+    return pl.pallas_call(
+        kernel,
+        out_shape=outs,
+        in_specs=specs,
+        out_specs=tuple(pl.BlockSpec(memory_space=pltpu.VMEM) for _ in outs),
+        scratch_shapes=scratch,
+        name=name,
+        compiler_params=pltpu.CompilerParams(vmem_limit_bytes=48 << 20),
+    )(*operands)
+
+
+def head_lanes():
+    return lax.broadcasted_iota(jnp.int32, (ROW, 128), 1) < HEAD_DIM
+
+
+def lane_group(rows):
+    return lax.broadcasted_iota(jnp.int32, (rows, 128), 1) // 32
+
+
+def allowed_block(seg_col, seg_row, block):
+    query_at = lax.broadcasted_iota(jnp.int32, (ROW, ROW), 0)
+    key_at = lax.broadcasted_iota(jnp.int32, (ROW, ROW), 1)
+    return (seg_col[block * ROW : (block + 1) * ROW, :] == seg_row[block : block + 1, :]) & (
+        query_at >= key_at
+    )
+
+
+def scores_of(query_low, key_low, allowed):
+    return jnp.where(allowed, matmul_nt(query_low, key_low) * score_scale, neg_large)
+
+
+def forward_kernel(
+    at, x_ref, own_ref, far_ref, out_own, out_far, seg_col, seg_row,
+    vec_ref, weight_ref, out_ref, normed_ref, qkv_ref, att_ref, keep_ref, send_ref,
+):
+    y_pos, team = at[0], at[1]
+    group = lane_group(16)
+    for ref, out_part, side in ((own_ref, out_own, y_pos), (far_ref, out_far, 1 - y_pos)):
+        base = side * 512
+        for z in range(4):
+            for t in range(4):
+                start = pl.multiple_of(base + t * 128 + z * 32, 32)
+                weight_ref[pl.ds(start, 32), :] = ref[z, t * 32 : (t + 1) * 32, :]
+        for t in range(4):
+            tile = jnp.zeros((16, 128), jnp.float32)
+            for z in range(4):
+                piece = ref[z, 128:144, 0:128].astype(jnp.float32)
+                shift = (z - t) * 32 % 128
+                piece = pltpu.roll(piece, shift, 1) if shift else piece
+                tile = jnp.where(group == z, piece, tile)
+            vec_ref[:, pl.ds(pl.multiple_of(base + t * 128, 128), 128)] = tile
+        out_ref[pl.ds(pl.multiple_of(side * 128, 128), 128), :] = out_part[...]
+    gain, shift_row = vec_ref[0:1, :], vec_ref[1:2, :]
+    for block in range(4):
+        rows = slice(block * ROW, (block + 1) * ROW)
+        value, _, _ = normalize(x_ref[rows, :].astype(jnp.float32), gain, shift_row)
+        normed_ref[rows, :] = value.astype(LOW)
+    for block in range(4):
+        rows = slice(block * ROW, (block + 1) * ROW)
+        mixed = matmul(normed_ref[rows, :], weight_ref[...])
+        for pair in range(2):
+            lanes = pl.ds(pl.multiple_of(pair * 512 + team * 128, 128), 128)
+            for which in range(3):
+                cols = slice(which * 256 + pair * 128, which * 256 + (pair + 1) * 128)
+                piece = mixed[:, cols]
+                if which == 0:
+                    piece = piece + vec_ref[2:3, lanes]
+                if which == 2:
+                    piece = piece + vec_ref[3:4, lanes]
+                qkv_ref[rows, cols] = piece.astype(LOW)
+    first = head_lanes()
+    for block in range(4):
+        rows = slice(block * ROW, (block + 1) * ROW)
+        allowed = allowed_block(seg_col, seg_row, block)
+        for pair in range(2):
+            query, key, value = (
+                qkv_ref[rows, w * 256 + pair * 128 : w * 256 + (pair + 1) * 128] for w in range(3)
+            )
+            heads = []
+            for mask in (first, ~first):
+                scores = scores_of(jnp.where(mask, query, jnp.zeros_like(query)), key, allowed)
+                row_max = jnp.max(scores, axis=-1, keepdims=True)
+                exp_scores = jnp.exp(scores - row_max)
+                row_total = jnp.sum(exp_scores, axis=-1, keepdims=True)
+                heads.append(matmul((exp_scores / row_total).astype(LOW), value))
+            att_ref[rows, pair * 128 : (pair + 1) * 128] = jnp.where(first, heads[0], heads[1]).astype(LOW)
+    keep_ref[...] = matmul(att_ref[0:256, :], out_ref[...])
+    send_ref[...] = matmul(att_ref[256:512, :], out_ref[...])
+
+
+def residual_kernel(at, x_ref, sum_ref, near_ref, vec_ref, res_ref, low_ref):
+    total = sum_ref[...] + near_ref[...].astype(jnp.float32)
+    residual = x_ref[...].astype(jnp.float32) + total + vec_ref[4:5, :]
+    res_ref[...] = residual
+    value, _, _ = normalize(residual, vec_ref[5:6, :], vec_ref[6:7, :])
+    low_ref[...] = value.astype(LOW)
+
+
+def up_kernel(
+    at, n0, n1, n2, n3, own_ref, far_ref, bias_ref, uplow_ref,
+    team_ref, weight_ref, hidden_ref, slope_ref, mine_ref, theirs_ref, grad_ref,
+):
+    y_pos = at[0]
+    for block, ref in enumerate((n0, n1, n2, n3)):
+        team_ref[block * ROW : (block + 1) * ROW, :] = ref[...]
+    for ref, side in ((own_ref, y_pos), (far_ref, 1 - y_pos)):
+        for z in range(4):
+            for t in range(4):
+                start = pl.multiple_of(side * 512 + t * 128 + z * 32, 32)
+                weight_ref[pl.ds(start, 32), :] = ref[z, t * 32 : (t + 1) * 32, :]
+    for block in range(4):
+        rows = slice(block * ROW, (block + 1) * ROW)
+        pre_act = matmul(team_ref[rows, :], weight_ref[...]) + bias_ref[...]
+        act_value, act_slope = gelu_parts(pre_act)
+        hidden_ref[rows, :] = act_value.astype(LOW)
+        slope_ref[rows, :] = act_slope
+    grad_ref[...] = matmul_tn(hidden_ref[...], uplow_ref[...])
+    mine_ref[...] = grad_ref[pl.ds(pl.multiple_of(y_pos * 512, 512), 512), :]
+    theirs_ref[...] = grad_ref[pl.ds(pl.multiple_of((1 - y_pos) * 512, 512), 512), :].astype(LOW)
+
+
+def down_kernel(
+    at, uplow_ref, own_ref, far_ref, slope_ref, weight_ref,
+    pre_ref, sum_ref, keep_ref, send_ref,
+):
+    y_pos = at[0]
+    sum_ref[...] = jnp.zeros_like(sum_ref)
+    for ref, side in ((own_ref, y_pos), (far_ref, 1 - y_pos)):
+        cols = pl.ds(pl.multiple_of(side * 512, 512), 512)
+        for block in range(4):
+            rows = slice(block * ROW, (block + 1) * ROW)
+            grad_pre = matmul_nt(uplow_ref[rows, :], ref[...]) * slope_ref[rows, cols]
+            pre_ref[rows, cols] = grad_pre.astype(LOW)
+            sum_ref[0:1, cols] += jnp.sum(grad_pre, axis=0, keepdims=True)
+    keep_ref[...] = matmul_nt(pre_ref[0:256, :], weight_ref[...])
+    send_ref[...] = matmul_nt(pre_ref[256:512, :], weight_ref[...])
+
+
+def spread(at, grad_ref, mine_ref, theirs_ref):
+    y_pos = at[0]
+    for z in range(4):
+        for t in range(4):
+            near = pl.multiple_of(y_pos * 512 + t * 128 + z * 32, 32)
+            away = pl.multiple_of((1 - y_pos) * 512 + t * 128 + z * 32, 32)
+            mine_ref[z, t * 32 : (t + 1) * 32, :] = grad_ref[pl.ds(near, 32), :]
+            theirs_ref[z, t * 32 : (t + 1) * 32, :] = grad_ref[pl.ds(away, 32), :].astype(LOW)
+
+
+def up_grad_kernel(at, team_ref, pre_ref, mine_ref, theirs_ref, grad_ref):
+    grad_ref[...] = matmul_tn(team_ref[...], pre_ref[...])
+    spread(at, grad_ref, mine_ref, theirs_ref)
+
+
+def output_kernel(at, hidden_ref, own_ref, far_ref, keep_ref, send_ref):
+    y_pos = at[0]
+    near = pl.ds(pl.multiple_of(y_pos * 512, 512), 512)
+    away = pl.ds(pl.multiple_of((1 - y_pos) * 512, 512), 512)
+    for ref, base in ((keep_ref, 0), (send_ref, 256)):
+        rows = slice(base, base + 256)
+        ref[...] = matmul(hidden_ref[rows, near], own_ref[...]) + matmul(hidden_ref[rows, away], far_ref[...])
+
+
+def residual_back_kernel(
+    at, res_ref, sum_ref, near_ref, up_ref, vec_ref, grad_ref, low_ref, rows_ref
+):
+    _, scaled, inverse = normalize(res_ref[...], vec_ref[5:6, :], vec_ref[6:7, :])
+    grad_normed = sum_ref[...] + near_ref[...].astype(jnp.float32)
+    upstream = up_ref[...]
+    grad = upstream + normalize_back(grad_normed, scaled, inverse, vec_ref[5:6, :])
+    grad_ref[...] = grad
+    low_ref[...] = grad.astype(LOW)
+    total = lambda value: jnp.sum(value, axis=0, keepdims=True)
+    rows_ref[...] = jnp.zeros_like(rows_ref)
+    rows_ref[0:1, :] = total(grad)
+    rows_ref[1:2, :] = total(grad_normed * scaled)
+    rows_ref[2:3, :] = total(grad_normed)
+    rows_ref[3:4, :] = total(upstream)
+
+
+def out_grad_kernel(at, r0, r1, r2, r3, att_ref, team_ref, mine_ref, theirs_ref, grad_ref):
+    y_pos = at[0]
+    for block, ref in enumerate((r0, r1, r2, r3)):
+        team_ref[block * ROW : (block + 1) * ROW, :] = ref[...]
+    grad_ref[...] = matmul_tn(att_ref[...], team_ref[...])
+    mine_ref[...] = grad_ref[pl.ds(pl.multiple_of(y_pos * 128, 128), 128), :]
+    theirs_ref[...] = grad_ref[pl.ds(pl.multiple_of((1 - y_pos) * 128, 128), 128), :].astype(LOW)
+
+
+def backward_kernel(
+    at, team_ref, out_ref, qkv_ref, normed_ref, x_ref, weight_ref, seg_col, seg_row, rows_ref,
+    mine_ref, theirs_ref, keep_ref, send_ref,
+    mixed_ref, grad_ref, att_ref, vec_ref,
+):
+    y_pos, team = at[0], at[1]
+    att_ref[...] = matmul_nt(team_ref[...], out_ref[...]).astype(LOW)
+    vec_ref[...] = rows_ref[...]
+    first = head_lanes()
+    for pair in range(2):
+        query_sum = jnp.zeros((1, 128), jnp.float32)
+        value_sum = jnp.zeros((1, 128), jnp.float32)
+        for block in range(4):
+            rows = slice(block * ROW, (block + 1) * ROW)
+            allowed = allowed_block(seg_col, seg_row, block)
+            query, key, value = (
+                qkv_ref[rows, w * 256 + pair * 128 : w * 256 + (pair + 1) * 128] for w in range(3)
+            )
+            grad_att = att_ref[rows, pair * 128 : (pair + 1) * 128]
+            parts = []
+            for mask in (first, ~first):
+                scores = scores_of(jnp.where(mask, query, jnp.zeros_like(query)), key, allowed)
+                row_max = jnp.max(scores, axis=-1, keepdims=True)
+                log_total = row_max + jnp.log(jnp.sum(jnp.exp(scores - row_max), axis=-1, keepdims=True))
+                probability = jnp.where(allowed, jnp.exp(scores - log_total), 0.0)
+                grad_prob = matmul_nt(jnp.where(mask, grad_att, jnp.zeros_like(grad_att)), value)
+                grad_value = matmul_tn(probability.astype(LOW), grad_att)
+                row_dot = jnp.sum(probability * grad_prob, axis=-1, keepdims=True)
+                score_low = (probability * (grad_prob - row_dot)).astype(LOW)
+                parts.append(
+                    (matmul(score_low, key) * score_scale, matmul_tn(score_low, query) * score_scale, grad_value)
+                )
+            for which in range(3):
+                merged = jnp.where(first, parts[0][which], parts[1][which])
+                mixed_ref[rows, which * 256 + pair * 128 : which * 256 + (pair + 1) * 128] = merged.astype(LOW)
+                if which == 0:
+                    query_sum = query_sum + jnp.sum(merged, axis=0, keepdims=True)
+                if which == 2:
+                    value_sum = value_sum + jnp.sum(merged, axis=0, keepdims=True)
+        lanes = pl.ds(pl.multiple_of(pair * 512 + team * 128, 128), 128)
+        vec_ref[2:3, lanes] = query_sum
+        vec_ref[3:4, lanes] = value_sum
+    grad_ref[...] = matmul_tn(normed_ref[...], mixed_ref[...])
+    spread(at, grad_ref, mine_ref, theirs_ref)
+    keep_ref[...] = matmul_nt(mixed_ref[0:256, :], weight_ref[...])
+    send_ref[...] = matmul_nt(mixed_ref[256:512, :], weight_ref[...])
+    gain_sum = jnp.zeros((1, D), jnp.float32)
+    shift_sum = jnp.zeros((1, D), jnp.float32)
+    for block in range(4):
+        rows = slice(block * ROW, (block + 1) * ROW)
+        _, scaled, _ = normalize(x_ref[rows, :].astype(jnp.float32), 1.0, 0.0)
+        source, at_row = (keep_ref, block) if block < 2 else (send_ref, block - 2)
+        partial = source[at_row * ROW : (at_row + 1) * ROW, :]
+        gain_sum = gain_sum + jnp.sum(partial * scaled, axis=0, keepdims=True)
+        shift_sum = shift_sum + jnp.sum(partial, axis=0, keepdims=True)
+    vec_ref[0:1, :] = gain_sum
+    vec_ref[1:2, :] = shift_sum
+    group = lane_group(16)
+    for ref, side, kind in ((mine_ref, y_pos, jnp.float32), (theirs_ref, 1 - y_pos, LOW)):
+        for z in range(4):
+            tile = jnp.zeros((16, 128), jnp.float32)
+            for t in range(4):
+                piece = vec_ref[:, pl.ds(pl.multiple_of(side * 512 + t * 128, 128), 128)]
+                shift = (t - z) * 32 % 128
+                piece = pltpu.roll(piece, shift, 1) if shift else piece
+                tile = jnp.where(group == t, piece, tile)
+            ref[z, 128:144, 0:128] = tile.astype(kind)
+            ref[z, 128:144, 128:768] = jnp.zeros((16, 640), kind)
+
+
+def team_body(x_in, cotangent, params, first_moment, second_moment, seq_lengths, seq_device):
+    rows = x_in.shape[0]
+    share = D // 32
+    vec_rows = 8 + FF // D
+    y_pos = lax.axis_index("y")
+    x_pos = lax.axis_index("x")
+    c_pos = lax.axis_index("c")
+    z_pos = lax.axis_index("z")
+    team_pos = x_pos * 2 + c_pos
+    at = jnp.stack([y_pos, team_pos]).astype(jnp.int32)
+
+    qkv_part, out_part, up_part, down_part, vec_part = local_pieces(params.astype(LOW), share)
+    qkv_send = qkv_part.reshape(share, 6, 4, 128).transpose(2, 0, 1, 3).reshape(4, share, 768)
+    vec_row = jnp.broadcast_to(jnp.pad(vec_part, ((0, 4), (0, 736)))[None], (4, 16, 768))
+    qkv_team = team_exchange(jnp.concatenate([qkv_send, vec_row], axis=1))
+    vec_team = qkv_team[:, share:, :32].transpose(1, 0, 2).reshape(16, 128)
+    qkv_shard = jnp.concatenate(
+        [qkv_team[:, :share].reshape(4 * share, 768), jnp.pad(vec_team, ((0, 0), (0, 640)))], axis=0
+    )
+    qkv_own = z_gather(qkv_shard).reshape(4, 144, 768)
+    out_own = z_gather(out_part)
+    up_send = up_part.reshape(share, 2, 4, 512).transpose(2, 0, 1, 3).reshape(4, share, 1024)
+    up_own = z_gather(team_exchange(up_send).reshape(4 * share, 1024)).reshape(4, 4 * share, 1024)
+    down_own = z_gather(down_part)
+    qkv_far, out_far, up_far, down_far = (swap(v, "y") for v in (qkv_own, out_own, up_own, down_own))
+
+    steps = jnp.arange(2, dtype=jnp.int32)
+    team_devices = (
+        ((y_pos * 2 + (x_pos ^ steps[None, :])) * 2 + (c_pos ^ steps[:, None])) * 4 + z_pos
+    ).reshape(4)
+    seg_ids, live_mask = segments(seq_lengths, seq_device, team_devices.astype(jnp.int32), rows)
+    seg_col = seg_ids.reshape(4 * rows, 1)
+
+    upstream = cotangent * live_mask[0][:, None].astype(jnp.float32)
+    tokens = jnp.stack(team_gather(jnp.stack([x_in, upstream.astype(LOW)])))
+    x_team = tokens[:, 0].reshape(TOK, D)
+    up_low = tokens[:, 1].reshape(TOK, D)
+
+    vectors, qkv_weight, out_weight, normed1, qkv_low, attended, keep, send = call(
+        forward_kernel,
+        "attention_forward",
+        (
+            sds((16, D)), sds((D, 768), LOW), sds((256, D), LOW), sds((TOK, D), LOW),
+            sds((TOK, 768), LOW), sds((TOK, 256), LOW), sds((256, D)), sds((256, D)),
+        ),
+        (at, x_team, qkv_own, qkv_far, out_own, out_far, seg_col, seg_ids),
+    )
+    up_bias = lax.dynamic_index_in_dim(
+        vectors[7 : 7 + FF // D].reshape(2, 4, 512), team_pos, 1, keepdims=False
+    ).reshape(1, 1024)
+    summed, near = team_reduce(keep, send)
+    residual, normed2 = call(
+        residual_kernel, "residual", (sds((rows, D)), sds((rows, D), LOW)), (at, x_in, summed, near, vectors)
+    )
+    normed2, up_weight, hidden, slope, down_mine, down_theirs = call(
+        up_kernel,
+        "up_forward",
+        (
+            sds((TOK, D), LOW), sds((D, 1024), LOW), sds((TOK, 1024), LOW), sds((TOK, 1024)),
+            sds((512, D)), sds((512, D), LOW),
+        ),
+        (at, *team_gather(normed2), up_own, up_far, up_bias, up_low),
+        [pltpu.VMEM((1024, D), jnp.float32)],
+    )
+    y_sum = lambda mine, theirs: (mine + swap(theirs, "y").astype(jnp.float32)).astype(LOW)
+    down_sum = z_reduce(y_sum(down_mine, down_theirs))
+    pre_low, pre_sum, keep, send = call(
+        down_kernel,
+        "down_backward",
+        (sds((TOK, 1024), LOW), sds((8, 1024)), sds((256, D)), sds((256, D))),
+        (at, up_low, down_own, down_far, slope, up_weight),
+    )
+    summed, near = team_reduce(keep, send)
+    grad_residual, res_low, row_sums = call(
+        residual_back_kernel,
+        "residual_backward",
+        (sds((rows, D)), sds((rows, D), LOW), sds((8, D))),
+        (at, residual, summed, near, upstream, vectors),
+    )
+    up_mine, up_theirs = call(
+        up_grad_kernel,
+        "up_grad",
+        (sds((4, 4 * share, 1024)), sds((4, 4 * share, 1024), LOW)),
+        (at, normed2, pre_low),
+        [pltpu.VMEM((D, 1024), jnp.float32)],
+    )
+    up_sum = z_reduce(y_sum(up_mine, up_theirs).reshape(TOK, 1024))
+    keep, send = call(
+        output_kernel, "down_forward", (sds((256, D)), sds((256, D))), (at, hidden, down_own, down_far)
+    )
+    summed, near = team_reduce(keep, send)
+    output = residual + summed + near.astype(jnp.float32) + vectors[7 + FF // D]
+    res_team, out_mine, out_theirs = call(
+        out_grad_kernel,
+        "out_grad",
+        (sds((TOK, D), LOW), sds((128, D)), sds((128, D), LOW)),
+        (at, *team_gather(res_low), attended),
+        [pltpu.VMEM((256, D), jnp.float32)],
+    )
+    out_sum = z_reduce(y_sum(out_mine, out_theirs))
+    own_team = (jnp.arange(4, dtype=jnp.int32) == team_pos).astype(jnp.float32)[None, :, None]
+    grad_rows = jnp.concatenate(
+        [
+            jnp.zeros((4, D), jnp.float32),
+            row_sums[:3],
+            (pre_sum[0].reshape(2, 1, 512) * own_team).reshape(FF // D, D),
+            row_sums[3:4],
+            jnp.zeros((4, D), jnp.float32),
+        ]
+    )
+    qkv_mine, qkv_theirs, keep, send = call(
+        backward_kernel,
+        "attention_backward",
+        (sds((4, 144, 768)), sds((4, 144, 768), LOW), sds((256, D)), sds((256, D))),
+        (at, res_team, out_weight, qkv_low, normed1, x_team, qkv_weight, seg_col, seg_ids, grad_rows),
+        [
+            pltpu.VMEM((TOK, 768), LOW), pltpu.VMEM((D, 768), jnp.float32),
+            pltpu.VMEM((TOK, 256), LOW), pltpu.VMEM((16, D), jnp.float32),
+        ],
+    )
+    qkv_sum = z_reduce(y_sum(qkv_mine, qkv_theirs).reshape(576, 768))
+    vec_back = qkv_sum[4 * share :, :128].reshape(16, 4, 32).transpose(1, 0, 2)
+    qkv_back = jnp.concatenate(
+        [qkv_sum[: 4 * share].reshape(4, share, 768), jnp.pad(vec_back, ((0, 0), (0, 0), (0, 736)))], axis=1
+    )
+    qkv_back = team_exchange(qkv_back).astype(jnp.float32)
+    up_back = team_exchange(up_sum.reshape(4, share, 1024)).astype(jnp.float32)
+
+    summed, near = team_reduce(keep, send)
+    grad_normed1 = summed + near.astype(jnp.float32)
+    _, scaled1, inverse1 = normalize(x_in.astype(jnp.float32), vectors[0], vectors[1])
+    grad_input = grad_residual + normalize_back(grad_normed1, scaled1, inverse1, vectors[0])
+    owned = jnp.concatenate(
+        [
+            qkv_back[:, :share].reshape(4, share, 6, 128).transpose(1, 2, 0, 3).reshape(-1),
+            out_sum.astype(jnp.float32).reshape(-1),
+            up_back.reshape(4, share, 2, 512).transpose(1, 2, 0, 3).reshape(-1),
+            down_sum.astype(jnp.float32).reshape(-1),
+            jnp.sum(qkv_back[:, share : share + vec_rows, :32], axis=0).reshape(-1),
+        ]
+    )
+    new_params, new_first, new_second = adam(params, first_moment, second_moment, owned, share)
+    return (output, grad_input, owned, new_params, new_first, new_second)
+
 
 def solution(mesh):
+    shape = dict(mesh.shape)
+    if shape["dp"] == 8 and shape["shard"] == 4:
+        mesh = Mesh(mesh.devices.reshape(2, 2, 2, 4), ("y", "x", "c", "z"))
+        axes, step = ("y", "x", "c", "z"), team_body
+    else:
+        axes, step = ("dp", "shard"), body
     return jax.shard_map(
-        body,
+        step,
         mesh=mesh,
-        in_specs=(
-            P(("dp", "shard"), None),
-            P(("dp", "shard"), None),
-            P(("dp", "shard")),
-            P(("dp", "shard")),
-            P(("dp", "shard")),
-            P(),
-            P(),
-        ),
-        out_specs=(
-            P(("dp", "shard"), None),
-            P(("dp", "shard"), None),
-            P(("dp", "shard")),
-            P(("dp", "shard")),
-            P(("dp", "shard")),
-            P(("dp", "shard")),
-        ),
+        in_specs=(P(axes, None), P(axes, None), P(axes), P(axes), P(axes), P(), P()),
+        out_specs=(P(axes, None), P(axes, None), P(axes), P(axes), P(axes), P(axes)),
         check_vma=False,
     )

time: 1510 us -> 343 us (0.23)
  waiting for transfers between devices: 1320 us -> 137 us
  matrix products: 66.5 us -> 0 us
  Pallas kernels: 0 us -> 44.1 us
  starting transfers between devices: 0.59 us -> 34.8 us
  blocking collectives: 72.2 us -> 46 us
  local copies, waits for them, and re-layouts: 15.5 us -> 35.6 us
  other arithmetic: 11.2 us -> 30.3 us
    reduce_scatter x4, waiting for transfers between devices: 1030 us -> 13.4 us  [z_reduce(): return lax.psum_scatter(values, 'z', scatter_dimension=0, tiled=True)]
    all_gather x4 -> x2, waiting for transfers between devices: 200 us -> 0.01 us  [z_gather(): return lax.all_gather(shard, 'z', axis=0, tiled=True)]
    ppermute x0 -> x25, waiting for transfers between devices: none -> 114 us  [swap(): return lax.ppermute(values, axis, SWAP)]
    unnamed x10 -> x6, waiting for transfers between devices: 97.6 us -> 0.75 us
    dot_general x18 -> x0, matrix products: 66.5 us -> none  [the longest x4 27.7 us: matmul_tn(): lax.dot_general(left_side, right_side, (((0,), (0,)), ((), ())), preferre...]
    pallas_call x0 -> x9, Pallas kernels: none -> 44.1 us  [call(): pl.pallas_call(kernel, out_shape=outs, in_specs=specs, out_specs=tuple((p...]
    all_gather x1 -> x2, blocking collectives: 72.2 us -> 46 us  [z_gather(): return lax.all_gather(shard, 'z', axis=0, tiled=True)]
    ppermute x0 -> x25, starting transfers between devices: none -> 19.8 us  [swap(): return lax.ppermute(values, axis, SWAP)]
  transfers between devices with their start and end apart: 9 -> 35, of which waited for: 8 -> 20; matrix products, arithmetic and copies ran while one was open for 4% -> 9% of each run, Pallas kernels for 0% -> 11%
where the time goes in v1:
time: 343 us; the launch traced here: 342 us
  waiting for transfers between devices  137 us (40%)
  blocking collectives  46 us (13%)
  Pallas kernels  44.1 us (13%)
  local copies, waits for them, and re-layouts  35.6 us (10%)
  starting transfers between devices  34.8 us (10%)
  other arithmetic  30.3 us (9%)
  between operations  14.7 us (4%)
    ppermute x25, waiting for transfers between devices, swap(): return lax.ppermute(values, axis, SWAP)  114 us
    all_gather x2, blocking collectives, z_gather(): return lax.all_gather(shard, 'z', axis=0, tiled=True)  46 us
    pallas_call x9, Pallas kernels, call(): pl.pallas_call(kernel, out_shape=outs, in_specs=specs, out_specs=tuple((p...  44.1 us
    unnamed x88, local copies, waits for them, and re-layouts  26.3 us
    ppermute x25, starting transfers between devices, swap(): return lax.ppermute(values, axis, SWAP)  19.8 us
    all_to_all x4, starting transfers between devices, team_exchange(): return lax.all_to_all(values, TEAM, 0, 0, tiled=True)  14.8 us
    reduce_scatter x4, waiting for transfers between devices, z_reduce(): return lax.psum_scatter(values, 'z', scatter_dimension=0, tiled=True)  13.4 us
    all_to_all x4, waiting for transfers between devices, team_exchange(): return lax.all_to_all(values, TEAM, 0, 0, tiled=True)  8.86 us
  transfers between devices with their start and end apart: 35, of which 20 were waited for; matrix products, arithmetic and copies ran while one was open for 9% of the time, Pallas kernels for 11%

profile of v1, /device:TPU:0, one launch (start us, length us, event | category | flops | bytes accessed | tf_op | source)
XLA Modules:
  0.0 342.3 jit_solution(10522752090820134928)
XLA Ops:
  7.2 1.5 convert_element_type.80
  9.9 4.2 %all-to-all-start.1 = ((bf16[4,32,1024]{2,1,0:T(8,128)(2,1)}), bf16[4,32,1024]{2,1,0:T(8,128)(2,1)S(1)}, u32[]{:S(2)}, u32[]{:S(2)}) async-start(bf16[4,32,1024]{2,1,0:T(8,128)(2,1)} %reshape.208), calls=%async_computation.1 | async-start | bytes 524288 | tf_op jit(solution)/shard_map/all_to_all | solution.py:262
  16.1 4.1 %all-to-all-done.1 = bf16[4,32,1024]{2,1,0:T(8,128)(2,1)S(1)} async-done(((bf16[4,32,1024]{2,1,0:T(8,128)(2,1)}), bf16[4,32,1024]{2,1,0:T(8,128)(2,1)S(1)}, u32[]{:S(2)}, u32[]{:S(2)}) %all-to-all-start.1) | async-done | bytes 262176 | tf_op jit(solution)/shard_map/all_to_all | solution.py:262
  20.2 3.5 %all-to-all-start = ((bf16[4,48,768]{2,1,0:T(8,128)(2,1)}), bf16[4,48,768]{2,1,0:T(8,128)(2,1)S(1)}, u32[]{:S(2)}, u32[]{:S(2)}) async-start(bf16[4,48,768]{2,1,0:T(8,128)(2,1)} %pad_maximum_fusion.2), calls=%async_computation | async-start | bytes 589824 | tf_op jit(solution)/shard_map/all_to_all | solution.py:262
  25.4 1.0 fusion.20
  26.4 2.0 collective-permute-start
  28.4 1.8 all-to-all-done
  30.3 10.9 %collective-permute-done = bf16[2,128,1024]{2,1,0:T(8,128)(2,1)} collective-permute-done((bf16[2,128,1024]{2,1,0:T(8,128)(2,1)}, bf16[2,128,1024]{2,1,0:T(8,128)(2,1)}, u32[]{:S(2)}, u32[]{:S(2)}) %collective-permute-start) | collective-permute-done | bytes 524320 | tf_op jit(solution)/shard_map/ppermute | solution.py:250
  41.3 29.7 %all_gather.12 = bf16[576,768]{1,0:T(8,128)(2,1)S(1)} all-gather(bf16[144,768]{1,0:T(8,128)(2,1)S(1)} %fusion.17), channel_id=1, replica_groups=mesh['y'=2,'x'=2,'c'=2,'z'=4] {'z'}, dimensions={0}, use_global_device_ids=true | all-gather | bytes 1105920 | tf_op jit(solution)/shard_map/all_gather | solution.py:254
  71.0 1.5 collective-permute-start.3
  73.4 16.3 %all_gather.13.out_own = bf16[128,1024]{1,0:T(8,128)(2,1)S(1)} all-gather(bf16[32,1024]{1,0:T(8,128)(2,1)S(1)} %reshape.206), channel_id=1, replica_groups=mesh['y'=2,'x'=2,'c'=2,'z'=4] {'z'}, dimensions={0}, use_global_device_ids=true | all-gather | bytes 327680 | tf_op jit(solution)/shard_map/all_gather | solution.py:254
  90.6 1.8 pad_maximum_fusion
  92.4 1.5 fusion.22
  93.9 4.2 %collective-permute-done.4.out_far = bf16[128,1024]{1,0:T(8,128)(2,1)S(1)} collective-permute-done((bf16[128,1024]{1,0:T(8,128)(2,1)S(1)}, bf16[128,1024]{1,0:T(8,128)(2,1)S(1)}, u32[]{:S(2)}, u32[]{:S(2)}) %collective-permute-start.4) | collective-permute-done | bytes 262176 | tf_op jit(solution)/shard_map/ppermute | solution.py:250
  98.1 9.1 %attention_forward.1 = (f32[16,1024]{1,0:T(8,128)S(1)}, bf16[1024,768]{1,0:T(8,128)(2,1)}, bf16[256,1024]{1,0:T(8,128)(2,1)S(1)}, bf16[512,1024]{1,0:T(8,128)(2,...) custom-call(s32[2]{0:T(128)S(1)} %pad_add_fusion.at, ...), custom_call_target="tpu_custom_call" | custom-call | tf_op jit(solution)/shard_map/attention_forward/pallas_call | solution.py:283
  107.2 1.0 copy-done.12
  109.8 1.5 collective-permute-start.10
  112.7 1.4 add.144
  114.1 1.5 collective-permute-start.6
  115.7 6.8 %collective-permute-done.6.near_ref = bf16[128,1024]{1,0:T(8,128)(2,1)S(1)} collective-permute-done((bf16[128,1024]{1,0:T(8,128)(2,1)S(1)}, bf16[128,1024]{1,0:T(8,128)(2,1)S(1)}, u32[]{:S(2)}, u32[]{:S(2)}) %collective-permute-start.6) | collective-permute-done | bytes 262176 | tf_op jit(solution)/shard_map/ppermute | solution.py:250
  123.4 1.5 collective-permute-start.7
  125.6 5.4 %collective-permute-done.7.n1 = bf16[128,1024]{1,0:T(8,128)(2,1)S(1)} collective-permute-done((bf16[128,1024]{1,0:T(8,128)(2,1)S(1)}, bf16[128,1024]{1,0:T(8,128)(2,1)S(1)}, u32[]{:S(2)}, u32[]{:S(2)}) %collective-permute-start.7) | collective-permute-done | bytes 262176 | tf_op jit(solution)/shard_map/ppermute | solution.py:250
  132.5 3.7 %collective-permute-done.10.far_ref = bf16[4,128,1024]{2,1,0:T(8,128)(2,1)} collective-permute-done((bf16[4,128,1024]{2,1,0:T(8,128)(2,1)}, bf16[4,128,1024]{2,1,0:T(8,128)(2,1)}, u32[]{:S(2)}, u32[]{:S(2)}) %collective-permute-start.10) | collective-permute-done | bytes 1048608 | tf_op jit(solution)/shard_map/ppermute | solution.py:250
  136.9 1.2 copy-done.7
  141.9 7.5 %up_forward.1 = (bf16[512,1024]{1,0:T(8,128)(2,1)S(1)}, bf16[1024,1024]{1,0:T(8,128)(2,1)}, bf16[512,1024]{1,0:T(8,128)(2,1)S(1)}, f32[512,1024]{1,0:T(8,128)}, ...) custom-call(s32[2]{0:T(128)S(1)} %pad_add_fusion.at, bf16[128,1024]{1,0:T(8,128)(2,1)S(1)} %copy-done.22, ...), custom_call_target="tpu_custom_call" | custom-call | tf_op jit(solution)/shard_map/up_forward/pallas_call | solution.py:283
  151.3 6.8 %collective-permute-done.11.far_ref = bf16[512,1024]{1,0:T(8,128)(2,1)S(1)} collective-permute-done((bf16[512,1024]{1,0:T(8,128)(2,1)}, bf16[512,1024]{1,0:T(8,128)(2,1)S(1)}, u32[]{:S(2)}, u32[]{:S(2)}) %collective-permute-start.11) | collective-permute-done | bytes 1048608 | tf_op jit(solution)/shard_map/ppermute | solution.py:250
  159.1 6.7 %down_backward.1 = (bf16[512,1024]{1,0:T(8,128)(2,1)S(1)}, f32[8,1024]{1,0:T(8,128)S(1)}, f32[256,1024]{1,0:T(8,128)S(1)}, f32[256,1024]{1,0:T(8,128)S(1)}) custom-call(s32[2]{0:T(128)S(1)} %pad_add_fusion.at, bf16[512,1024]{1,0:T(8,128)(2,1)S(1)} %bitcast.46, bf16[512,1024]{1,0:T(8,128)(2,1)S(1)} %copy-done.2, bf16[512,1024]{1,0:T(8,128)(2,1)} %copy-done.3, ...), custom_call_target="tpu_custom_call" | custom-call | tf_op jit(solution)/shard_map/down_backward/pallas_call | solution.py:283
  165.8 2.6 collective-permute-done.14
  168.7 1.8 collective-permute-start.15
  170.5 6.8 %collective-permute-done.15.near_ref = bf16[128,1024]{1,0:T(8,128)(2,1)S(1)} collective-permute-done((bf16[128,1024]{1,0:T(8,128)(2,1)S(1)}, bf16[128,1024]{1,0:T(8,128)(2,1)S(1)}, u32[]{:S(2)}, u32[]{:S(2)}) %collective-permute-start.15) | collective-permute-done | bytes 262176 | tf_op jit(solution)/shard_map/ppermute | solution.py:250
  177.3 1.1 residual_backward.1
  179.1 1.5 collective-permute-start.16
  180.6 2.1 up_grad.1
  182.7 1.3 copy-done.5
  184.0 1.5 collective-permute-start.23
  185.5 1.1 collective-permute-done.16.r1
  187.0 1.1 collective-permute-done.18.r3
  188.2 1.1 out_grad.1
  189.3 1.0 copy-done.13
  190.3 1.5 collective-permute-start.22
  191.8 22.0 %collective-permute-done.22 = bf16[128,1024]{1,0:T(8,128)(2,1)S(1)} collective-permute-done((bf16[128,1024]{1,0:T(8,128)(2,1)S(1)}, bf16[128,1024]{1,0:T(8,128)(2,1)S(1)}, u32[]{:S(2)}, u32[]{:S(2)}) %collective-permute-start.22) | collective-permute-done | bytes 262176 | tf_op jit(solution)/shard_map/ppermute | solution.py:250
  214.6 3.3 add_convert_fusion.1
  218.0 1.5 collective-permute-start.24
  219.5 21.7 %collective-permute-done.24 = bf16[512,1024]{1,0:T(8,128)(2,1)S(1)} collective-permute-done((bf16[512,1024]{1,0:T(8,128)(2,1)S(1)}, bf16[512,1024]{1,0:T(8,128)(2,1)S(1)}, u32[]{:S(2)}, u32[]{:S(2)}) %collective-permute-start.24) | collective-permute-done | bytes 1048608 | tf_op jit(solution)/shard_map/ppermute | solution.py:250
  241.2 3.1 add_convert_fusion
  244.4 1.2 copy-done.11
  245.7 2.8 down_forward.1
  249.7 1.2 copy-done.14
  251.0 1.1 copy-done.16
  252.1 1.0 copy-done.18
  253.1 13.1 %attention_backward.1 = (f32[4,144,768]{2,1,0:T(8,128)}, bf16[4,144,768]{2,1,0:T(8,128)(2,1)S(1)}, f32[256,1024]{1,0:T(8,128)S(1)}, f32[256,1024]{1,0:T(8,128)}) custom-call(s32[2]{0:T(128)S(1)} %pad_add_fusion.at, bf16[512,1024]{1,0:T(8,128)(2,1)S(1)} %copy-done.14, bf16[256,1024]{1,0:T(8,128)(2,1)S(1)} %copy-done.18, bf16[512,768]{1,0:T(8,128)(2,1)S(1)} %copy-done.16, ...), custom_call_target="tpu_custom_call" | custom-call | tf_op jit(solution)/shard_map/attention_backward/pallas_call | solution.py:283
  266.2 1.5 collective-permute-start.21
  268.3 1.5 add.146
  270.5 17.8 %collective-permute-done.21 = bf16[4,144,768]{2,1,0:T(8,128)(2,1)S(1)} collective-permute-done((bf16[4,144,768]{2,1,0:T(8,128)(2,1)S(1)}, bf16[4,144,768]{2,1,0:T(8,128)(2,1)S(1)}, u32[]{:S(2)}, u32[]{:S(2)}) %collective-permute-start.21) | collective-permute-done | bytes 884768 | tf_op jit(solution)/shard_map/ppermute | solution.py:250
  288.3 1.1 add_convert_fusion.2
  290.3 1.4 add.155
  294.5 3.4 all-to-all-start.3
  297.9 1.0 convert_bitcast_fusion
  299.1 1.4 collective-permute-done.20
  300.8 13.4 %reduce-scatter.5.cloned.1.call-done = bf16[144,768]{1,0:T(8,128)(2,1)} async-done(((bf16[576,768]{1,0:T(8,128)(2,1)}), bf16[144,768]{1,0:T(8,128)(2,1)}) %reduce-scatter.5.cloned.1.call-update) | async-done | bytes 221200 | tf_op jit(solution)/shard_map/reduce_scatter | solution.py:258
  316.6 3.7 %all-to-all-start.2 = ((bf16[4,48,768]{2,1,0:T(8,128)(2,1)}), bf16[4,48,768]{2,1,0:T(8,128)(2,1)S(1)}, u32[]{:S(2)}, u32[]{:S(2)}) async-start(bf16[4,48,768]{2,1,0:T(8,128)(2,1)} %fusion.15), calls=%async_computation.3 | async-start | bytes 589824 | tf_op jit(solution)/shard_map/all_to_all | solution.py:262
  320.4 2.0 fusion.9
  323.4 3.0 all-to-all-done.2
  330.6 4.8 %multiply_subtract_fusion = (f32[393600]{0:T(1024)}, f32[393600]{0:T(1024)}, f32[393600]{0:T(1024)}) fusion(f32[393600]{0:T(1024)S(1)} %copy-done.31, f32[393600]{0:T(1024)} %constant_dynamic-update-slice_fusion, f32[393600]{0:T(1024)S(1)} %copy-done.33, f32[393600]{0:T(1024)} %param.11), kind=kLoop, calls=%fused_computation.6 | loop fusion | flops 6691200 | bytes 11020800 | tf_op jit(solution)/shard_map/sub | solution.py:209
  (199 shorter events, 37.0 us)
Async XLA Ops:
  8.8 5.9 %copy-start.38 = (s32[128]{0:T(128)S(1)}, s32[128]{0:T(128)}, u32[]{:S(2)}) copy-start(s32[128]{0:T(128)} %param.12) | copy-start | bytes 1540
  8.8 5.9 %copy-start.39 = (s32[128]{0:T(128)S(1)}, s32[128]{0:T(128)}, u32[]{:S(2)}) copy-start(s32[128]{0:T(128)} %param.13) | copy-start | bytes 1540
  9.9 10.2 %all-to-all-start.1 = ((bf16[4,32,1024]{2,1,0:T(8,128)(2,1)}), bf16[4,32,1024]{2,1,0:T(8,128)(2,1)S(1)}, u32[]{:S(2)}, u32[]{:S(2)}) async-start(bf16[4,32,1024]{2,1,0:T(8,128)(2,1)} %reshape.208), calls=%async_computation.1 | async-start | bytes 524288 | tf_op jit(solution)/shard_map/all_to_all | solution.py:262
  14.2 10.3 %copy-start.36 = (f32[128,1024]{1,0:T(8,128)S(1)}, f32[128,1024]{1,0:T(8,128)}, u32[]{:S(2)}) copy-start(f32[128,1024]{1,0:T(8,128)} %param.8) | copy-start | bytes 1572868
  14.8 10.6 %copy-start = (bf16[128,1024]{1,0:T(8,128)(2,1)S(1)}, bf16[128,1024]{1,0:T(8,128)(2,1)}, u32[]{:S(2)}) copy-start(bf16[128,1024]{1,0:T(8,128)(2,1)} %x_ref.1) | copy-start | bytes 786436
  20.2 3.5 %copy-start.34 = (bf16[4,32,1024]{2,1,0:T(8,128)(2,1)}, bf16[4,32,1024]{2,1,0:T(8,128)(2,1)S(1)}, u32[]{:S(2)}) copy-start(bf16[4,32,1024]{2,1,0:T(8,128)(2,1)S(1)} %all-to-all-done.1) | copy-start | bytes 786436
  20.2 10.0 %all-to-all-start = ((bf16[4,48,768]{2,1,0:T(8,128)(2,1)}), bf16[4,48,768]{2,1,0:T(8,128)(2,1)S(1)}, u32[]{:S(2)}, u32[]{:S(2)}) async-start(bf16[4,48,768]{2,1,0:T(8,128)(2,1)} %pad_maximum_fusion.2), calls=%async_computation | async-start | bytes 589824 | tf_op jit(solution)/shard_map/all_to_all | solution.py:262
  23.6 86.2 %all-gather.3.cloned.1.call-start = ((), (), s32[]{:S(2)}) async-start(), calls=%async_computation.8 | async-start | bytes 1310720 | tf_op jit(solution)/shard_map/all_gather | solution.py:254
  24.4 87.0 %all-gather.5.cloned.1.call-start = ((), (), s32[]{:S(2)}) async-start(), calls=%async_computation.9 | async-start | bytes 1310720 | tf_op jit(solution)/shard_map/all_gather | solution.py:254
  26.4 14.8 %collective-permute-start = (bf16[2,128,1024]{2,1,0:T(8,128)(2,1)}, bf16[2,128,1024]{2,1,0:T(8,128)(2,1)}, u32[]{:S(2)}, u32[]{:S(2)}) collective-permute-start(bf16[2,128,1024]{2,1,0:T(8,128)(2,1)} %get-tuple-element.88), channel_id=1, source_target_pairs={{0,8},{8,0},{1,9},{9,1},{2,10},{10,2},{3,11},{11,3},{4,12},{12,4},... | collective-permute-start | bytes 1572872 | tf_op jit(solution)/shard_map/ppermute | solution.py:250
  28.4 62.2 %collective-permute-start.1 = (bf16[2,128,1024]{2,1,0:T(8,128)(2,1)}, bf16[2,128,1024]{2,1,0:T(8,128)(2,1)}, u32[]{:S(2)}, u32[]{:S(2)}) collective-permute-start(bf16[2,128,1024]{2,1,0:T(8,128)(2,1)} %get-tuple-element.88), channel_id=1, source_target_pairs={{0,4},{4,0},{1,5},{5,1},{2,6},{6,2},{3,7},{7,3},{8,12},{12,8},{9,1... | collective-permute-start | bytes 1572872 | tf_op jit(solution)/shard_map/ppermute | solution.py:250
  41.3 49.3 %collective-permute-start.2 = (bf16[2,128,1024]{2,1,0:T(8,128)(2,1)}, bf16[2,128,1024]{2,1,0:T(8,128)(2,1)}, u32[]{:S(2)}, u32[]{:S(2)}) collective-permute-start(bf16[2,128,1024]{2,1,0:T(8,128)(2,1)} %collective-permute-done), channel_id=1, source_target_pairs={{0,4},{4,0},{1,5},{5,1},{2,6},{6,2},{3,7},{7,3},{8,12},{12,8},{9,1... | collective-permute-start | bytes 1572872 | tf_op jit(solution)/shard_map/ppermute | solution.py:250
  71.0 27.1 %collective-permute-start.3 = (bf16[4,144,768]{2,1,0:T(8,128)(2,1)S(1)}, bf16[4,144,768]{2,1,0:T(8,128)(2,1)S(1)}, u32[]{:S(2)}, u32[]{:S(2)}) collective-permute-start(bf16[4,144,768]{2,1,0:T(8,128)(2,1)S(1)} %bitcast.47), channel_id=1, source_target_pairs={{0,16},{16,0},{1,17},{17,1},{2,18},{18,2},{3,19},{19,3},{4,20},{20... | collective-permute-start | bytes 2654216 | tf_op jit(solution)/shard_map/ppermute | solution.py:250
  73.3 219.7 %reduce-scatter.7.cloned.1.call-start = ((), (), s32[]{:S(2)}) async-start(), calls=%async_computation.11 | async-start | bytes 327680 | tf_op jit(solution)/shard_map/reduce_scatter | solution.py:258
  89.7 8.3 %collective-permute-start.4 = (bf16[128,1024]{1,0:T(8,128)(2,1)S(1)}, bf16[128,1024]{1,0:T(8,128)(2,1)S(1)}, u32[]{:S(2)}, u32[]{:S(2)}) collective-permute-start(bf16[128,1024]{1,0:T(8,128)(2,1)S(1)} %all_gather.13.out_own), channel_id=1, source_target_pairs={{0,16},{16,0},{1,17},{17,1},{2,18},{18,2},{3,19},{19,3},{4,20},{20... | collective-permute-start | bytes 786440 | tf_op jit(solution)/shard_map/ppermute | solution.py:250
  107.2 1.0 copy-start.12
  109.8 2.9 collective-permute-start.5
  109.8 26.3 %collective-permute-start.10 = (bf16[4,128,1024]{2,1,0:T(8,128)(2,1)}, bf16[4,128,1024]{2,1,0:T(8,128)(2,1)}, u32[]{:S(2)}, u32[]{:S(2)}) collective-permute-start(bf16[4,128,1024]{2,1,0:T(8,128)(2,1)} %bitcast.49), channel_id=1, source_target_pairs={{0,16},{16,0},{1,17},{17,1},{2,18},{18,2},{3,19},{19,3},{4,20},{20... | collective-permute-start | bytes 3145736 | tf_op jit(solution)/shard_map/ppermute | solution.py:250
  111.3 46.8 %collective-permute-start.11 = (bf16[512,1024]{1,0:T(8,128)(2,1)}, bf16[512,1024]{1,0:T(8,128)(2,1)S(1)}, u32[]{:S(2)}, u32[]{:S(2)}) collective-permute-start(bf16[512,1024]{1,0:T(8,128)(2,1)} %all-gather.5.cloned.1.call-done.own_ref), channel_id=1, source_target_pairs={{0,16},{16,0},{1,17},{17,1},{2,18},{18,2},{3,19},{19,3},{4,20},{20... | collective-permute-start | bytes 3145736 | tf_op jit(solution)/shard_map/ppermute | solution.py:250
  114.1 8.4 %collective-permute-start.6 = (bf16[128,1024]{1,0:T(8,128)(2,1)S(1)}, bf16[128,1024]{1,0:T(8,128)(2,1)S(1)}, u32[]{:S(2)}, u32[]{:S(2)}) collective-permute-start(bf16[128,1024]{1,0:T(8,128)(2,1)S(1)} %slice.180), channel_id=1, source_target_pairs={{0,8},{8,0},{1,9},{9,1},{2,10},{10,2},{3,11},{11,3},{4,12},{12,4},... | collective-permute-start | bytes 786440 | tf_op jit(solution)/shard_map/ppermute | solution.py:250
  123.4 7.7 %collective-permute-start.7 = (bf16[128,1024]{1,0:T(8,128)(2,1)S(1)}, bf16[128,1024]{1,0:T(8,128)(2,1)S(1)}, u32[]{:S(2)}, u32[]{:S(2)}) collective-permute-start(bf16[128,1024]{1,0:T(8,128)(2,1)S(1)} %get-tuple-element.44.n0), channel_id=1, source_target_pairs={{0,8},{8,0},{1,9},{9,1},{2,10},{10,2},{3,11},{11,3},{4,12},{12,4},... | collective-permute-start | bytes 786440 | tf_op jit(solution)/shard_map/ppermute | solution.py:250
  124.9 6.9 %collective-permute-start.8 = (bf16[128,1024]{1,0:T(8,128)(2,1)S(1)}, bf16[128,1024]{1,0:T(8,128)(2,1)S(1)}, u32[]{:S(2)}, u32[]{:S(2)}) collective-permute-start(bf16[128,1024]{1,0:T(8,128)(2,1)S(1)} %get-tuple-element.44.n0), channel_id=1, source_target_pairs={{0,4},{4,0},{1,5},{5,1},{2,6},{6,2},{3,7},{7,3},{8,12},{12,8},{9,1... | collective-permute-start | bytes 786440 | tf_op jit(solution)/shard_map/ppermute | solution.py:250
  131.0 5.2 %collective-permute-start.9 = (bf16[128,1024]{1,0:T(8,128)(2,1)S(1)}, bf16[128,1024]{1,0:T(8,128)(2,1)S(1)}, u32[]{:S(2)}, u32[]{:S(2)}) collective-permute-start(bf16[128,1024]{1,0:T(8,128)(2,1)S(1)} %collective-permute-done.7.n1), channel_id=1, source_target_pairs={{0,4},{4,0},{1,5},{5,1},{2,6},{6,2},{3,7},{7,3},{8,12},{12,8},{9,1... | collective-permute-start | bytes 786440 | tf_op jit(solution)/shard_map/ppermute | solution.py:250
  136.9 1.2 copy-start.7
  141.9 17.1 %copy-start.1 = (bf16[4,1,128,1024]{3,2,1,0:T(8,128)(2,1)S(1)}, bf16[4,1,128,1024]{3,2,1,0:T(8,128)(2,1)}, u32[]{:S(2)}) copy-start(bf16[4,1,128,1024]{3,2,1,0:T(8,128)(2,1)} %get-tuple-element.83) | copy-start | bytes 3145732
  141.9 17.1 %copy-start.2 = (bf16[512,1024]{1,0:T(8,128)(2,1)S(1)}, bf16[512,1024]{1,0:T(8,128)(2,1)}, u32[]{:S(2)}) copy-start(bf16[512,1024]{1,0:T(8,128)(2,1)} %all-gather.5.cloned.1.call-done.own_ref) | copy-start | bytes 3145732
  149.4 1.0 copy-start.10
  150.4 1.0 copy-start.29
  158.1 1.0 copy-start.3
  165.8 2.7 collective-permute-start.14
  168.5 8.8 %copy-start.6 = (f32[128,1024]{1,0:T(8,128)S(1)}, f32[128,1024]{1,0:T(8,128)}, u32[]{:S(2)}) copy-start(f32[128,1024]{1,0:T(8,128)} %get-tuple-element.80.up_ref) | copy-start | bytes 1572868
  168.7 8.6 %collective-permute-start.15 = (bf16[128,1024]{1,0:T(8,128)(2,1)S(1)}, bf16[128,1024]{1,0:T(8,128)(2,1)S(1)}, u32[]{:S(2)}, u32[]{:S(2)}) collective-permute-start(bf16[128,1024]{1,0:T(8,128)(2,1)S(1)} %slice.178), channel_id=1, source_target_pairs={{0,8},{8,0},{1,9},{9,1},{2,10},{10,2},{3,11},{11,3},{4,12},{12,4},... | collective-permute-start | bytes 786440 | tf_op jit(solution)/shard_map/ppermute | solution.py:250
  179.1 7.5 %collective-permute-start.16 = (bf16[128,1024]{1,0:T(8,128)(2,1)S(1)}, bf16[128,1024]{1,0:T(8,128)(2,1)S(1)}, u32[]{:S(2)}, u32[]{:S(2)}) collective-permute-start(bf16[128,1024]{1,0:T(8,128)(2,1)S(1)} %get-tuple-element.53.r0), channel_id=1, source_target_pairs={{0,8},{8,0},{1,9},{9,1},{2,10},{10,2},{3,11},{11,3},{4,12},{12,4},... | collective-permute-start | bytes 786440 | tf_op jit(solution)/shard_map/ppermute | solution.py:250
  182.7 1.3 copy-start.5
  184.0 30.5 %collective-permute-start.23 = (bf16[4,128,1024]{2,1,0:T(8,128)(2,1)S(1)}, bf16[4,128,1024]{2,1,0:T(8,128)(2,1)}, u32[]{:S(2)}, u32[]{:S(2)}) collective-permute-start(bf16[4,128,1024]{2,1,0:T(8,128)(2,1)S(1)} %get-tuple-element.71), channel_id=1, source_target_pairs={{0,16},{16,0},{1,17},{17,1},{2,18},{18,2},{3,19},{19,3},{4,20},{20... | collective-permute-start | bytes 3145736 | tf_op jit(solution)/shard_map/ppermute | solution.py:250
  185.5 1.5 collective-permute-start.17
  186.6 1.5 collective-permute-start.18
  189.2 1.1 copy-start.13
  190.3 23.4 %collective-permute-start.22 = (bf16[128,1024]{1,0:T(8,128)(2,1)S(1)}, bf16[128,1024]{1,0:T(8,128)(2,1)S(1)}, u32[]{:S(2)}, u32[]{:S(2)}) collective-permute-start(bf16[128,1024]{1,0:T(8,128)(2,1)S(1)} %get-tuple-element.67), channel_id=1, source_target_pairs={{0,16},{16,0},{1,17},{17,1},{2,18},{18,2},{3,19},{19,3},{4,20},{20... | collective-permute-start | bytes 786440 | tf_op jit(solution)/shard_map/ppermute | solution.py:250
  214.5 80.0 %reduce-scatter.9.cloned.1.call-start = ((), (), s32[]{:S(2)}) async-start(), calls=%async_computation.12 | async-start | bytes 1310720 | tf_op jit(solution)/shard_map/reduce_scatter | solution.py:258
  214.6 3.4 copy-start.30
  217.9 80.0 %reduce-scatter.11.cloned.1.call-start = ((), (), s32[]{:S(2)}) async-start(), calls=%async_computation.13 | async-start | bytes 1310720 | tf_op jit(solution)/shard_map/reduce_scatter | solution.py:258
  218.0 23.3 %collective-permute-start.24 = (bf16[512,1024]{1,0:T(8,128)(2,1)S(1)}, bf16[512,1024]{1,0:T(8,128)(2,1)S(1)}, u32[]{:S(2)}, u32[]{:S(2)}) collective-permute-start(bf16[512,1024]{1,0:T(8,128)(2,1)S(1)} %copy-done.30), channel_id=1, source_target_pairs={{0,16},{16,0},{1,17},{17,1},{2,18},{18,2},{3,19},{19,3},{4,20},{20... | collective-permute-start | bytes 3145736 | tf_op jit(solution)/shard_map/ppermute | solution.py:250
  241.2 3.2 copy-start.4
  244.3 69.8 %reduce-scatter.5.cloned.1.call-start = ((), (), s32[]{:S(2)}) async-start(), calls=%async_computation.10 | async-start | bytes 1105920 | tf_op jit(solution)/shard_map/reduce_scatter | solution.py:258
  244.4 1.2 copy-start.11
  248.4 1.0 copy-start.8
  249.4 18.9 %collective-permute-start.12 = (f32[256,1024]{1,0:T(8,128)}, f32[256,1024]{1,0:T(8,128)}, u32[]{:S(2)}, u32[]{:S(2)}) collective-permute-start(f32[256,1024]{1,0:T(8,128)} %get-tuple-element.47), channel_id=1, source_target_pairs={{0,4},{4,0},{1,5},{5,1},{2,6},{6,2},{3,7},{7,3},{8,12},{12,8},{9,1... | collective-permute-start | bytes 3145736 | tf_op jit(solution)/shard_map/ppermute | solution.py:250
  249.7 1.2 copy-start.14
  251.0 1.1 copy-start.16
  252.1 1.0 copy-start.18
  253.1 15.2 %copy-start.9 = (f32[256,1024]{1,0:T(8,128)S(1)}, f32[256,1024]{1,0:T(8,128)}, u32[]{:S(2)}) copy-start(f32[256,1024]{1,0:T(8,128)} %copy-done.8) | copy-start | bytes 3145732
  266.2 22.1 %collective-permute-start.21 = (bf16[4,144,768]{2,1,0:T(8,128)(2,1)S(1)}, bf16[4,144,768]{2,1,0:T(8,128)(2,1)S(1)}, u32[]{:S(2)}, u32[]{:S(2)}) collective-permute-start(bf16[4,144,768]{2,1,0:T(8,128)(2,1)S(1)} %get-tuple-element.65), channel_id=1, source_target_pairs={{0,16},{16,0},{1,17},{17,1},{2,18},{18,2},{3,19},{19,3},{4,20},{20... | collective-permute-start | bytes 2654216 | tf_op jit(solution)/shard_map/ppermute | solution.py:250
  267.8 22.5 %collective-permute-start.19 = (f32[256,1024]{1,0:T(8,128)}, f32[256,1024]{1,0:T(8,128)}, u32[]{:S(2)}, u32[]{:S(2)}) collective-permute-start(f32[256,1024]{1,0:T(8,128)} %get-tuple-element.63), channel_id=1, source_target_pairs={{0,4},{4,0},{1,5},{5,1},{2,6},{6,2},{3,7},{7,3},{8,12},{12,8},{9,1... | collective-permute-start | bytes 3145736 | tf_op jit(solution)/shard_map/ppermute | solution.py:250
  268.3 19.9 %copy-start.32 = (f32[4,144,768]{2,1,0:T(8,128)S(1)}, f32[4,144,768]{2,1,0:T(8,128)}, u32[]{:S(2)}) copy-start(f32[4,144,768]{2,1,0:T(8,128)} %get-tuple-element.64) | copy-start | bytes 5308420
  269.9 19.6 %collective-permute-start.13 = (bf16[128,1024]{1,0:T(8,128)(2,1)S(1)}, bf16[128,1024]{1,0:T(8,128)(2,1)S(1)}, u32[]{:S(2)}, u32[]{:S(2)}) collective-permute-start(bf16[128,1024]{1,0:T(8,128)(2,1)S(1)} %slice.179), channel_id=1, source_target_pairs={{0,8},{8,0},{1,9},{9,1},{2,10},{10,2},{3,11},{11,3},{4,12},{12,4},... | collective-permute-start | bytes 786440 | tf_op jit(solution)/shard_map/ppermute | solution.py:250
  292.4 8.1 %collective-permute-start.20 = (bf16[128,1024]{1,0:T(8,128)(2,1)}, bf16[128,1024]{1,0:T(8,128)(2,1)S(1)}, u32[]{:S(2)}, u32[]{:S(2)}) collective-permute-start(bf16[128,1024]{1,0:T(8,128)(2,1)} %slice.177), channel_id=1, source_target_pairs={{0,8},{8,0},{1,9},{9,1},{2,10},{10,2},{3,11},{11,3},{4,12},{12,4},... | collective-permute-start | bytes 786440 | tf_op jit(solution)/shard_map/ppermute | solution.py:250
  294.5 22.1 %all-to-all-start.3 = ((bf16[4,32,1024]{2,1,0:T(8,128)(2,1)}), bf16[4,32,1024]{2,1,0:T(8,128)(2,1)S(1)}, u32[]{:S(2)}, u32[]{:S(2)}) async-start(bf16[4,32,1024]{2,1,0:T(8,128)(2,1)} %bitcast.69), calls=%async_computation.6 | async-start | bytes 524288 | tf_op jit(solution)/shard_map/all_to_all | solution.py:262
  298.9 21.4 %copy-start.20 = (f32[128,1024]{1,0:T(8,128)S(1)}, f32[128,1024]{1,0:T(8,128)}, u32[]{:S(2)}) copy-start(f32[128,1024]{1,0:T(8,128)} %copy-done.19) | copy-start | bytes 1572868
  300.5 16.1 %copy-start.35 = (bf16[128,1024]{1,0:T(8,128)(2,1)}, bf16[128,1024]{1,0:T(8,128)(2,1)S(1)}, u32[]{:S(2)}) copy-start(bf16[128,1024]{1,0:T(8,128)(2,1)S(1)} %collective-permute-done.20) | copy-start | bytes 786436
  316.6 9.8 %all-to-all-start.2 = ((bf16[4,48,768]{2,1,0:T(8,128)(2,1)}), bf16[4,48,768]{2,1,0:T(8,128)(2,1)S(1)}, u32[]{:S(2)}, u32[]{:S(2)}) async-start(bf16[4,48,768]{2,1,0:T(8,128)(2,1)} %fusion.15), calls=%async_computation.3 | async-start | bytes 589824 | tf_op jit(solution)/shard_map/all_to_all | solution.py:262
  326.4 1.3 copy-start.37
  327.6 3.1 copy-start.31
  327.7 2.9 copy-start.33
  (11 other events, 9.1 us)
Sparse Core Ops, SparseCore 0:
  26.0 39.2 all-gather.2
  73.4 27.6 all-gather.4
  214.6 17.8 reduce-scatter.6
  234.6 25.5 reduce-scatter.8
  262.3 25.7 reduce-scatter.10
  290.9 23.2 reduce-scatter.4

commit v2 on v1

--- a/solution.py
+++ b/solution.py
@@ -198,15 +198,13 @@
     )
 
 
-def adam(params, first_moment, second_moment, owned, share):
-    local_index = jnp.arange(owned.shape[0], dtype=jnp.int32)
-    matrix_mask = (local_index < share * (4 * D + 2 * FF)).astype(jnp.float32)
+def adam(params, first_moment, second_moment, owned, decay):
     new_first = beta_first * first_moment + (1.0 - beta_first) * owned
     new_second = beta_second * second_moment + (1.0 - beta_second) * owned * owned
     fix_first = 1.0 - beta_first**STEP
     fix_second = 1.0 - beta_second**STEP
     ratio = new_first / fix_first / (jnp.sqrt(new_second / fix_second) + adam_eps)
-    new_params = params - learn_rate * (ratio + decay_rate * matrix_mask * params)
+    new_params = params - learn_rate * (ratio + decay * params)
     return (new_params, new_first, new_second)
 
 
@@ -236,8 +234,11 @@
         lax.psum_scatter(grads[4], ("dp", "shard"), scatter_dimension=1, tiled=True),
     )
     owned = jnp.concatenate([piece.reshape(-1) for piece in owned_parts])
-    new_params, new_first, new_second = adam(params, first_moment, second_moment, owned, share)
+    local_index = jnp.arange(owned.shape[0], dtype=jnp.int32)
+    decay = decay_rate * (local_index < share * (4 * D + 2 * FF)).astype(jnp.float32)
+    new_params, new_first, new_second = adam(params, first_moment, second_moment, owned, decay)
     return (output[0], grad_input[0], owned, new_params, new_first, new_second)
+
 
 SWAP = ((0, 1), (1, 0))
 TEAM = ("x", "c")
@@ -262,33 +263,76 @@
     return lax.all_to_all(values, TEAM, 0, 0, tiled=True)
 
 
-def team_gather(own):
+def team_gather(own, dep=None):
     near = swap(own, "x")
-    return (own, near, swap(own, "c"), swap(near, "c"))
+    onward = near if dep is None else after(near, dep)
+    return (own, near, swap(own, "c"), swap(onward, "c"))
 
 
 def team_reduce(keep, send):
-    summed = keep + swap(send, "c")
-    return (summed[:ROW], swap(summed[ROW:].astype(LOW), "x"))
+    recv = swap(send, "c")
+    away = (keep[ROW:] + recv[ROW:]).astype(LOW)
+    near = swap(away, "x")
+    return (keep, recv, near)
+
+
+def team_total(keep, recv, near):
+    return keep[:ROW] + recv[:ROW] + near.astype(jnp.float32)
 
 
 def sds(shape, dtype=jnp.float32):
     return jax.ShapeDtypeStruct(shape, dtype)
 
 
-def call(kernel, name, outs, operands, scratch=()):
-    specs = [pl.BlockSpec(memory_space=pltpu.SMEM)] + [
-        pl.BlockSpec(memory_space=pltpu.VMEM) for _ in operands[1:]
-    ]
+def after(value, dep):
+    return lax.optimization_barrier((value, dep))[0]
+
+
+def call(kernel, outs, at, operands, scratch=()):
+    n_in, n_out = len(operands), len(outs)
+
+    def staged(at_ref, *refs):
+        hbm_in, hbm_out = refs[:n_in], refs[n_in : n_in + n_out]
+        ins = refs[n_in + n_out : 2 * n_in + n_out]
+        results = refs[2 * n_in + n_out : 2 * (n_in + n_out)]
+        in_sems, out_sems = refs[-2:]
+        tmp = refs[2 * (n_in + n_out) : -2]
+        loads = [pltpu.make_async_copy(hbm_in[i], ins[i], in_sems.at[i]) for i in range(n_in)]
+        stores = [pltpu.make_async_copy(results[i], hbm_out[i], out_sems.at[i]) for i in range(n_out)]
+        waited, sent = set(), set()
+        for load in loads:
+            load.start()
+
+        def ready(*which):
+            for i in which or range(n_in):
+                if i not in waited:
+                    waited.add(i)
+                    loads[i].wait()
+
+        def flush(*which):
+            for i in which or range(n_out):
+                if i not in sent:
+                    sent.add(i)
+                    stores[i].start()
+
+        kernel(at_ref, ins, results, tmp, ready, flush)
+        ready()
+        flush()
+        for store in stores:
+            store.wait()
+
+    hbm = pl.BlockSpec(memory_space=pl.ANY)
     return pl.pallas_call(
-        kernel,
+        staged,
         out_shape=outs,
-        in_specs=specs,
-        out_specs=tuple(pl.BlockSpec(memory_space=pltpu.VMEM) for _ in outs),
-        scratch_shapes=scratch,
-        name=name,
-        compiler_params=pltpu.CompilerParams(vmem_limit_bytes=48 << 20),
-    )(*operands)
+        in_specs=[pl.BlockSpec(memory_space=pltpu.SMEM)] + [hbm] * n_in,
+        out_specs=(hbm,) * n_out,
+        scratch_shapes=[pltpu.VMEM(v.shape, v.dtype) for v in operands]
+        + [pltpu.VMEM(v.shape, v.dtype) for v in outs]
+        + list(scratch)
+        + [pltpu.SemaphoreType.DMA((n_in,)), pltpu.SemaphoreType.DMA((n_out,))],
+        compiler_params=pltpu.CompilerParams(vmem_limit_bytes=60 << 20),
+    )(at, *operands)
 
 
 def head_lanes():
@@ -299,39 +343,44 @@
     return lax.broadcasted_iota(jnp.int32, (rows, 128), 1) // 32
 
 
-def allowed_block(seg_col, seg_row, block):
+def allowed_block(seg_ref, block):
     query_at = lax.broadcasted_iota(jnp.int32, (ROW, ROW), 0)
     key_at = lax.broadcasted_iota(jnp.int32, (ROW, ROW), 1)
-    return (seg_col[block * ROW : (block + 1) * ROW, :] == seg_row[block : block + 1, :]) & (
-        query_at >= key_at
-    )
+    seg_row = seg_ref[block : block + 1, :].astype(jnp.float32)
+    seg_col = jnp.sum(jnp.where(query_at == key_at, seg_row, 0.0), axis=1, keepdims=True)
+    return (seg_col == seg_row) & (query_at >= key_at)
 
 
 def scores_of(query_low, key_low, allowed):
     return jnp.where(allowed, matmul_nt(query_low, key_low) * score_scale, neg_large)
 
 
-def forward_kernel(
-    at, x_ref, own_ref, far_ref, out_own, out_far, seg_col, seg_row,
-    vec_ref, weight_ref, out_ref, normed_ref, qkv_ref, att_ref, keep_ref, send_ref,
-):
+def forward_kernel(at, ins, outs, tmp, ready, flush):
+    x_ref, own_ref, far_ref, seg_ref = ins
+    vec_ref, weight_ref, out_ref, normed_ref, qkv_ref, att_ref, keep_ref, send_ref = outs
     y_pos, team = at[0], at[1]
     group = lane_group(16)
-    for ref, out_part, side in ((own_ref, out_own, y_pos), (far_ref, out_far, 1 - y_pos)):
+    for index, ref, side in ((1, own_ref, y_pos), (2, far_ref, 1 - y_pos)):
+        ready(index)
         base = side * 512
         for z in range(4):
             for t in range(4):
                 start = pl.multiple_of(base + t * 128 + z * 32, 32)
                 weight_ref[pl.ds(start, 32), :] = ref[z, t * 32 : (t + 1) * 32, :]
+            top = pl.multiple_of(side * 128 + z * 32, 32)
+            out_ref[pl.ds(top, 32), 0:768] = ref[z, 128:160, :]
+            out_ref[pl.ds(top, 16), 768:1024] = ref[z, 160:176, 0:256]
+            out_ref[pl.ds(pl.multiple_of(top + 16, 16), 16), 768:1024] = ref[z, 160:176, 256:512]
         for t in range(4):
             tile = jnp.zeros((16, 128), jnp.float32)
             for z in range(4):
-                piece = ref[z, 128:144, 0:128].astype(jnp.float32)
+                piece = ref[z, 160:176, 512:640].astype(jnp.float32)
                 shift = (z - t) * 32 % 128
                 piece = pltpu.roll(piece, shift, 1) if shift else piece
                 tile = jnp.where(group == z, piece, tile)
             vec_ref[:, pl.ds(pl.multiple_of(base + t * 128, 128), 128)] = tile
-        out_ref[pl.ds(pl.multiple_of(side * 128, 128), 128), :] = out_part[...]
+    flush(0, 1, 2)
+    ready(0, 3)
     gain, shift_row = vec_ref[0:1, :], vec_ref[1:2, :]
     for block in range(4):
         rows = slice(block * ROW, (block + 1) * ROW)
@@ -350,10 +399,11 @@
                 if which == 2:
                     piece = piece + vec_ref[3:4, lanes]
                 qkv_ref[rows, cols] = piece.astype(LOW)
+    flush(3, 4)
     first = head_lanes()
     for block in range(4):
         rows = slice(block * ROW, (block + 1) * ROW)
-        allowed = allowed_block(seg_col, seg_row, block)
+        allowed = allowed_block(seg_ref, block)
         for pair in range(2):
             query, key, value = (
                 qkv_ref[rows, w * 256 + pair * 128 : w * 256 + (pair + 1) * 128] for w in range(3)
@@ -366,22 +416,41 @@
                 row_total = jnp.sum(exp_scores, axis=-1, keepdims=True)
                 heads.append(matmul((exp_scores / row_total).astype(LOW), value))
             att_ref[rows, pair * 128 : (pair + 1) * 128] = jnp.where(first, heads[0], heads[1]).astype(LOW)
+    send_ref[...] = matmul(att_ref[256:512, :], out_ref[...])
+    flush(5, 7)
     keep_ref[...] = matmul(att_ref[0:256, :], out_ref[...])
-    send_ref[...] = matmul(att_ref[256:512, :], out_ref[...])
-
-
-def residual_kernel(at, x_ref, sum_ref, near_ref, vec_ref, res_ref, low_ref):
-    total = sum_ref[...] + near_ref[...].astype(jnp.float32)
+
+
+def split_kernel(at, ins, outs, tmp, ready, flush):
+    left_ref, own_ref, far_ref = ins
+    keep_ref, send_ref = outs
+    depth = own_ref.shape[0]
+    near = pl.ds(pl.multiple_of(at[0] * depth, depth), depth)
+    away = pl.ds(pl.multiple_of((1 - at[0]) * depth, depth), depth)
+    ready()
+    for which, ref, base in ((1, send_ref, 256), (0, keep_ref, 0)):
+        rows = slice(base, base + 256)
+        ref[...] = matmul(left_ref[rows, near], own_ref[...]) + matmul(left_ref[rows, away], far_ref[...])
+        flush(which)
+
+
+def residual_kernel(at, ins, outs, tmp, ready, flush):
+    x_ref, keep_ref, recv_ref, near_ref, vec_ref = ins
+    res_ref, low_ref = outs
+    ready()
+    total = team_total(keep_ref, recv_ref, near_ref[...])
     residual = x_ref[...].astype(jnp.float32) + total + vec_ref[4:5, :]
     res_ref[...] = residual
     value, _, _ = normalize(residual, vec_ref[5:6, :], vec_ref[6:7, :])
     low_ref[...] = value.astype(LOW)
 
 
-def up_kernel(
-    at, n0, n1, n2, n3, own_ref, far_ref, bias_ref, uplow_ref,
-    team_ref, weight_ref, hidden_ref, slope_ref, mine_ref, theirs_ref, grad_ref,
-):
+def up_kernel(at, ins, outs, tmp, ready, flush):
+    n0, n1, n2, n3, own_ref, far_ref, vec_ref, uplow_ref = ins
+    team = at[1]
+    team_ref, weight_ref, hidden_ref, slope_ref, mine_ref, theirs_ref = outs
+    grad_ref, = tmp
+    ready(4, 5, 6, 0, 1, 2, 3)
     y_pos = at[0]
     for block, ref in enumerate((n0, n1, n2, n3)):
         team_ref[block * ROW : (block + 1) * ROW, :] = ref[...]
@@ -390,21 +459,26 @@
             for t in range(4):
                 start = pl.multiple_of(side * 512 + t * 128 + z * 32, 32)
                 weight_ref[pl.ds(start, 32), :] = ref[z, t * 32 : (t + 1) * 32, :]
+    flush(0, 1)
+    bias_lanes = pl.ds(pl.multiple_of((team % 2) * 512, 512), 512)
+    bias = jnp.concatenate([vec_ref[pl.ds(7 + 2 * side + team // 2, 1), bias_lanes] for side in range(2)], axis=1)
     for block in range(4):
         rows = slice(block * ROW, (block + 1) * ROW)
-        pre_act = matmul(team_ref[rows, :], weight_ref[...]) + bias_ref[...]
+        pre_act = matmul(team_ref[rows, :], weight_ref[...]) + bias
         act_value, act_slope = gelu_parts(pre_act)
         hidden_ref[rows, :] = act_value.astype(LOW)
         slope_ref[rows, :] = act_slope
+    flush(2, 3)
+    ready(7)
     grad_ref[...] = matmul_tn(hidden_ref[...], uplow_ref[...])
     mine_ref[...] = grad_ref[pl.ds(pl.multiple_of(y_pos * 512, 512), 512), :]
     theirs_ref[...] = grad_ref[pl.ds(pl.multiple_of((1 - y_pos) * 512, 512), 512), :].astype(LOW)
 
 
-def down_kernel(
-    at, uplow_ref, own_ref, far_ref, slope_ref, weight_ref,
-    pre_ref, sum_ref, keep_ref, send_ref,
-):
+def down_kernel(at, ins, outs, tmp, ready, flush):
+    uplow_ref, own_ref, far_ref, slope_ref, weight_ref = ins
+    pre_ref, sum_ref, keep_ref, send_ref = outs
+    ready(0, 1, 2, 3)
     y_pos = at[0]
     sum_ref[...] = jnp.zeros_like(sum_ref)
     for ref, side in ((own_ref, y_pos), (far_ref, 1 - y_pos)):
@@ -414,8 +488,11 @@
             grad_pre = matmul_nt(uplow_ref[rows, :], ref[...]) * slope_ref[rows, cols]
             pre_ref[rows, cols] = grad_pre.astype(LOW)
             sum_ref[0:1, cols] += jnp.sum(grad_pre, axis=0, keepdims=True)
+    flush(0, 1)
+    ready(4)
+    send_ref[...] = matmul_nt(pre_ref[256:512, :], weight_ref[...])
+    flush(3)
     keep_ref[...] = matmul_nt(pre_ref[0:256, :], weight_ref[...])
-    send_ref[...] = matmul_nt(pre_ref[256:512, :], weight_ref[...])
 
 
 def spread(at, grad_ref, mine_ref, theirs_ref):
@@ -428,25 +505,21 @@
             theirs_ref[z, t * 32 : (t + 1) * 32, :] = grad_ref[pl.ds(away, 32), :].astype(LOW)
 
 
-def up_grad_kernel(at, team_ref, pre_ref, mine_ref, theirs_ref, grad_ref):
+def up_grad_kernel(at, ins, outs, tmp, ready, flush):
+    team_ref, pre_ref = ins
+    mine_ref, theirs_ref = outs
+    grad_ref, = tmp
+    ready()
     grad_ref[...] = matmul_tn(team_ref[...], pre_ref[...])
     spread(at, grad_ref, mine_ref, theirs_ref)
 
 
-def output_kernel(at, hidden_ref, own_ref, far_ref, keep_ref, send_ref):
-    y_pos = at[0]
-    near = pl.ds(pl.multiple_of(y_pos * 512, 512), 512)
-    away = pl.ds(pl.multiple_of((1 - y_pos) * 512, 512), 512)
-    for ref, base in ((keep_ref, 0), (send_ref, 256)):
-        rows = slice(base, base + 256)
-        ref[...] = matmul(hidden_ref[rows, near], own_ref[...]) + matmul(hidden_ref[rows, away], far_ref[...])
-
-
-def residual_back_kernel(
-    at, res_ref, sum_ref, near_ref, up_ref, vec_ref, grad_ref, low_ref, rows_ref
-):
+def residual_back_kernel(at, ins, outs, tmp, ready, flush):
+    res_ref, keep_ref, recv_ref, near_ref, up_ref, vec_ref = ins
+    grad_ref, low_ref, rows_ref = outs
+    ready()
     _, scaled, inverse = normalize(res_ref[...], vec_ref[5:6, :], vec_ref[6:7, :])
-    grad_normed = sum_ref[...] + near_ref[...].astype(jnp.float32)
+    grad_normed = team_total(keep_ref, recv_ref, near_ref[...])
     upstream = up_ref[...]
     grad = upstream + normalize_back(grad_normed, scaled, inverse, vec_ref[5:6, :])
     grad_ref[...] = grad
@@ -459,30 +532,36 @@
     rows_ref[3:4, :] = total(upstream)
 
 
-def out_grad_kernel(at, r0, r1, r2, r3, att_ref, team_ref, mine_ref, theirs_ref, grad_ref):
-    y_pos = at[0]
-    for block, ref in enumerate((r0, r1, r2, r3)):
-        team_ref[block * ROW : (block + 1) * ROW, :] = ref[...]
-    grad_ref[...] = matmul_tn(att_ref[...], team_ref[...])
-    mine_ref[...] = grad_ref[pl.ds(pl.multiple_of(y_pos * 128, 128), 128), :]
-    theirs_ref[...] = grad_ref[pl.ds(pl.multiple_of((1 - y_pos) * 128, 128), 128), :].astype(LOW)
-
-
-def backward_kernel(
-    at, team_ref, out_ref, qkv_ref, normed_ref, x_ref, weight_ref, seg_col, seg_row, rows_ref,
-    mine_ref, theirs_ref, keep_ref, send_ref,
-    mixed_ref, grad_ref, att_ref, vec_ref,
-):
-    y_pos, team = at[0], at[1]
-    att_ref[...] = matmul_nt(team_ref[...], out_ref[...]).astype(LOW)
-    vec_ref[...] = rows_ref[...]
+def out_grad_kernel(at, ins, outs, tmp, ready, flush):
+    att_ref = ins[4]
+    mine_ref, theirs_ref = outs
+    ready(4)
+    for ref, side in ((theirs_ref, 1 - at[0]), (mine_ref, at[0])):
+        cols = pl.ds(pl.multiple_of(side * 128, 128), 128)
+        total = jnp.zeros((128, D), jnp.float32)
+        for block in range(4):
+            ready(block)
+            total = total + matmul_tn(att_ref[block * ROW : (block + 1) * ROW, cols], ins[block][...])
+        ref[...] = total.astype(ref.dtype)
+
+
+def backward_kernel(at, ins, outs, tmp, ready, flush):
+    out_ref, qkv_ref, seg_ref, normed_ref = ins[4:]
+    mine_ref, theirs_ref, mixed_ref, bias_ref = outs
+    grad_ref, att_ref = tmp
+    ready(4)
+    for block in range(4):
+        ready(block)
+        att_ref[block * ROW : (block + 1) * ROW, :] = matmul_nt(ins[block][...], out_ref[...]).astype(LOW)
+    ready(5, 6)
+    bias_ref[...] = jnp.zeros_like(bias_ref)
     first = head_lanes()
     for pair in range(2):
         query_sum = jnp.zeros((1, 128), jnp.float32)
         value_sum = jnp.zeros((1, 128), jnp.float32)
         for block in range(4):
             rows = slice(block * ROW, (block + 1) * ROW)
-            allowed = allowed_block(seg_col, seg_row, block)
+            allowed = allowed_block(seg_ref, block)
             query, key, value = (
                 qkv_ref[rows, w * 256 + pair * 128 : w * 256 + (pair + 1) * 128] for w in range(3)
             )
@@ -507,13 +586,32 @@
                     query_sum = query_sum + jnp.sum(merged, axis=0, keepdims=True)
                 if which == 2:
                     value_sum = value_sum + jnp.sum(merged, axis=0, keepdims=True)
-        lanes = pl.ds(pl.multiple_of(pair * 512 + team * 128, 128), 128)
-        vec_ref[2:3, lanes] = query_sum
-        vec_ref[3:4, lanes] = value_sum
+        bias_ref[0:1, pair * 128 : (pair + 1) * 128] = query_sum
+        bias_ref[1:2, pair * 128 : (pair + 1) * 128] = value_sum
+    flush(2, 3)
+    ready()
     grad_ref[...] = matmul_tn(normed_ref[...], mixed_ref[...])
     spread(at, grad_ref, mine_ref, theirs_ref)
+
+
+def vector_kernel(at, ins, outs, tmp, ready, flush):
+    mixed_ref, weight_ref, x_ref, rows_ref, pre_ref, bias_ref = ins
+    mine_ref, theirs_ref, keep_ref, send_ref = outs
+    vec_ref, = tmp
+    y_pos, team = at[0], at[1]
+    ready()
+    vec_ref[...] = jnp.zeros_like(vec_ref)
+    vec_ref[4:7, :] = rows_ref[0:3, :]
+    vec_ref[11:12, :] = rows_ref[3:4, :]
+    for side in range(2):
+        at_row = pl.ds(7 + 2 * side + team // 2, 1)
+        vec_ref[at_row, pl.ds(pl.multiple_of((team % 2) * 512, 512), 512)] = pre_ref[0:1, side * 512 : (side + 1) * 512]
+        lanes = pl.ds(pl.multiple_of(side * 512 + team * 128, 128), 128)
+        vec_ref[2:4, lanes] = bias_ref[0:2, side * 128 : (side + 1) * 128]
+    send_ref[...] = matmul_nt(mixed_ref[256:512, :], weight_ref[...])
+    flush(3)
     keep_ref[...] = matmul_nt(mixed_ref[0:256, :], weight_ref[...])
-    send_ref[...] = matmul_nt(mixed_ref[256:512, :], weight_ref[...])
+    flush(2)
     gain_sum = jnp.zeros((1, D), jnp.float32)
     shift_sum = jnp.zeros((1, D), jnp.float32)
     for block in range(4):
@@ -534,152 +632,265 @@
                 shift = (t - z) * 32 % 128
                 piece = pltpu.roll(piece, shift, 1) if shift else piece
                 tile = jnp.where(group == t, piece, tile)
-            ref[z, 128:144, 0:128] = tile.astype(kind)
-            ref[z, 128:144, 128:768] = jnp.zeros((16, 640), kind)
-
-
-def team_body(x_in, cotangent, params, first_moment, second_moment, seq_lengths, seq_device):
+            ref[z] = tile.astype(kind)
+
+
+def fold_kernel(at, ins, outs, tmp, ready, flush):
+    mine_ref, recv_ref, vec_mine, vec_recv = ins
+    ready()
+    for hop in (1, 2, 3, 0):
+        dest = lax.rem(at[2] + hop, 4)
+        ref = outs[hop]
+        ref[0:128, :] = (mine_ref[dest] + recv_ref[dest].astype(jnp.float32)).astype(ref.dtype)
+        ref[128:144, 0:128] = (vec_mine[dest] + vec_recv[dest].astype(jnp.float32)).astype(ref.dtype)
+        ref[128:144, 128:768] = jnp.zeros((16, 640), ref.dtype)
+        flush(hop)
+
+
+def step_rows(params_ref, first_ref, second_ref, grad_ref, new_refs, start, count, chunk, decay):
+    def visit(index, carry):
+        rows = pl.ds(pl.multiple_of(start + index * chunk, 8), chunk)
+        outs = adam(params_ref[rows, :], first_ref[rows, :], second_ref[rows, :], grad_ref[rows, :], decay)
+        for ref, value in zip(new_refs, outs):
+            ref[rows, :] = value
+        return carry
+
+    lax.fori_loop(0, count // chunk, visit, 0)
+
+
+def run_copies(pairs, sems, base):
+    copies = [pltpu.make_async_copy(src, dst, sems.at[base + i]) for i, (src, dst) in enumerate(pairs)]
+    for copy in copies:
+        copy.start()
+    for copy in copies:
+        copy.wait()
+
+
+def early_kernel(at, p_hbm, m_hbm, v_hbm, up_hbm, down_hbm, *refs):
+    hbm_outs = refs[:4]
+    p_ref, m_ref, v_ref, up_ref, down_ref, g_ref, np_ref, nm_ref, nv_ref, sems = refs[4:]
+    part = lambda ref: ref.at[pl.ds(1024, 2048), :]
+    pairs = [(up_hbm, up_ref), (down_hbm, down_ref)]
+    pairs.extend((part(hbm), ref) for hbm, ref in ((p_hbm, p_ref), (m_hbm, m_ref), (v_hbm, v_ref)))
+    run_copies(pairs, sems, 0)
+    for j in range(8):
+        cols = slice(j * 128, (j + 1) * 128)
+        g_ref[pl.ds(1024 + j, 128, stride=8), :] = down_ref[:, cols].astype(jnp.float32)
+        for t in range(4):
+            flat = (j // 4) * 16 + t * 4 + j % 4
+            g_ref[pl.ds(flat, 32, stride=32), :] = up_ref[t, :, cols].astype(jnp.float32)
+    step_rows(p_ref, m_ref, v_ref, g_ref, (np_ref, nm_ref, nv_ref), 0, 2048, 128, decay_rate)
+    run_copies([(src, part(dst)) for src, dst in zip((g_ref, np_ref, nm_ref, nv_ref), hbm_outs)], sems, 5)
+
+
+def late_kernel(at, p_hbm, m_hbm, v_hbm, qkv_hbm, out_hbm, *refs):
+    hbm_outs = refs[4:8]
+    p_ref, m_ref, v_ref, qkv_ref, out_ref, g_ref, np_ref, nm_ref, nv_ref, sems = refs[8:]
+    spans = lambda ref, hbm: (
+        (hbm.at[pl.ds(0, 1024), :], ref.at[pl.ds(0, 1024), :]),
+        (hbm.at[pl.ds(3072, 3), :], ref.at[pl.ds(1024, 3), :]),
+    )
+    pairs = [(qkv_hbm, qkv_ref), (out_hbm, out_ref)]
+    for hbm, ref in ((p_hbm, p_ref), (m_hbm, m_ref), (v_hbm, v_ref)):
+        pairs.extend(spans(ref, hbm))
+    run_copies(pairs, sems, 0)
+    for g in range(6):
+        for t in range(4):
+            g_ref[pl.ds(g * 4 + t, 32, stride=24), :] = qkv_ref[t, 0:32, g * 128 : (g + 1) * 128].astype(jnp.float32)
+    for j in range(8):
+        g_ref[pl.ds(768 + j, 32, stride=8), :] = out_ref[:, j * 128 : (j + 1) * 128].astype(jnp.float32)
+    total = jnp.zeros((16, 128), jnp.float32)
+    for t in range(4):
+        total = total + qkv_ref[t, 32:48, 0:128].astype(jnp.float32)
+    group = lane_group(1)
+    turned = [pltpu.roll(total, q * 32, 1) if q else total for q in range(4)]
+    for r in range(3):
+        row = jnp.zeros((1, 128), jnp.float32)
+        for q in range(4):
+            row = jnp.where(group == q, turned[q][4 * r + q : 4 * r + q + 1, :], row)
+        g_ref[1024 + r : 1025 + r, :] = row
+    new_refs = (np_ref, nm_ref, nv_ref)
+    step_rows(p_ref, m_ref, v_ref, g_ref, new_refs, 0, 1024, 128, decay_rate)
+    tail = slice(1024, 1027)
+    outs = adam(p_ref[tail, :], m_ref[tail, :], v_ref[tail, :], g_ref[tail, :], 0.0)
+    for ref, value in zip(new_refs, outs):
+        ref[tail, :] = value
+    pairs = []
+    for hbm, ref in zip(hbm_outs, (g_ref,) + new_refs):
+        pairs.extend((src, dst) for dst, src in spans(ref, hbm))
+    run_copies(pairs, sems, 8)
+
+
+def adam_call(kernel, at, arrays, previous, rows, extra_sems):
+    hbm = pl.BlockSpec(memory_space=pltpu.HBM)
+    operands = tuple(arrays) + tuple(previous)
+    grads = [pltpu.VMEM(v.shape, v.dtype) for v in arrays[3:]]
+    block = pltpu.VMEM((rows, 128), jnp.float32)
+    return pl.pallas_call(
+        kernel,
+        out_shape=tuple(sds(arrays[0].shape) for _ in range(4)),
+        in_specs=[pl.BlockSpec(memory_space=pltpu.SMEM)] + [hbm] * len(operands),
+        out_specs=(hbm,) * 4,
+        scratch_shapes=[block] * 3 + grads + [block] * 4 + [pltpu.SemaphoreType.DMA((extra_sems,))],
+        input_output_aliases={1 + len(arrays) + i: i for i in range(len(previous))},
+        compiler_params=pltpu.CompilerParams(vmem_limit_bytes=60 << 20),
+    )(at, *operands)
+
+
+def join_kernel(at, ins, outs, tmp, ready, flush):
+    own_ref, r1, r2, r3 = ins
+    pay_ref, = outs
+    ready()
+    total = own_ref[...]
+    for ref in (r1, r2, r3):
+        total = total + ref[...].astype(jnp.float32)
+    for t in range(4):
+        pay_ref[t, 0:32, :] = total[t * 32 : (t + 1) * 32, :].astype(LOW)
+        tile = total[128:144, 0:128]
+        pay_ref[t, 32:48, 0:128] = (pltpu.roll(tile, 128 - t * 32, 1) if t else tile).astype(LOW)
+        pay_ref[t, 32:48, 128:768] = jnp.zeros((16, 640), LOW)
+
+
+def team_body(*arrays):
+    return team_step(*arrays)
+
+
+def team_step(x_in, cotangent, params, first_moment, second_moment, seq_lengths, seq_device):
     rows = x_in.shape[0]
     share = D // 32
-    vec_rows = 8 + FF // D
     y_pos = lax.axis_index("y")
     x_pos = lax.axis_index("x")
     c_pos = lax.axis_index("c")
     z_pos = lax.axis_index("z")
     team_pos = x_pos * 2 + c_pos
-    at = jnp.stack([y_pos, team_pos]).astype(jnp.int32)
+    at = jnp.stack([y_pos, team_pos, z_pos]).astype(jnp.int32)
 
     qkv_part, out_part, up_part, down_part, vec_part = local_pieces(params.astype(LOW), share)
     qkv_send = qkv_part.reshape(share, 6, 4, 128).transpose(2, 0, 1, 3).reshape(4, share, 768)
     vec_row = jnp.broadcast_to(jnp.pad(vec_part, ((0, 4), (0, 736)))[None], (4, 16, 768))
     qkv_team = team_exchange(jnp.concatenate([qkv_send, vec_row], axis=1))
     vec_team = qkv_team[:, share:, :32].transpose(1, 0, 2).reshape(16, 128)
-    qkv_shard = jnp.concatenate(
-        [qkv_team[:, :share].reshape(4 * share, 768), jnp.pad(vec_team, ((0, 0), (0, 640)))], axis=0
-    )
-    qkv_own = z_gather(qkv_shard).reshape(4, 144, 768)
-    out_own = z_gather(out_part)
+    rest = jnp.concatenate(
+        [out_part[:16, 768:], out_part[16:, 768:], vec_team, jnp.zeros((16, 128), LOW)], axis=1
+    )
+    qkv_shard = jnp.concatenate([qkv_team[:, :share].reshape(4 * share, 768), out_part[:, :768], rest])
+    qkv_own = z_gather(qkv_shard).reshape(4, 176, 768)
+    qkv_far = swap(qkv_own, "y")
     up_send = up_part.reshape(share, 2, 4, 512).transpose(2, 0, 1, 3).reshape(4, share, 1024)
-    up_own = z_gather(team_exchange(up_send).reshape(4 * share, 1024)).reshape(4, 4 * share, 1024)
-    down_own = z_gather(down_part)
-    qkv_far, out_far, up_far, down_far = (swap(v, "y") for v in (qkv_own, out_own, up_own, down_own))
+    up_team = team_exchange(after(up_send, qkv_shard))
+    up_own = z_gather(up_team.reshape(4 * share, 1024)).reshape(4, 4 * share, 1024)
+    up_far = swap(up_own, "y")
+    down_own = z_gather(after(down_part, up_team))
 
     steps = jnp.arange(2, dtype=jnp.int32)
     team_devices = (
         ((y_pos * 2 + (x_pos ^ steps[None, :])) * 2 + (c_pos ^ steps[:, None])) * 4 + z_pos
     ).reshape(4)
     seg_ids, live_mask = segments(seq_lengths, seq_device, team_devices.astype(jnp.int32), rows)
-    seg_col = seg_ids.reshape(4 * rows, 1)
 
     upstream = cotangent * live_mask[0][:, None].astype(jnp.float32)
-    tokens = jnp.stack(team_gather(jnp.stack([x_in, upstream.astype(LOW)])))
+    token_pack = after(jnp.stack([x_in, upstream.astype(LOW)]), up_team)
+    tokens = jnp.stack(team_gather(token_pack))
     x_team = tokens[:, 0].reshape(TOK, D)
     up_low = tokens[:, 1].reshape(TOK, D)
 
     vectors, qkv_weight, out_weight, normed1, qkv_low, attended, keep, send = call(
         forward_kernel,
-        "attention_forward",
         (
             sds((16, D)), sds((D, 768), LOW), sds((256, D), LOW), sds((TOK, D), LOW),
             sds((TOK, 768), LOW), sds((TOK, 256), LOW), sds((256, D)), sds((256, D)),
         ),
-        (at, x_team, qkv_own, qkv_far, out_own, out_far, seg_col, seg_ids),
-    )
-    up_bias = lax.dynamic_index_in_dim(
-        vectors[7 : 7 + FF // D].reshape(2, 4, 512), team_pos, 1, keepdims=False
-    ).reshape(1, 1024)
-    summed, near = team_reduce(keep, send)
+        at,
+        (x_team, qkv_own, qkv_far, seg_ids),
+    )
+    keep, recv, near = team_reduce(keep, send)
     residual, normed2 = call(
-        residual_kernel, "residual", (sds((rows, D)), sds((rows, D), LOW)), (at, x_in, summed, near, vectors)
-    )
+        residual_kernel, (sds((rows, D)), sds((rows, D), LOW)), at, (x_in, keep, recv, near, vectors)
+    )
+    norm_blocks = team_gather(normed2)
+    down_far = swap(after(down_own, normed2), "y")
     normed2, up_weight, hidden, slope, down_mine, down_theirs = call(
         up_kernel,
-        "up_forward",
         (
             sds((TOK, D), LOW), sds((D, 1024), LOW), sds((TOK, 1024), LOW), sds((TOK, 1024)),
             sds((512, D)), sds((512, D), LOW),
         ),
-        (at, *team_gather(normed2), up_own, up_far, up_bias, up_low),
+        at,
+        (*norm_blocks, up_own, up_far, vectors, up_low),
         [pltpu.VMEM((1024, D), jnp.float32)],
     )
-    y_sum = lambda mine, theirs: (mine + swap(theirs, "y").astype(jnp.float32)).astype(LOW)
-    down_sum = z_reduce(y_sum(down_mine, down_theirs))
+    down_recv = swap(down_theirs, "y")
     pre_low, pre_sum, keep, send = call(
         down_kernel,
-        "down_backward",
         (sds((TOK, 1024), LOW), sds((8, 1024)), sds((256, D)), sds((256, D))),
-        (at, up_low, down_own, down_far, slope, up_weight),
-    )
-    summed, near = team_reduce(keep, send)
+        at,
+        (up_low, down_own, down_far, slope, up_weight),
+    )
+    keep, recv, near = team_reduce(keep, send)
+    y_sum = lambda mine, recv: (mine + recv.astype(jnp.float32)).astype(LOW)
+    down_pay = y_sum(after(down_mine, pre_sum), down_recv)
+    down_sum = z_reduce(down_pay)
     grad_residual, res_low, row_sums = call(
         residual_back_kernel,
-        "residual_backward",
         (sds((rows, D)), sds((rows, D), LOW), sds((8, D))),
-        (at, residual, summed, near, upstream, vectors),
+        at,
+        (residual, keep, recv, after(near, down_pay), upstream, vectors),
     )
     up_mine, up_theirs = call(
         up_grad_kernel,
-        "up_grad",
         (sds((4, 4 * share, 1024)), sds((4, 4 * share, 1024), LOW)),
-        (at, normed2, pre_low),
+        at,
+        (normed2, after(pre_low, res_low)),
         [pltpu.VMEM((D, 1024), jnp.float32)],
     )
-    up_sum = z_reduce(y_sum(up_mine, up_theirs).reshape(TOK, 1024))
+    up_recv = swap(up_theirs, "y")
+    res_blocks = team_gather(res_low, up_theirs)
+    out_mine, out_theirs = call(out_grad_kernel, (sds((128, D)), sds((128, D), LOW)), at, (*res_blocks, attended))
+    out_recv = swap(out_theirs, "y")
+    qkv_mine, qkv_theirs, mixed_low, bias_sums = call(
+        backward_kernel,
+        (sds((4, 128, 768)), sds((4, 128, 768), LOW), sds((TOK, 768), LOW), sds((8, 256))),
+        at,
+        (*res_blocks, out_weight, qkv_low, seg_ids, normed1),
+        [pltpu.VMEM((D, 768), jnp.float32), pltpu.VMEM((TOK, 256), LOW)],
+    )
+    qkv_recv = swap(qkv_theirs, "y")
+    vec_mine, vec_theirs, keep, send = call(
+        vector_kernel,
+        (sds((4, 16, 128)), sds((4, 16, 128), LOW), sds((256, D)), sds((256, D))),
+        at,
+        (mixed_low, qkv_weight, x_team, row_sums, pre_sum, bias_sums),
+        [pltpu.VMEM((16, D), jnp.float32)],
+    )
+    vec_recv = swap(vec_theirs, "y")
+    up_pay = y_sum(after(up_mine, qkv_theirs), up_recv).reshape(TOK, D)
+    up_sum = z_reduce(up_pay)
+    out_sum = z_reduce(y_sum(after(out_mine, qkv_theirs), out_recv))
+    own, *pieces = call(
+        fold_kernel, (sds((144, 768)),) + (sds((144, 768), LOW),) * 3, at, (qkv_mine, qkv_recv, vec_mine, vec_recv)
+    )
+    up_back = team_exchange(after(up_sum, own).reshape(4, share, 1024))
+    turned = [
+        lax.ppermute(piece, "z", [(i, (i + hop) % 4) for i in range(4)])
+        for hop, piece in zip((1, 2, 3), pieces)
+    ]
+
+    final_keep, final_send = keep, send
     keep, send = call(
-        output_kernel, "down_forward", (sds((256, D)), sds((256, D))), (at, hidden, down_own, down_far)
-    )
-    summed, near = team_reduce(keep, send)
-    output = residual + summed + near.astype(jnp.float32) + vectors[7 + FF // D]
-    res_team, out_mine, out_theirs = call(
-        out_grad_kernel,
-        "out_grad",
-        (sds((TOK, D), LOW), sds((128, D)), sds((128, D), LOW)),
-        (at, *team_gather(res_low), attended),
-        [pltpu.VMEM((256, D), jnp.float32)],
-    )
-    out_sum = z_reduce(y_sum(out_mine, out_theirs))
-    own_team = (jnp.arange(4, dtype=jnp.int32) == team_pos).astype(jnp.float32)[None, :, None]
-    grad_rows = jnp.concatenate(
-        [
-            jnp.zeros((4, D), jnp.float32),
-            row_sums[:3],
-            (pre_sum[0].reshape(2, 1, 512) * own_team).reshape(FF // D, D),
-            row_sums[3:4],
-            jnp.zeros((4, D), jnp.float32),
-        ]
-    )
-    qkv_mine, qkv_theirs, keep, send = call(
-        backward_kernel,
-        "attention_backward",
-        (sds((4, 144, 768)), sds((4, 144, 768), LOW), sds((256, D)), sds((256, D))),
-        (at, res_team, out_weight, qkv_low, normed1, x_team, qkv_weight, seg_col, seg_ids, grad_rows),
-        [
-            pltpu.VMEM((TOK, 768), LOW), pltpu.VMEM((D, 768), jnp.float32),
-            pltpu.VMEM((TOK, 256), LOW), pltpu.VMEM((16, D), jnp.float32),
-        ],
-    )
-    qkv_sum = z_reduce(y_sum(qkv_mine, qkv_theirs).reshape(576, 768))
-    vec_back = qkv_sum[4 * share :, :128].reshape(16, 4, 32).transpose(1, 0, 2)
-    qkv_back = jnp.concatenate(
-        [qkv_sum[: 4 * share].reshape(4, share, 768), jnp.pad(vec_back, ((0, 0), (0, 0), (0, 736)))], axis=1
-    )
-    qkv_back = team_exchange(qkv_back).astype(jnp.float32)
-    up_back = team_exchange(up_sum.reshape(4, share, 1024)).astype(jnp.float32)
-
-    summed, near = team_reduce(keep, send)
-    grad_normed1 = summed + near.astype(jnp.float32)
+        split_kernel, (sds((256, D)), sds((256, D))), at,
+        (after(hidden, vec_theirs), down_own, down_far),
+    )
+    output = residual + team_total(*team_reduce(keep, send)) + vectors[7 + FF // D]
+    grad_normed1 = team_total(*team_reduce(final_keep, final_send))
     _, scaled1, inverse1 = normalize(x_in.astype(jnp.float32), vectors[0], vectors[1])
     grad_input = grad_residual + normalize_back(grad_normed1, scaled1, inverse1, vectors[0])
-    owned = jnp.concatenate(
-        [
-            qkv_back[:, :share].reshape(4, share, 6, 128).transpose(1, 2, 0, 3).reshape(-1),
-            out_sum.astype(jnp.float32).reshape(-1),
-            up_back.reshape(4, share, 2, 512).transpose(1, 2, 0, 3).reshape(-1),
-            down_sum.astype(jnp.float32).reshape(-1),
-            jnp.sum(qkv_back[:, share : share + vec_rows, :32], axis=0).reshape(-1),
-        ]
-    )
-    new_params, new_first, new_second = adam(params, first_moment, second_moment, owned, share)
+
+    state = tuple(v.reshape(-1, 128) for v in (params, first_moment, second_moment))
+    early = adam_call(early_kernel, at, (*state, up_back, down_sum), (), 2048, 9)
+    (qkv_pay,) = call(join_kernel, (sds((4, 48, 768), LOW),), at, (after(own, early[0]), *turned))
+    qkv_back = team_exchange(qkv_pay)
+    final = adam_call(late_kernel, at, (*state, qkv_back, out_sum), early, 1032, 16)
+    owned, new_params, new_first, new_second = (v.reshape(-1) for v in final)
     return (output, grad_input, owned, new_params, new_first, new_second)
 
 
@@ -690,10 +901,13 @@
         axes, step = ("y", "x", "c", "z"), team_body
     else:
         axes, step = ("dp", "shard"), body
-    return jax.shard_map(
+    mapped = jax.shard_map(
         step,
         mesh=mesh,
         in_specs=(P(axes, None), P(axes, None), P(axes), P(axes), P(axes), P(), P()),
         out_specs=(P(axes, None), P(axes, None), P(axes), P(axes), P(axes), P(axes)),
         check_vma=False,
     )
+    if step is body:
+        return mapped
+    return mapped

time: 343 us -> 316 us (0.921)
  blocking collectives: 46 us -> 0 us
  Pallas kernels: 44.1 us -> 84.1 us
  local copies, waits for them, and re-layouts: 35.6 us -> 13.2 us
  other arithmetic: 30.3 us -> 21.5 us
  waiting for transfers between devices: 137 us -> 143 us
    all_gather x2 -> x0, blocking collectives: 46 us -> none  [z_gather(): return lax.all_gather(shard, 'z', axis=0, tiled=True)]
    pallas_call x9 -> x14, Pallas kernels: 44.1 us -> 84.1 us  [the longest x12 73.3 us: call(): pl.pallas_call(staged, out_shape=outs, in_specs=[pl.BlockSpec(memory_spac...]
    all_gather x2 -> x3, waiting for transfers between devices: 0.01 us -> 20.4 us  [z_gather(): return lax.all_gather(shard, 'z', axis=0, tiled=True)]
    unnamed x88 -> x60, local copies, waits for them, and re-layouts: 26.3 us -> 8.01 us
    ppermute x25, waiting for transfers between devices: 114 us -> 96.3 us  [swap(): return lax.ppermute(values, axis, SWAP)]
    all_to_all x4, waiting for transfers between devices: 8.86 us -> 15.2 us  [team_exchange(): return lax.all_to_all(values, TEAM, 0, 0, tiled=True)]
    ppermute x0 -> x3, starting transfers between devices: none -> 5.18 us  [team_step(): lax.ppermute(piece, 'z', [(i, (i + hop) % 4) for i in range(4)])]
    sub x1 -> x0, other arithmetic: 4.83 us -> none  [adam(): params - learn_rate * (ratio + decay_rate * matrix_mask * params)]
  transfers between devices with their start and end apart: 35 -> 38, of which waited for: 20 -> 20; matrix products, arithmetic and copies ran while one was open for 9% -> 7% of each run, Pallas kernels for 11% -> 20%
where the time goes in v2:
time: 316 us; the launch traced here: 315 us
  waiting for transfers between devices  143 us (45%)
  Pallas kernels  84.1 us (27%)
  starting transfers between devices  38.1 us (12%)
  other arithmetic  21.5 us (7%)
  between operations  14.7 us (5%)
  local copies, waits for them, and re-layouts  13.2 us (4%)
    ppermute x25, waiting for transfers between devices, swap(): return lax.ppermute(values, axis, SWAP)  96.3 us
    pallas_call x12, Pallas kernels, call(): pl.pallas_call(staged, out_shape=outs, in_specs=[pl.BlockSpec(memory_spac...  73.3 us
    all_gather x3, waiting for transfers between devices, z_gather(): return lax.all_gather(shard, 'z', axis=0, tiled=True)  20.4 us
    ppermute x25, starting transfers between devices, swap(): return lax.ppermute(values, axis, SWAP)  18 us
    all_to_all x4, waiting for transfers between devices, team_exchange(): return lax.all_to_all(values, TEAM, 0, 0, tiled=True)  15.2 us
    all_to_all x4, starting transfers between devices, team_exchange(): return lax.all_to_all(values, TEAM, 0, 0, tiled=True)  14.5 us
    reduce_scatter x3, waiting for transfers between devices, z_reduce(): return lax.psum_scatter(values, 'z', scatter_dimension=0, tiled=True)  10.9 us
    pallas_call x2, Pallas kernels, adam_call(): pl.pallas_call(kernel, out_shape=tuple((sds(arrays[0].shape) for _ in ran...  10.7 us
  transfers between devices with their start and end apart: 38, of which 20 were waited for; matrix products, arithmetic and copies ran while one was open for 7% of the time, Pallas kernels for 20%

profile of v2, /device:TPU:0, one launch (start us, length us, event | category | flops | bytes accessed | tf_op | source)
XLA Modules:
  0.0 315.0 jit_solution(1108213643359921778)
XLA Ops:
  7.2 1.5 convert_element_type.64
  9.8 4.2 %all-to-all-start = ((bf16[4,48,768]{2,1,0:T(8,128)(2,1)}), bf16[4,48,768]{2,1,0:T(8,128)(2,1)S(1)}, u32[]{:S(2)}, u32[]{:S(2)}) async-start(bf16[4,48,768]{2,1,0:T(8,128)(2,1)} %pad_maximum_fusion.2), calls=%async_computation | async-start | bytes 589824 | tf_op jit(solution)/shard_map/all_to_all | solution.py:263
  14.2 6.3 %all-to-all-done = bf16[4,48,768]{2,1,0:T(8,128)(2,1)S(1)} async-done(((bf16[4,48,768]{2,1,0:T(8,128)(2,1)}), bf16[4,48,768]{2,1,0:T(8,128)(2,1)S(1)}, u32[]{:S(2)}, u32[]{:S(2)}) %all-to-all-start) | async-done | bytes 294944 | tf_op jit(solution)/shard_map/all_to_all | solution.py:263
  23.3 3.4 %all-to-all-start.1 = ((bf16[4,32,1024]{2,1,0:T(8,128)(2,1)}), bf16[4,32,1024]{2,1,0:T(8,128)(2,1)S(1)}, u32[]{:S(2)}, u32[]{:S(2)}) async-start(bf16[4,32,1024]{2,1,0:T(8,128)(2,1)} %reshape.163), calls=%async_computation.1 | async-start | bytes 524288 | tf_op jit(solution)/shard_map/all_to_all | solution.py:263
  26.9 5.8 %all-to-all-done.1 = bf16[4,32,1024]{2,1,0:T(8,128)(2,1)S(1)} async-done(((bf16[4,32,1024]{2,1,0:T(8,128)(2,1)}), bf16[4,32,1024]{2,1,0:T(8,128)(2,1)S(1)}, u32[]{:S(2)}, u32[]{:S(2)}) %all-to-all-start.1) | async-done | bytes 262176 | tf_op jit(solution)/shard_map/all_to_all | solution.py:263
  33.5 0.9 convert_bitcast_fusion
  35.0 16.1 %all-gather.4.cloned.1.call-done = bf16[704,768]{1,0:T(8,128)(2,1)} async-done(((bf16[176,768]{1,0:T(8,128)(2,1)}), bf16[704,768]{1,0:T(8,128)(2,1)}) %all-gather.4.cloned.1.call-update) | async-done | bytes 1081360 | tf_op jit(solution)/shard_map/all_gather | solution.py:255
  51.0 1.5 collective-permute-start.3
  55.4 1.3 pad_maximum_fusion
  56.7 1.5 fusion.22
  58.2 18.2 %collective-permute-done.3.refs_2_ = bf16[4,176,768]{2,1,0:T(8,128)(2,1)S(1)} collective-permute-done((bf16[4,176,768]{2,1,0:T(8,128)(2,1)}, bf16[4,176,768]{2,1,0:T(8,128)(2,1)S(1)}, u32[]{:S(2)}, u32[]{:S(2)}) %collective-permute-start.3) | collective-permute-done | bytes 1081376 | tf_op jit(solution)/shard_map/ppermute | solution.py:251
  76.4 1.0 copy-done.9
  77.3 10.4 %shard_map.118 = (f32[16,1024]{1,0:T(8,128)}, bf16[1024,768]{1,0:T(8,128)(2,1)}, bf16[256,1024]{1,0:T(8,128)(2,1)}, bf16[512,1024]{1,0:T(8,128)(2,1)}, bf16[512,...) custom-call(s32[3]{0:T(128)} %pad_add_fusion.at_ref.at, ...), custom_call_target="tpu_custom_call" | custom-call | tf_op jit(solution)/shard_map/pallas_call | solution.py:325
  87.8 2.9 collective-permute-done.4.refs_2_
  90.7 1.5 fusion.17
  92.1 1.5 collective-permute-start.5
  93.7 1.4 collective-permute-start.9
  95.0 5.5 %collective-permute-done.5.refs_3_ = bf16[128,1024]{1,0:T(8,128)(2,1)S(1)} collective-permute-done((bf16[128,1024]{1,0:T(8,128)(2,1)S(1)}, bf16[128,1024]{1,0:T(8,128)(2,1)S(1)}, u32[]{:S(2)}, u32[]{:S(2)}) %collective-permute-start.5) | collective-permute-done | bytes 262176 | tf_op jit(solution)/shard_map/ppermute | solution.py:251
  101.3 3.4 %shard_map.119 = (f32[128,1024]{1,0:T(8,128)}, bf16[128,1024]{1,0:T(8,128)(2,1)}) custom-call(s32[3]{0:T(128)} %pad_add_fusion.at_ref.at, bf16[128,1024]{1,0:T(8,128)(2,1)} %refs_0_.1, f32[256,1024]{1,0:T(8,128)} %get-tuple-element.70.refs_1_, f32[256,1024]{1,0:T(8,128)} %copy-done.4, bf16[128,1024]{1,0:T(8,128)(2,1)} %copy-done.25, ...), custom_call_target="tpu_custom_call" | custom-call | tf_op jit(solution)/shard_map/pallas_call | solution.py:325
  104.6 4.3 %all-gather.8.cloned.1.call-done.refs_1_ = bf16[512,1024]{1,0:T(8,128)(2,1)} async-done(((bf16[128,1024]{1,0:T(8,128)(2,1)}), bf16[512,1024]{1,0:T(8,128)(2,1)}) %all-gather.8.cloned.1.call-update) | async-done | bytes 1048592 | tf_op jit(solution)/shard_map/all_gather | solution.py:255
  109.0 1.5 collective-permute-start.10
  110.5 1.5 collective-permute-start.6
  111.9 6.0 %collective-permute-done.6.refs_1_ = bf16[128,1024]{1,0:T(8,128)(2,1)S(1)} collective-permute-done((bf16[128,1024]{1,0:T(8,128)(2,1)}, bf16[128,1024]{1,0:T(8,128)(2,1)S(1)}, u32[]{:S(2)}, u32[]{:S(2)}) %collective-permute-start.6) | collective-permute-done | bytes 262176 | tf_op jit(solution)/shard_map/ppermute | solution.py:251
  117.9 1.9 collective-permute-done.9.refs_5_
  119.9 0.9 copy-done.10
  121.0 8.4 %shard_map.120 = (bf16[512,1024]{1,0:T(8,128)(2,1)}, bf16[1024,1024]{1,0:T(8,128)(2,1)}, bf16[512,1024]{1,0:T(8,128)(2,1)}, f32[512,1024]{1,0:T(8,128)}, f32[512,1024]{1,0:T(8,128)}, /*index=5*/bf16[512,1024]{1,0:T(8,128)(2,1)}) custom-call(s32[3]{0:T(128)} %pad_add_fusion.at_ref.at, bf16[128,1024]{1,0:T(8,128)(2,1)} %get-tuple-element.74.refs_0_, ...), custom_call_target="tpu_custom_call" | custom-call | tf_op jit(solution)/shard_map/pallas_call | solution.py:325
  129.4 11.9 %collective-permute-done.10.refs_2_ = bf16[512,1024]{1,0:T(8,128)(2,1)S(1)} collective-permute-done((bf16[512,1024]{1,0:T(8,128)(2,1)}, bf16[512,1024]{1,0:T(8,128)(2,1)S(1)}, u32[]{:S(2)}, u32[]{:S(2)}) %collective-permute-start.10) | collective-permute-done | bytes 1048608 | tf_op jit(solution)/shard_map/ppermute | solution.py:251
  141.3 1.0 copy-done.2
  142.2 8.6 %shard_map.121 = (bf16[512,1024]{1,0:T(8,128)(2,1)}, f32[8,1024]{1,0:T(8,128)}, f32[256,1024]{1,0:T(8,128)}, f32[256,1024]{1,0:T(8,128)}) custom-call(s32[3]{0:T(128)} %pad_add_fusion.at_ref.at, bf16[512,1024]{1,0:T(8,128)(2,1)} %bitcast.41, bf16[512,1024]{1,0:T(8,128)(2,1)} %all-gather.8.cloned.1.call-done.refs_1_, bf16[512,1024]{1,0:T(8,128)(2,1)} %copy-done.2, ...), custom_call_target="tpu_custom_call" | custom-call | tf_op jit(solution)/shard_map/pallas_call | solution.py:325
  150.9 1.5 collective-permute-start.13
  152.4 1.4 collective-permute-done.11.refs_2_
  153.8 2.2 fusion.16
  156.5 20.2 %collective-permute-done.13 = bf16[512,1024]{1,0:T(8,128)(2,1)S(1)} collective-permute-done((bf16[512,1024]{1,0:T(8,128)(2,1)}, bf16[512,1024]{1,0:T(8,128)(2,1)S(1)}, u32[]{:S(2)}, u32[]{:S(2)}) %collective-permute-start.13) | collective-permute-done | bytes 1048608 | tf_op jit(solution)/shard_map/ppermute | solution.py:251
  176.7 1.4 add_convert_fusion.1
  178.8 4.1 %shard_map.122 = (f32[128,1024]{1,0:T(8,128)}, bf16[128,1024]{1,0:T(8,128)(2,1)}, f32[8,1024]{1,0:T(8,128)}) custom-call(s32[3]{0:T(128)} %pad_add_fusion.at_ref.at, f32[128,1024]{1,0:T(8,128)} %get-tuple-element.73.refs_0_, f32[256,1024]{1,0:T(8,128)} %get-tuple-element.80.refs_1_, f32[256,1024]{1,0:T(8,128)} %copy-done.3, bf16[128,1024]{1,0:T(8,128)(2,1)} %copy-done.24, ...), custom_call_target="tpu_custom_call" | custom-call | tf_op jit(solution)/shard_map/pallas_call | solution.py:325
  182.9 5.5 %shard_map.123 = (f32[4,128,1024]{2,1,0:T(8,128)}, bf16[4,128,1024]{2,1,0:T(8,128)(2,1)}) custom-call(s32[3]{0:T(128)} %pad_add_fusion.at_ref.at, bf16[512,1024]{1,0:T(8,128)(2,1)} %get-tuple-element.88.refs_0_, bf16[512,1024]{1,0:T(8,128)(2,1)} %get-tuple-element.90.refs_1_), custom_call_target="tpu_custom_call" | custom-call | tf_op jit(solution)/shard_map/pallas_call | solution.py:325
  188.4 1.5 collective-permute-start.23
  190.5 6.9 %collective-permute-done.14.refs_1_ = bf16[128,1024]{1,0:T(8,128)(2,1)S(1)} collective-permute-done((bf16[128,1024]{1,0:T(8,128)(2,1)S(1)}, bf16[128,1024]{1,0:T(8,128)(2,1)S(1)}, u32[]{:S(2)}, u32[]{:S(2)}) %collective-permute-start.14) | collective-permute-done | bytes 262176 | tf_op jit(solution)/shard_map/ppermute | solution.py:251
  197.4 1.5 collective-permute-done.16.refs_3_
  199.6 13.2 %shard_map.124 = (f32[4,128,768]{2,1,0:T(8,128)}, bf16[4,128,768]{2,1,0:T(8,128)(2,1)}, bf16[512,768]{1,0:T(8,128)(2,1)}, f32[8,256]{1,0:T(8,128)}) custom-call(s32[3]{0:T(128)} %pad_add_fusion.at_ref.at, bf16[128,1024]{1,0:T(8,128)(2,1)} %get-tuple-element.87.refs_0_, bf16[128,1024]{1,0:T(8,128)(2,1)} %copy-done.12, bf16[128,1024]{1,0:T(8,128)(2,1)} %copy-done.13, ...), custom_call_target="tpu_custom_call" | custom-call | tf_op jit(solution)/shard_map/pallas_call | solution.py:325
  213.4 2.6 add_convert_fusion
  216.7 4.9 %shard_map.125 = (f32[4,16,128]{2,1,0:T(8,128)}, bf16[4,16,128]{2,1,0:T(8,128)(2,1)}, f32[256,1024]{1,0:T(8,128)}, f32[256,1024]{1,0:T(8,128)}) custom-call(s32[3]{0:T(128)} %pad_add_fusion.at_ref.at, bf16[512,768]{1,0:T(8,128)(2,1)} %get-tuple-element.96.refs_0_, bf16[1024,768]{1,0:T(8,128)(2,1)} %get-tuple-element.97.refs_1_, bf16[512,1024]{1,0:T(8,128)(2,1)} %bitcast.38, ...), custom_call_target="tpu_custom_call" | custom-call | tf_op jit(solution)/shard_map/pallas_call | solution.py:325
  221.6 4.9 %shard_map.126 = (f32[256,1024]{1,0:T(8,128)}, f32[256,1024]{1,0:T(8,128)}) custom-call(s32[3]{0:T(128)} %pad_add_fusion.at_ref.at, bf16[512,1024]{1,0:T(8,128)(2,1)} %get-tuple-element.101.refs_0_, bf16[512,1024]{1,0:T(8,128)(2,1)} %all-gather.8.cloned.1.call-done.refs_1_, bf16[512,1024]{1,0:T(8,128)(2,1)} %copy-done.2), custom_call_target="tpu_custom_call" | custom-call | tf_op jit(solution)/shard_map/pallas_call | solution.py:325
  227.5 1.5 collective-permute-start.21
  229.0 3.8 %shard_map.130 = (f32[128,1024]{1,0:T(8,128)}, bf16[128,1024]{1,0:T(8,128)(2,1)}) custom-call(s32[3]{0:T(128)} %pad_add_fusion.at_ref.at, bf16[128,1024]{1,0:T(8,128)(2,1)} %get-tuple-element.87.refs_0_, bf16[128,1024]{1,0:T(8,128)(2,1)} %copy-done.12, bf16[128,1024]{1,0:T(8,128)(2,1)} %copy-done.13, bf16[128,1024]{1,0:T(8,128)(2,1)} %copy-done.14, ...), custom_call_target="tpu_custom_call" | custom-call | tf_op jit(solution)/shard_map/pallas_call | solution.py:325
  234.2 1.5 collective-permute-start.22
  235.7 1.1 fusion.12
  237.6 15.5 %collective-permute-done.27 = bf16[128,1024]{1,0:T(8,128)(2,1)S(1)} collective-permute-done((bf16[128,1024]{1,0:T(8,128)(2,1)}, bf16[128,1024]{1,0:T(8,128)(2,1)S(1)}, u32[]{:S(2)}, u32[]{:S(2)}) %collective-permute-start.27) | collective-permute-done | bytes 262176 | tf_op jit(solution)/shard_map/ppermute | solution.py:251
  253.1 1.8 add_convert_fusion.2
  255.5 3.4 %shard_map.127 = (f32[144,768]{1,0:T(8,128)}, bf16[144,768]{1,0:T(8,128)(2,1)}, bf16[144,768]{1,0:T(8,128)(2,1)}, bf16[144,768]{1,0:T(8,128)(2,1)}) custom-call(s32[3]{0:T(128)} %pad_add_fusion.at_ref.at, f32[4,128,768]{2,1,0:T(8,128)} %get-tuple-element.107.refs_0_, bf16[4,128,768]{2,1,0:T(8,128)(2,1)} %collective-permute-done.21.refs_1_, ...), custom_call_target="tpu_custom_call" | custom-call | tf_op jit(solution)/shard_map/pallas_call | solution.py:325
  258.9 1.6 collective-permute-start.24
  260.5 1.4 collective-permute-start.25
  261.9 2.2 collective-permute-start.26
  264.7 2.1 fusion.15
  266.8 3.9 %collective-permute-done.20 = bf16[128,1024]{1,0:T(8,128)(2,1)S(1)} collective-permute-done((bf16[128,1024]{1,0:T(8,128)(2,1)S(1)}, bf16[128,1024]{1,0:T(8,128)(2,1)S(1)}, u32[]{:S(2)}, u32[]{:S(2)}) %collective-permute-start.20) | collective-permute-done | bytes 262176 | tf_op jit(solution)/shard_map/ppermute | solution.py:251
  271.0 3.4 %all-to-all-start.2 = ((bf16[4,32,1024]{2,1,0:T(8,128)(2,1)}), bf16[4,32,1024]{2,1,0:T(8,128)(2,1)S(1)}, u32[]{:S(2)}, u32[]{:S(2)}) async-start(bf16[4,32,1024]{2,1,0:T(8,128)(2,1)} %bitcast.62), calls=%async_computation.3 | async-start | bytes 524288 | tf_op jit(solution)/shard_map/all_to_all | solution.py:263
  274.4 2.8 reduce-scatter.6.cloned.1.call-done.down_hbm
  277.2 3.1 all-to-all-done.2.up_hbm
  281.1 6.4 %shard_map.128 = (f32[3075,128]{1,0:T(8,128)}, f32[3075,128]{1,0:T(8,128)}, f32[3075,128]{1,0:T(8,128)}, f32[3075,128]{1,0:T(8,128)}) custom-call(s32[3]{0:T(128)} %pad_add_fusion.at_ref.at, f32[3075,128]{1,0:T(8,128)} %bitcast.35, f32[3075,128]{1,0:T(8,128)} %bitcast.42, f32[3075,128]{1,0:T(8,128)} %bitcast.44, bf16[4,32,1024]{2,1,0:T(8,128)(2,1)} %copy-done.16, ...), custom_call_target="tpu_custom_call" | custom-call | tf_op jit(solution)/shard_map/pallas_call | solution.py:729
  287.5 3.0 shard_map.129
  290.5 3.5 %all-to-all-start.3 = ((bf16[4,48,768]{2,1,0:T(8,128)(2,1)}), bf16[4,48,768]{2,1,0:T(8,128)(2,1)S(1)}, u32[]{:S(2)}, u32[]{:S(2)}) async-start(bf16[4,48,768]{2,1,0:T(8,128)(2,1)} %shard_map.129), calls=%async_computation.5 | async-start | bytes 589824 | tf_op jit(solution)/shard_map/all_to_all | solution.py:263
  294.0 1.0 fusion.7
  295.0 8.1 %reduce-scatter.8.cloned.1.call-done.out_hbm = bf16[32,1024]{1,0:T(8,128)(2,1)} async-done(((bf16[128,1024]{1,0:T(8,128)(2,1)}), bf16[32,1024]{1,0:T(8,128)(2,1)}) %reduce-scatter.8.cloned.1.call-update) | async-done | bytes 65552 | tf_op jit(solution)/shard_map/reduce_scatter | solution.py:259
  303.8 4.3 %shard_map.131 = (f32[3075,128]{1,0:T(8,128)}, f32[3075,128]{1,0:T(8,128)}, f32[3075,128]{1,0:T(8,128)}, f32[3075,128]{1,0:T(8,128)}) custom-call(s32[3]{0:T(128)} %pad_add_fusion.at_ref.at, f32[3075,128]{1,0:T(8,128)} %bitcast.36, f32[3075,128]{1,0:T(8,128)} %bitcast.43, ...), custom_call_target="tpu_custom_call", output_to_operand_aliasing={{0}: (6, {}), {1}: (7, {}), {2}: (8, {}), {3}: (9, {})} | custom-call | tf_op jit(solution)/shard_map/pallas_call | solution.py:729
  (147 shorter events, 19.3 us)
Async XLA Ops:
  9.8 10.6 %all-to-all-start = ((bf16[4,48,768]{2,1,0:T(8,128)(2,1)}), bf16[4,48,768]{2,1,0:T(8,128)(2,1)S(1)}, u32[]{:S(2)}, u32[]{:S(2)}) async-start(bf16[4,48,768]{2,1,0:T(8,128)(2,1)} %pad_maximum_fusion.2), calls=%async_computation | async-start | bytes 589824 | tf_op jit(solution)/shard_map/all_to_all | solution.py:263
  14.1 36.9 %all-gather.4.cloned.1.call-start = ((), (), s32[]{:S(2)}) async-start(), calls=%async_computation.7 | async-start | bytes 1351680 | tf_op jit(solution)/shard_map/all_gather | solution.py:255
  14.1 8.7 %copy-start.27 = (s32[128]{0:T(128)S(1)}, s32[128]{0:T(128)}, u32[]{:S(2)}) copy-start(s32[128]{0:T(128)} %param.12) | copy-start | bytes 1540
  14.1 8.7 %copy-start.28 = (s32[128]{0:T(128)S(1)}, s32[128]{0:T(128)}, u32[]{:S(2)}) copy-start(s32[128]{0:T(128)} %param.13) | copy-start | bytes 1540
  20.6 12.9 %copy-start.19 = (f32[128,1024]{1,0:T(8,128)S(1)}, f32[128,1024]{1,0:T(8,128)}, u32[]{:S(2)}) copy-start(f32[128,1024]{1,0:T(8,128)} %param.8) | copy-start | bytes 1572868
  21.4 13.1 %copy-start = (bf16[128,1024]{1,0:T(8,128)(2,1)S(1)}, bf16[128,1024]{1,0:T(8,128)(2,1)}, u32[]{:S(2)}) copy-start(bf16[128,1024]{1,0:T(8,128)(2,1)} %refs_0_.1) | copy-start | bytes 786436
  23.3 9.4 %all-to-all-start.1 = ((bf16[4,32,1024]{2,1,0:T(8,128)(2,1)}), bf16[4,32,1024]{2,1,0:T(8,128)(2,1)S(1)}, u32[]{:S(2)}, u32[]{:S(2)}) async-start(bf16[4,32,1024]{2,1,0:T(8,128)(2,1)} %reshape.163), calls=%async_computation.1 | async-start | bytes 524288 | tf_op jit(solution)/shard_map/all_to_all | solution.py:263
  26.8 66.9 %all-gather.6.cloned.1.call-start = ((), (), s32[]{:S(2)}) async-start(), calls=%async_computation.8 | async-start | bytes 1310720 | tf_op jit(solution)/shard_map/all_gather | solution.py:255
  33.5 75.5 %all-gather.8.cloned.1.call-start = ((), (), s32[]{:S(2)}) async-start(), calls=%async_computation.9 | async-start | bytes 1310720 | tf_op jit(solution)/shard_map/all_gather | solution.py:255
  34.5 18.0 %collective-permute-start = (bf16[2,128,1024]{2,1,0:T(8,128)(2,1)S(1)}, bf16[2,128,1024]{2,1,0:T(8,128)(2,1)S(1)}, u32[]{:S(2)}, u32[]{:S(2)}) collective-permute-start(bf16[2,128,1024]{2,1,0:T(8,128)(2,1)S(1)} %pad_maximum_fusion.1), channel_id=1, source_target_pairs={{0,8},{8,0},{1,9},{9,1},{2,10},{10,2},{3,11},{11,3},{4,12},{12,4},... | collective-permute-start | bytes 1572872 | tf_op jit(solution)/shard_map/ppermute | solution.py:251
  51.0 25.4 %collective-permute-start.3 = (bf16[4,176,768]{2,1,0:T(8,128)(2,1)}, bf16[4,176,768]{2,1,0:T(8,128)(2,1)S(1)}, u32[]{:S(2)}, u32[]{:S(2)}) collective-permute-start(bf16[4,176,768]{2,1,0:T(8,128)(2,1)} %bitcast.52), channel_id=1, source_target_pairs={{0,16},{16,0},{1,17},{17,1},{2,18},{18,2},{3,19},{19,3},{4,20},{20... | collective-permute-start | bytes 3244040 | tf_op jit(solution)/shard_map/ppermute | solution.py:251
  52.5 2.9 collective-permute-start.1
  52.5 2.9 collective-permute-start.2
  55.2 215.8 %reduce-scatter.4.cloned.1.call-start = ((), (), s32[]{:S(2)}) async-start(), calls=%async_computation.10 | async-start | bytes 1310720 | tf_op jit(solution)/shard_map/reduce_scatter | solution.py:259
  76.4 1.0 copy-start.9
  87.7 2.9 collective-permute-start.4
  90.7 9.9 %copy-start.4 = (f32[256,1024]{1,0:T(8,128)}, f32[256,1024]{1,0:T(8,128)S(1)}, u32[]{:S(2)}) copy-start(f32[256,1024]{1,0:T(8,128)S(1)} %collective-permute-done.4.refs_2_) | copy-start | bytes 3145732
  92.1 8.4 %collective-permute-start.5 = (bf16[128,1024]{1,0:T(8,128)(2,1)S(1)}, bf16[128,1024]{1,0:T(8,128)(2,1)S(1)}, u32[]{:S(2)}, u32[]{:S(2)}) collective-permute-start(bf16[128,1024]{1,0:T(8,128)(2,1)S(1)} %fusion.17), channel_id=1, source_target_pairs={{0,8},{8,0},{1,9},{9,1},{2,10},{10,2},{3,11},{11,3},{4,12},{12,4},... | collective-permute-start | bytes 786440 | tf_op jit(solution)/shard_map/ppermute | solution.py:251
  93.7 26.2 %collective-permute-start.9 = (bf16[4,128,1024]{2,1,0:T(8,128)(2,1)}, bf16[4,128,1024]{2,1,0:T(8,128)(2,1)S(1)}, u32[]{:S(2)}, u32[]{:S(2)}) collective-permute-start(bf16[4,128,1024]{2,1,0:T(8,128)(2,1)} %bitcast.54), channel_id=1, source_target_pairs={{0,16},{16,0},{1,17},{17,1},{2,18},{18,2},{3,19},{19,3},{4,20},{20... | collective-permute-start | bytes 3145736 | tf_op jit(solution)/shard_map/ppermute | solution.py:251
  109.0 32.3 %collective-permute-start.10 = (bf16[512,1024]{1,0:T(8,128)(2,1)}, bf16[512,1024]{1,0:T(8,128)(2,1)S(1)}, u32[]{:S(2)}, u32[]{:S(2)}) collective-permute-start(bf16[512,1024]{1,0:T(8,128)(2,1)} %all-gather.8.cloned.1.call-done.refs_1_), channel_id=1, source_target_pairs={{0,16},{16,0},{1,17},{17,1},{2,18},{18,2},{3,19},{19,3},{4,20},{20... | collective-permute-start | bytes 3145736 | tf_op jit(solution)/shard_map/ppermute | solution.py:251
  110.5 7.5 %collective-permute-start.6 = (bf16[128,1024]{1,0:T(8,128)(2,1)}, bf16[128,1024]{1,0:T(8,128)(2,1)S(1)}, u32[]{:S(2)}, u32[]{:S(2)}) collective-permute-start(bf16[128,1024]{1,0:T(8,128)(2,1)} %get-tuple-element.74.refs_0_), channel_id=1, source_target_pairs={{0,8},{8,0},{1,9},{9,1},{2,10},{10,2},{3,11},{11,3},{4,12},{12,4},... | collective-permute-start | bytes 786440 | tf_op jit(solution)/shard_map/ppermute | solution.py:251
  111.9 8.0 %collective-permute-start.7 = (bf16[128,1024]{1,0:T(8,128)(2,1)}, bf16[128,1024]{1,0:T(8,128)(2,1)S(1)}, u32[]{:S(2)}, u32[]{:S(2)}) collective-permute-start(bf16[128,1024]{1,0:T(8,128)(2,1)} %get-tuple-element.74.refs_0_), channel_id=1, source_target_pairs={{0,4},{4,0},{1,5},{5,1},{2,6},{6,2},{3,7},{7,3},{8,12},{12,8},{9,1... | collective-permute-start | bytes 786440 | tf_op jit(solution)/shard_map/ppermute | solution.py:251
  117.9 2.0 copy-start.21
  117.9 2.0 collective-permute-start.8
  119.9 1.0 copy-start.10
  119.9 1.0 copy-start.22
  119.9 1.1 copy-start.23
  141.3 1.0 copy-start.2
  142.2 34.5 %copy-start.5 = (f32[512,1024]{1,0:T(8,128)S(1)}, f32[512,1024]{1,0:T(8,128)}, u32[]{:S(2)}) copy-start(f32[512,1024]{1,0:T(8,128)} %get-tuple-element.84) | copy-start | bytes 6291460
  150.8 2.9 collective-permute-start.11
  150.9 25.8 %collective-permute-start.13 = (bf16[512,1024]{1,0:T(8,128)(2,1)}, bf16[512,1024]{1,0:T(8,128)(2,1)S(1)}, u32[]{:S(2)}, u32[]{:S(2)}) collective-permute-start(bf16[512,1024]{1,0:T(8,128)(2,1)} %get-tuple-element.85), channel_id=1, source_target_pairs={{0,16},{16,0},{1,17},{17,1},{2,18},{18,2},{3,19},{19,3},{4,20},{20... | collective-permute-start | bytes 3145736 | tf_op jit(solution)/shard_map/ppermute | solution.py:251
  153.8 24.3 %copy-start.3 = (f32[256,1024]{1,0:T(8,128)}, f32[256,1024]{1,0:T(8,128)S(1)}, u32[]{:S(2)}) copy-start(f32[256,1024]{1,0:T(8,128)S(1)} %collective-permute-done.11.refs_2_) | copy-start | bytes 3145732
  155.9 22.2 %collective-permute-start.12 = (bf16[128,1024]{1,0:T(8,128)(2,1)}, bf16[128,1024]{1,0:T(8,128)(2,1)S(1)}, u32[]{:S(2)}, u32[]{:S(2)}) collective-permute-start(bf16[128,1024]{1,0:T(8,128)(2,1)} %fusion.16), channel_id=1, source_target_pairs={{0,8},{8,0},{1,9},{9,1},{2,10},{10,2},{3,11},{11,3},{4,12},{12,4},... | collective-permute-start | bytes 786440 | tf_op jit(solution)/shard_map/ppermute | solution.py:251
  178.1 0.7 copy-start.24
  182.9 6.9 %copy-start.11 = (bf16[128,1024]{1,0:T(8,128)(2,1)S(1)}, bf16[128,1024]{1,0:T(8,128)(2,1)}, u32[]{:S(2)}) copy-start(bf16[128,1024]{1,0:T(8,128)(2,1)} %get-tuple-element.87.refs_0_) | copy-start | bytes 786436
  188.4 25.0 %copy-start.6 = (f32[4,128,1024]{2,1,0:T(8,128)S(1)}, f32[4,128,1024]{2,1,0:T(8,128)}, u32[]{:S(2)}) copy-start(f32[4,128,1024]{2,1,0:T(8,128)} %get-tuple-element.112) | copy-start | bytes 6291460
  188.4 25.0 %collective-permute-start.23 = (bf16[4,128,1024]{2,1,0:T(8,128)(2,1)}, bf16[4,128,1024]{2,1,0:T(8,128)(2,1)}, u32[]{:S(2)}, u32[]{:S(2)}) collective-permute-start(bf16[4,128,1024]{2,1,0:T(8,128)(2,1)} %get-tuple-element.91), channel_id=1, source_target_pairs={{0,16},{16,0},{1,17},{17,1},{2,18},{18,2},{3,19},{19,3},{4,20},{20... | collective-permute-start | bytes 3145736 | tf_op jit(solution)/shard_map/ppermute | solution.py:251
  189.8 7.5 %collective-permute-start.14 = (bf16[128,1024]{1,0:T(8,128)(2,1)S(1)}, bf16[128,1024]{1,0:T(8,128)(2,1)S(1)}, u32[]{:S(2)}, u32[]{:S(2)}) collective-permute-start(bf16[128,1024]{1,0:T(8,128)(2,1)S(1)} %copy-done.11), channel_id=1, source_target_pairs={{0,8},{8,0},{1,9},{9,1},{2,10},{10,2},{3,11},{11,3},{4,12},{12,4},... | collective-permute-start | bytes 786440 | tf_op jit(solution)/shard_map/ppermute | solution.py:251
  190.5 6.9 %collective-permute-start.15 = (bf16[128,1024]{1,0:T(8,128)(2,1)S(1)}, bf16[128,1024]{1,0:T(8,128)(2,1)S(1)}, u32[]{:S(2)}, u32[]{:S(2)}) collective-permute-start(bf16[128,1024]{1,0:T(8,128)(2,1)S(1)} %copy-done.11), channel_id=1, source_target_pairs={{0,4},{4,0},{1,5},{5,1},{2,6},{6,2},{3,7},{7,3},{8,12},{12,8},{9,1... | collective-permute-start | bytes 786440 | tf_op jit(solution)/shard_map/ppermute | solution.py:251
  197.3 1.5 copy-start.12
  197.3 1.5 collective-permute-start.16
  197.3 1.5 copy-start.13
  198.9 0.7 copy-start.14
  216.0 61.2 %reduce-scatter.6.cloned.1.call-start = ((), (), s32[]{:S(2)}) async-start(), calls=%async_computation.11 | async-start | bytes 1310720 | tf_op jit(solution)/shard_map/reduce_scatter | solution.py:259
  216.6 86.4 %reduce-scatter.8.cloned.1.call-start = ((), (), s32[]{:S(2)}) async-start(), calls=%async_computation.12 | async-start | bytes 327680 | tf_op jit(solution)/shard_map/reduce_scatter | solution.py:259
  221.6 5.0 %copy-start.1 = (bf16[128,1024]{1,0:T(8,128)(2,1)S(1)}, bf16[128,1024]{1,0:T(8,128)(2,1)}, u32[]{:S(2)}) copy-start(bf16[128,1024]{1,0:T(8,128)(2,1)} %refs_0_.1) | copy-start | bytes 786436
  221.6 12.6 %copy-start.29 = (bf16[4,16,128]{2,1,0:T(8,128)(2,1)S(1)}, bf16[4,16,128]{2,1,0:T(8,128)(2,1)}, u32[]{:S(2)}) copy-start(bf16[4,16,128]{2,1,0:T(8,128)(2,1)} %get-tuple-element.100) | copy-start | bytes 49156
  226.5 9.2 %copy-start.18 = (f32[256,1024]{1,0:T(8,128)S(1)}, f32[256,1024]{1,0:T(8,128)}, u32[]{:S(2)}) copy-start(f32[256,1024]{1,0:T(8,128)} %get-tuple-element.102) | copy-start | bytes 3145732
  226.5 9.2 %collective-permute-start.17 = (f32[256,1024]{1,0:T(8,128)}, f32[256,1024]{1,0:T(8,128)}, u32[]{:S(2)}, u32[]{:S(2)}) collective-permute-start(f32[256,1024]{1,0:T(8,128)} %get-tuple-element.103), channel_id=1, source_target_pairs={{0,4},{4,0},{1,5},{5,1},{2,6},{6,2},{3,7},{7,3},{8,12},{12,8},{9,1... | collective-permute-start | bytes 3145736 | tf_op jit(solution)/shard_map/ppermute | solution.py:251
  226.8 37.3 %collective-permute-start.19 = (f32[256,1024]{1,0:T(8,128)}, f32[256,1024]{1,0:T(8,128)S(1)}, u32[]{:S(2)}, u32[]{:S(2)}) collective-permute-start(f32[256,1024]{1,0:T(8,128)} %get-tuple-element.106), channel_id=1, source_target_pairs={{0,4},{4,0},{1,5},{5,1},{2,6},{6,2},{3,7},{7,3},{8,12},{12,8},{9,1... | collective-permute-start | bytes 3145736 | tf_op jit(solution)/shard_map/ppermute | solution.py:251
  227.5 27.4 %collective-permute-start.21 = (bf16[4,128,768]{2,1,0:T(8,128)(2,1)}, bf16[4,128,768]{2,1,0:T(8,128)(2,1)}, u32[]{:S(2)}, u32[]{:S(2)}) collective-permute-start(bf16[4,128,768]{2,1,0:T(8,128)(2,1)} %get-tuple-element.108), channel_id=1, source_target_pairs={{0,16},{16,0},{1,17},{17,1},{2,18},{18,2},{3,19},{19,3},{4,20},{20... | collective-permute-start | bytes 2359304 | tf_op jit(solution)/shard_map/ppermute | solution.py:251
  232.8 20.3 %collective-permute-start.27 = (bf16[128,1024]{1,0:T(8,128)(2,1)}, bf16[128,1024]{1,0:T(8,128)(2,1)S(1)}, u32[]{:S(2)}, u32[]{:S(2)}) collective-permute-start(bf16[128,1024]{1,0:T(8,128)(2,1)} %get-tuple-element.122), channel_id=1, source_target_pairs={{0,16},{16,0},{1,17},{17,1},{2,18},{18,2},{3,19},{19,3},{4,20},{20... | collective-permute-start | bytes 786440 | tf_op jit(solution)/shard_map/ppermute | solution.py:251
  234.2 20.7 %collective-permute-start.22 = (bf16[4,16,128]{2,1,0:T(8,128)(2,1)S(1)}, bf16[4,16,128]{2,1,0:T(8,128)(2,1)S(1)}, u32[]{:S(2)}, u32[]{:S(2)}) collective-permute-start(bf16[4,16,128]{2,1,0:T(8,128)(2,1)S(1)} %copy-done.29), channel_id=1, source_target_pairs={{0,16},{16,0},{1,17},{17,1},{2,18},{18,2},{3,19},{19,3},{4,20},{20... | collective-permute-start | bytes 49160 | tf_op jit(solution)/shard_map/ppermute | solution.py:251
  236.8 27.3 %copy-start.15 = (f32[256,1024]{1,0:T(8,128)S(1)}, f32[256,1024]{1,0:T(8,128)}, u32[]{:S(2)}) copy-start(f32[256,1024]{1,0:T(8,128)} %get-tuple-element.105) | copy-start | bytes 3145732
  236.8 27.8 %collective-permute-start.18 = (bf16[128,1024]{1,0:T(8,128)(2,1)S(1)}, bf16[128,1024]{1,0:T(8,128)(2,1)S(1)}, u32[]{:S(2)}, u32[]{:S(2)}) collective-permute-start(bf16[128,1024]{1,0:T(8,128)(2,1)S(1)} %fusion.12), channel_id=1, source_target_pairs={{0,8},{8,0},{1,9},{9,1},{2,10},{10,2},{3,11},{11,3},{4,12},{12,4},... | collective-permute-start | bytes 786440 | tf_op jit(solution)/shard_map/ppermute | solution.py:251
  254.9 9.8 %copy-start.7 = (f32[128,1024]{1,0:T(8,128)S(1)}, f32[128,1024]{1,0:T(8,128)}, u32[]{:S(2)}) copy-start(f32[128,1024]{1,0:T(8,128)} %get-tuple-element.73.refs_0_) | copy-start | bytes 1572868
  258.9 28.6 %collective-permute-start.24 = (bf16[144,768]{1,0:T(8,128)(2,1)}, bf16[144,768]{1,0:T(8,128)(2,1)}, u32[]{:S(2)}, u32[]{:S(2)}) collective-permute-start(bf16[144,768]{1,0:T(8,128)(2,1)} %get-tuple-element.116), channel_id=1, source_target_pairs={{0,1},{1,2},{2,3},{3,0},{4,5},{5,6},{6,7},{7,4},{8,9},{9,10},{10,1... | collective-permute-start | bytes 663560 | tf_op jit(solution)/shard_map/ppermute | solution.py:874
  260.5 27.0 %collective-permute-start.25 = (bf16[144,768]{1,0:T(8,128)(2,1)}, bf16[144,768]{1,0:T(8,128)(2,1)}, u32[]{:S(2)}, u32[]{:S(2)}) collective-permute-start(bf16[144,768]{1,0:T(8,128)(2,1)} %get-tuple-element.117), channel_id=1, source_target_pairs={{0,2},{1,3},{2,0},{3,1},{4,6},{5,7},{6,4},{7,5},{8,10},{9,11},{10,... | collective-permute-start | bytes 663560 | tf_op jit(solution)/shard_map/ppermute | solution.py:874
  261.9 25.6 %collective-permute-start.26 = (bf16[144,768]{1,0:T(8,128)(2,1)}, bf16[144,768]{1,0:T(8,128)(2,1)}, u32[]{:S(2)}, u32[]{:S(2)}) collective-permute-start(bf16[144,768]{1,0:T(8,128)(2,1)} %get-tuple-element.118), channel_id=1, source_target_pairs={{0,3},{1,0},{2,1},{3,2},{4,7},{5,4},{6,5},{7,6},{8,11},{9,8},{10,9... | collective-permute-start | bytes 663560 | tf_op jit(solution)/shard_map/ppermute | solution.py:874
  264.1 6.5 %collective-permute-start.20 = (bf16[128,1024]{1,0:T(8,128)(2,1)S(1)}, bf16[128,1024]{1,0:T(8,128)(2,1)S(1)}, u32[]{:S(2)}, u32[]{:S(2)}) collective-permute-start(bf16[128,1024]{1,0:T(8,128)(2,1)S(1)} %fusion.9), channel_id=1, source_target_pairs={{0,8},{8,0},{1,9},{9,1},{2,10},{10,2},{3,11},{11,3},{4,12},{12,4},... | collective-permute-start | bytes 786440 | tf_op jit(solution)/shard_map/ppermute | solution.py:251
  271.0 9.4 %all-to-all-start.2 = ((bf16[4,32,1024]{2,1,0:T(8,128)(2,1)}), bf16[4,32,1024]{2,1,0:T(8,128)(2,1)S(1)}, u32[]{:S(2)}, u32[]{:S(2)}) async-start(bf16[4,32,1024]{2,1,0:T(8,128)(2,1)} %bitcast.62), calls=%async_computation.3 | async-start | bytes 524288 | tf_op jit(solution)/shard_map/all_to_all | solution.py:263
  287.5 6.5 %copy-start.20 = (f32[128,1024]{1,0:T(8,128)S(1)}, f32[128,1024]{1,0:T(8,128)}, u32[]{:S(2)}) copy-start(f32[128,1024]{1,0:T(8,128)} %get-tuple-element.104) | copy-start | bytes 1572868
  290.5 12.6 %all-to-all-start.3 = ((bf16[4,48,768]{2,1,0:T(8,128)(2,1)}), bf16[4,48,768]{2,1,0:T(8,128)(2,1)S(1)}, u32[]{:S(2)}, u32[]{:S(2)}) async-start(bf16[4,48,768]{2,1,0:T(8,128)(2,1)} %shard_map.129), calls=%async_computation.5 | async-start | bytes 589824 | tf_op jit(solution)/shard_map/all_to_all | solution.py:263
  303.1 0.7 copy-start.8
  (4 other events, 2.7 us)
Sparse Core Ops, SparseCore 0:
  21.5 29.5 all-gather.3
  52.6 27.3 all-gather.5
  81.5 27.3 all-gather.7
  216.2 26.2 reduce-scatter.3
  244.7 32.5 reduce-scatter.5
  279.3 23.6 reduce-scatter.7

commit v3 on v2

--- a/solution.py
+++ b/solution.py
@@ -251,6 +251,14 @@
     return lax.ppermute(values, axis, SWAP)
 
 
+def hop_to(piece, hop):
+    return lax.ppermute(piece, "z", [(i, (i + hop) % 4) for i in range(4)])
+
+
+def from_hop(at, hop):
+    return lax.rem(at[2] + 4 - hop, 4)
+
+
 def z_gather(shard):
     return lax.all_gather(shard, "z", axis=0, tiled=True)
 
@@ -266,7 +274,8 @@
 def team_gather(own, dep=None):
     near = swap(own, "x")
     onward = near if dep is None else after(near, dep)
-    return (own, near, swap(own, "c"), swap(onward, "c"))
+    beside = swap(own, "c")
+    return (own, near, beside, swap(onward, "c"))
 
 
 def team_reduce(keep, send):
@@ -356,31 +365,30 @@
 
 
 def forward_kernel(at, ins, outs, tmp, ready, flush):
-    x_ref, own_ref, far_ref, seg_ref = ins
+    x_ref, seg_ref = ins[:2]
     vec_ref, weight_ref, out_ref, normed_ref, qkv_ref, att_ref, keep_ref, send_ref = outs
     y_pos, team = at[0], at[1]
     group = lane_group(16)
-    for index, ref, side in ((1, own_ref, y_pos), (2, far_ref, 1 - y_pos)):
-        ready(index)
+    vec_ref[...] = jnp.zeros_like(vec_ref)
+    for index in range(8):
+        ready(2 + index)
+        ref, side = ins[2 + index], (y_pos if index < 4 else 1 - y_pos)
+        z = from_hop(at, index % 4)
         base = side * 512
-        for z in range(4):
-            for t in range(4):
-                start = pl.multiple_of(base + t * 128 + z * 32, 32)
-                weight_ref[pl.ds(start, 32), :] = ref[z, t * 32 : (t + 1) * 32, :]
-            top = pl.multiple_of(side * 128 + z * 32, 32)
-            out_ref[pl.ds(top, 32), 0:768] = ref[z, 128:160, :]
-            out_ref[pl.ds(top, 16), 768:1024] = ref[z, 160:176, 0:256]
-            out_ref[pl.ds(pl.multiple_of(top + 16, 16), 16), 768:1024] = ref[z, 160:176, 256:512]
         for t in range(4):
-            tile = jnp.zeros((16, 128), jnp.float32)
-            for z in range(4):
-                piece = ref[z, 160:176, 512:640].astype(jnp.float32)
-                shift = (z - t) * 32 % 128
-                piece = pltpu.roll(piece, shift, 1) if shift else piece
-                tile = jnp.where(group == z, piece, tile)
-            vec_ref[:, pl.ds(pl.multiple_of(base + t * 128, 128), 128)] = tile
+            start = pl.multiple_of(base + t * 128 + z * 32, 32)
+            weight_ref[pl.ds(start, 32), :] = ref[t * 32 : (t + 1) * 32, :]
+        top = pl.multiple_of(side * 128 + z * 32, 32)
+        out_ref[pl.ds(top, 32), 0:768] = ref[128:160, :]
+        out_ref[pl.ds(top, 16), 768:1024] = ref[160:176, 0:256]
+        out_ref[pl.ds(pl.multiple_of(top + 16, 16), 16), 768:1024] = ref[160:176, 256:512]
+        piece = ref[160:176, 512:640].astype(jnp.float32)
+        for t in range(4):
+            lanes = pl.ds(pl.multiple_of(base + t * 128, 128), 128)
+            turned = pltpu.roll(piece, lax.rem((z - t + 4) * 32, 128), 1)
+            vec_ref[:, lanes] = jnp.where(group == z, turned, vec_ref[:, lanes])
     flush(0, 1, 2)
-    ready(0, 3)
+    ready(0, 1)
     gain, shift_row = vec_ref[0:1, :], vec_ref[1:2, :]
     for block in range(4):
         rows = slice(block * ROW, (block + 1) * ROW)
@@ -448,8 +456,7 @@
 def up_kernel(at, ins, outs, tmp, ready, flush):
     n0, n1, n2, n3, own_ref, far_ref, vec_ref, uplow_ref = ins
     team = at[1]
-    team_ref, weight_ref, hidden_ref, slope_ref, mine_ref, theirs_ref = outs
-    grad_ref, = tmp
+    team_ref, weight_ref, hidden_ref, slope_ref, grad_ref = outs
     ready(4, 5, 6, 0, 1, 2, 3)
     y_pos = at[0]
     for block, ref in enumerate((n0, n1, n2, n3)):
@@ -470,9 +477,10 @@
         slope_ref[rows, :] = act_slope
     flush(2, 3)
     ready(7)
-    grad_ref[...] = matmul_tn(hidden_ref[...], uplow_ref[...])
-    mine_ref[...] = grad_ref[pl.ds(pl.multiple_of(y_pos * 512, 512), 512), :]
-    theirs_ref[...] = grad_ref[pl.ds(pl.multiple_of((1 - y_pos) * 512, 512), 512), :].astype(LOW)
+    for side in range(2):
+        grad = matmul_tn(hidden_ref[:, side * 512 : (side + 1) * 512], uplow_ref[...]).astype(LOW)
+        for z in range(4):
+            grad_ref[z, side] = grad[z * 128 : (z + 1) * 128, :]
 
 
 def down_kernel(at, ins, outs, tmp, ready, flush):
@@ -546,15 +554,21 @@
 
 
 def backward_kernel(at, ins, outs, tmp, ready, flush):
-    out_ref, qkv_ref, seg_ref, normed_ref = ins[4:]
-    mine_ref, theirs_ref, mixed_ref, bias_ref = outs
-    grad_ref, att_ref = tmp
+    out_ref, qkv_ref, seg_ref, normed_ref, x_ref, weight_ref, rows_ref, pre_ref = ins[4:]
+    keep_ref, send_ref = outs[8:]
+    mixed_ref, grad_ref, att_ref, vec_ref = tmp
+    team = at[1]
     ready(4)
     for block in range(4):
         ready(block)
         att_ref[block * ROW : (block + 1) * ROW, :] = matmul_nt(ins[block][...], out_ref[...]).astype(LOW)
-    ready(5, 6)
-    bias_ref[...] = jnp.zeros_like(bias_ref)
+    ready(5, 6, 10, 11)
+    vec_ref[...] = jnp.zeros_like(vec_ref)
+    vec_ref[4:7, :] = rows_ref[0:3, :]
+    vec_ref[11:12, :] = rows_ref[3:4, :]
+    for side in range(2):
+        at_row = pl.ds(7 + 2 * side + team // 2, 1)
+        vec_ref[at_row, pl.ds(pl.multiple_of((team % 2) * 512, 512), 512)] = pre_ref[0:1, side * 512 : (side + 1) * 512]
     first = head_lanes()
     for pair in range(2):
         query_sum = jnp.zeros((1, 128), jnp.float32)
@@ -586,32 +600,14 @@
                     query_sum = query_sum + jnp.sum(merged, axis=0, keepdims=True)
                 if which == 2:
                     value_sum = value_sum + jnp.sum(merged, axis=0, keepdims=True)
-        bias_ref[0:1, pair * 128 : (pair + 1) * 128] = query_sum
-        bias_ref[1:2, pair * 128 : (pair + 1) * 128] = value_sum
-    flush(2, 3)
+        lanes = pl.ds(pl.multiple_of(pair * 512 + team * 128, 128), 128)
+        vec_ref[2:3, lanes] = query_sum
+        vec_ref[3:4, lanes] = value_sum
     ready()
+    send_ref[...] = matmul_nt(mixed_ref[256:512, :], weight_ref[...])
+    keep_ref[...] = matmul_nt(mixed_ref[0:256, :], weight_ref[...])
+    flush(8, 9)
     grad_ref[...] = matmul_tn(normed_ref[...], mixed_ref[...])
-    spread(at, grad_ref, mine_ref, theirs_ref)
-
-
-def vector_kernel(at, ins, outs, tmp, ready, flush):
-    mixed_ref, weight_ref, x_ref, rows_ref, pre_ref, bias_ref = ins
-    mine_ref, theirs_ref, keep_ref, send_ref = outs
-    vec_ref, = tmp
-    y_pos, team = at[0], at[1]
-    ready()
-    vec_ref[...] = jnp.zeros_like(vec_ref)
-    vec_ref[4:7, :] = rows_ref[0:3, :]
-    vec_ref[11:12, :] = rows_ref[3:4, :]
-    for side in range(2):
-        at_row = pl.ds(7 + 2 * side + team // 2, 1)
-        vec_ref[at_row, pl.ds(pl.multiple_of((team % 2) * 512, 512), 512)] = pre_ref[0:1, side * 512 : (side + 1) * 512]
-        lanes = pl.ds(pl.multiple_of(side * 512 + team * 128, 128), 128)
-        vec_ref[2:4, lanes] = bias_ref[0:2, side * 128 : (side + 1) * 128]
-    send_ref[...] = matmul_nt(mixed_ref[256:512, :], weight_ref[...])
-    flush(3)
-    keep_ref[...] = matmul_nt(mixed_ref[0:256, :], weight_ref[...])
-    flush(2)
     gain_sum = jnp.zeros((1, D), jnp.float32)
     shift_sum = jnp.zeros((1, D), jnp.float32)
     for block in range(4):
@@ -624,27 +620,20 @@
     vec_ref[0:1, :] = gain_sum
     vec_ref[1:2, :] = shift_sum
     group = lane_group(16)
-    for ref, side, kind in ((mine_ref, y_pos, jnp.float32), (theirs_ref, 1 - y_pos, LOW)):
-        for z in range(4):
+    for hop in (2, 1, 3, 0):
+        z = lax.rem(at[2] + hop, 4)
+        for index, side in ((4 + hop, 1 - at[0]), (hop, at[0])):
+            for t in range(4):
+                start = pl.multiple_of(side * 512 + t * 128 + z * 32, 32)
+                outs[index][t * 32 : (t + 1) * 32, :] = grad_ref[pl.ds(start, 32), :].astype(outs[index].dtype)
             tile = jnp.zeros((16, 128), jnp.float32)
             for t in range(4):
                 piece = vec_ref[:, pl.ds(pl.multiple_of(side * 512 + t * 128, 128), 128)]
-                shift = (t - z) * 32 % 128
-                piece = pltpu.roll(piece, shift, 1) if shift else piece
-                tile = jnp.where(group == t, piece, tile)
-            ref[z] = tile.astype(kind)
-
-
-def fold_kernel(at, ins, outs, tmp, ready, flush):
-    mine_ref, recv_ref, vec_mine, vec_recv = ins
-    ready()
-    for hop in (1, 2, 3, 0):
-        dest = lax.rem(at[2] + hop, 4)
-        ref = outs[hop]
-        ref[0:128, :] = (mine_ref[dest] + recv_ref[dest].astype(jnp.float32)).astype(ref.dtype)
-        ref[128:144, 0:128] = (vec_mine[dest] + vec_recv[dest].astype(jnp.float32)).astype(ref.dtype)
-        ref[128:144, 128:768] = jnp.zeros((16, 640), ref.dtype)
-        flush(hop)
+                turned = pltpu.roll(piece, lax.rem((t - z + 4) * 32, 128), 1)
+                tile = jnp.where(group == t, turned, tile)
+            outs[index][128:144, 0:128] = tile.astype(outs[index].dtype)
+            outs[index][128:144, 128:768] = jnp.zeros((16, 640), outs[index].dtype)
+            flush(index)
 
 
 def step_rows(params_ref, first_ref, second_ref, grad_ref, new_refs, start, count, chunk, decay):
@@ -666,29 +655,25 @@
         copy.wait()
 
 
-def early_kernel(at, p_hbm, m_hbm, v_hbm, up_hbm, down_hbm, *refs):
+def early_kernel(at, p_hbm, m_hbm, v_hbm, down_hbm, *refs):
     hbm_outs = refs[:4]
-    p_ref, m_ref, v_ref, up_ref, down_ref, g_ref, np_ref, nm_ref, nv_ref, sems = refs[4:]
-    part = lambda ref: ref.at[pl.ds(1024, 2048), :]
-    pairs = [(up_hbm, up_ref), (down_hbm, down_ref)]
+    p_ref, m_ref, v_ref, down_ref, g_ref, np_ref, nm_ref, nv_ref, sems = refs[4:]
+    part = lambda ref: ref.at[pl.ds(2048, 1024), :]
+    pairs = [(down_hbm, down_ref)]
     pairs.extend((part(hbm), ref) for hbm, ref in ((p_hbm, p_ref), (m_hbm, m_ref), (v_hbm, v_ref)))
     run_copies(pairs, sems, 0)
     for j in range(8):
-        cols = slice(j * 128, (j + 1) * 128)
-        g_ref[pl.ds(1024 + j, 128, stride=8), :] = down_ref[:, cols].astype(jnp.float32)
-        for t in range(4):
-            flat = (j // 4) * 16 + t * 4 + j % 4
-            g_ref[pl.ds(flat, 32, stride=32), :] = up_ref[t, :, cols].astype(jnp.float32)
-    step_rows(p_ref, m_ref, v_ref, g_ref, (np_ref, nm_ref, nv_ref), 0, 2048, 128, decay_rate)
-    run_copies([(src, part(dst)) for src, dst in zip((g_ref, np_ref, nm_ref, nv_ref), hbm_outs)], sems, 5)
+        g_ref[pl.ds(j, 128, stride=8), :] = down_ref[:, j * 128 : (j + 1) * 128].astype(jnp.float32)
+    step_rows(p_ref, m_ref, v_ref, g_ref, (np_ref, nm_ref, nv_ref), 0, 1024, 128, decay_rate)
+    run_copies([(src, part(dst)) for src, dst in zip((g_ref, np_ref, nm_ref, nv_ref), hbm_outs)], sems, 4)
 
 
 def late_kernel(at, p_hbm, m_hbm, v_hbm, qkv_hbm, out_hbm, *refs):
     hbm_outs = refs[4:8]
     p_ref, m_ref, v_ref, qkv_ref, out_ref, g_ref, np_ref, nm_ref, nv_ref, sems = refs[8:]
     spans = lambda ref, hbm: (
-        (hbm.at[pl.ds(0, 1024), :], ref.at[pl.ds(0, 1024), :]),
-        (hbm.at[pl.ds(3072, 3), :], ref.at[pl.ds(1024, 3), :]),
+        (hbm.at[pl.ds(0, 2048), :], ref.at[pl.ds(0, 2048), :]),
+        (hbm.at[pl.ds(3072, 3), :], ref.at[pl.ds(2048, 3), :]),
     )
     pairs = [(qkv_hbm, qkv_ref), (out_hbm, out_ref)]
     for hbm, ref in ((p_hbm, p_ref), (m_hbm, m_ref), (v_hbm, v_ref)):
@@ -699,6 +684,17 @@
             g_ref[pl.ds(g * 4 + t, 32, stride=24), :] = qkv_ref[t, 0:32, g * 128 : (g + 1) * 128].astype(jnp.float32)
     for j in range(8):
         g_ref[pl.ds(768 + j, 32, stride=8), :] = out_ref[:, j * 128 : (j + 1) * 128].astype(jnp.float32)
+    for t in range(4):
+        for part in range(8):
+            flat = 1024 + (part // 4) * 16 + t * 4 + part % 4
+            if part < 6:
+                value = qkv_ref[t, 48:80, part * 128 : (part + 1) * 128]
+                g_ref[pl.ds(flat, 32, stride=32), :] = value.astype(jnp.float32)
+            else:
+                for half in range(2):
+                    lane = half * 256 + (part - 6) * 128
+                    value = qkv_ref[t, 80:96, lane : lane + 128]
+                    g_ref[pl.ds(flat + half * 512, 16, stride=32), :] = value.astype(jnp.float32)
     total = jnp.zeros((16, 128), jnp.float32)
     for t in range(4):
         total = total + qkv_ref[t, 32:48, 0:128].astype(jnp.float32)
@@ -708,10 +704,10 @@
         row = jnp.zeros((1, 128), jnp.float32)
         for q in range(4):
             row = jnp.where(group == q, turned[q][4 * r + q : 4 * r + q + 1, :], row)
-        g_ref[1024 + r : 1025 + r, :] = row
+        g_ref[2048 + r : 2049 + r, :] = row
     new_refs = (np_ref, nm_ref, nv_ref)
-    step_rows(p_ref, m_ref, v_ref, g_ref, new_refs, 0, 1024, 128, decay_rate)
-    tail = slice(1024, 1027)
+    step_rows(p_ref, m_ref, v_ref, g_ref, new_refs, 0, 2048, 128, decay_rate)
+    tail = slice(2048, 2051)
     outs = adam(p_ref[tail, :], m_ref[tail, :], v_ref[tail, :], g_ref[tail, :], 0.0)
     for ref, value in zip(new_refs, outs):
         ref[tail, :] = value
@@ -738,10 +734,10 @@
 
 
 def join_kernel(at, ins, outs, tmp, ready, flush):
-    own_ref, r1, r2, r3 = ins
+    mine_ref, recv_ref, r1, r2, r3, up_ref = ins
     pay_ref, = outs
     ready()
-    total = own_ref[...]
+    total = mine_ref[...] + recv_ref[...].astype(jnp.float32)
     for ref in (r1, r2, r3):
         total = total + ref[...].astype(jnp.float32)
     for t in range(4):
@@ -749,6 +745,10 @@
         tile = total[128:144, 0:128]
         pay_ref[t, 32:48, 0:128] = (pltpu.roll(tile, 128 - t * 32, 1) if t else tile).astype(LOW)
         pay_ref[t, 32:48, 128:768] = jnp.zeros((16, 640), LOW)
+        pay_ref[t, 48:80, :] = up_ref[t * 32 : (t + 1) * 32, 0:768]
+        pay_ref[t, 80:96, 0:256] = up_ref[t * 32 : t * 32 + 16, 768:1024]
+        pay_ref[t, 80:96, 256:512] = up_ref[t * 32 + 16 : t * 32 + 32, 768:1024]
+        pay_ref[t, 80:96, 512:768] = jnp.zeros((16, 256), LOW)
 
 
 def team_body(*arrays):
@@ -774,13 +774,14 @@
         [out_part[:16, 768:], out_part[16:, 768:], vec_team, jnp.zeros((16, 128), LOW)], axis=1
     )
     qkv_shard = jnp.concatenate([qkv_team[:, :share].reshape(4 * share, 768), out_part[:, :768], rest])
-    qkv_own = z_gather(qkv_shard).reshape(4, 176, 768)
-    qkv_far = swap(qkv_own, "y")
     up_send = up_part.reshape(share, 2, 4, 512).transpose(2, 0, 1, 3).reshape(4, share, 1024)
-    up_team = team_exchange(after(up_send, qkv_shard))
-    up_own = z_gather(up_team.reshape(4 * share, 1024)).reshape(4, 4 * share, 1024)
+    qkv_near = [qkv_shard] + [hop_to(qkv_shard, hop) for hop in (1, 2, 3)]
+    qkv_far = [swap(qkv_shard, "y")]
+    qkv_far = qkv_far + [swap(piece, "y") for piece in qkv_near[1:]]
+    up_team = team_exchange(after(up_send, qkv_shard)).reshape(4 * share, 1024)
+    up_own = z_gather(after(up_team, qkv_near[1:])).reshape(4, 4 * share, 1024)
     up_far = swap(up_own, "y")
-    down_own = z_gather(after(down_part, up_team))
+    down_own = z_gather(after(down_part, (up_team, qkv_near[1:])))
 
     steps = jnp.arange(2, dtype=jnp.int32)
     team_devices = (
@@ -790,7 +791,7 @@
 
     upstream = cotangent * live_mask[0][:, None].astype(jnp.float32)
     token_pack = after(jnp.stack([x_in, upstream.astype(LOW)]), up_team)
-    tokens = jnp.stack(team_gather(token_pack))
+    tokens = jnp.stack(team_gather(token_pack, qkv_near[1:]))
     x_team = tokens[:, 0].reshape(TOK, D)
     up_low = tokens[:, 1].reshape(TOK, D)
 
@@ -801,7 +802,7 @@
             sds((TOK, 768), LOW), sds((TOK, 256), LOW), sds((256, D)), sds((256, D)),
         ),
         at,
-        (x_team, qkv_own, qkv_far, seg_ids),
+        (x_team, seg_ids, *qkv_near, *qkv_far),
     )
     keep, recv, near = team_reduce(keep, send)
     residual, normed2 = call(
@@ -809,17 +810,16 @@
     )
     norm_blocks = team_gather(normed2)
     down_far = swap(after(down_own, normed2), "y")
-    normed2, up_weight, hidden, slope, down_mine, down_theirs = call(
+    normed2, up_weight, hidden, slope, down_grad = call(
         up_kernel,
         (
             sds((TOK, D), LOW), sds((D, 1024), LOW), sds((TOK, 1024), LOW), sds((TOK, 1024)),
-            sds((512, D)), sds((512, D), LOW),
+            sds((4, 2, 128, D), LOW),
         ),
         at,
         (*norm_blocks, up_own, up_far, vectors, up_low),
-        [pltpu.VMEM((1024, D), jnp.float32)],
-    )
-    down_recv = swap(down_theirs, "y")
+    )
+    down_sides = z_reduce(down_grad.reshape(1024, D)).reshape(2, 128, D)
     pre_low, pre_sum, keep, send = call(
         down_kernel,
         (sds((TOK, 1024), LOW), sds((8, 1024)), sds((256, D)), sds((256, D))),
@@ -827,69 +827,65 @@
         (up_low, down_own, down_far, slope, up_weight),
     )
     keep, recv, near = team_reduce(keep, send)
-    y_sum = lambda mine, recv: (mine + recv.astype(jnp.float32)).astype(LOW)
-    down_pay = y_sum(after(down_mine, pre_sum), down_recv)
-    down_sum = z_reduce(down_pay)
+    up_mine, up_theirs = call(
+        up_grad_kernel,
+        (sds((4, 4 * share, 1024)), sds((4, 4 * share, 1024), LOW)),
+        at,
+        (normed2, pre_low),
+        [pltpu.VMEM((D, 1024), jnp.float32)],
+    )
+    up_recv = swap(up_theirs, "y")
     grad_residual, res_low, row_sums = call(
         residual_back_kernel,
         (sds((rows, D)), sds((rows, D), LOW), sds((8, D))),
         at,
-        (residual, keep, recv, after(near, down_pay), upstream, vectors),
-    )
-    up_mine, up_theirs = call(
-        up_grad_kernel,
-        (sds((4, 4 * share, 1024)), sds((4, 4 * share, 1024), LOW)),
-        at,
-        (normed2, after(pre_low, res_low)),
-        [pltpu.VMEM((D, 1024), jnp.float32)],
-    )
-    up_recv = swap(up_theirs, "y")
-    res_blocks = team_gather(res_low, up_theirs)
+        (residual, keep, recv, after(near, up_theirs), upstream, vectors),
+    )
+    y_sum = lambda mine, recv: (mine + recv.astype(jnp.float32)).astype(LOW)
+    res_blocks = team_gather(res_low)
     out_mine, out_theirs = call(out_grad_kernel, (sds((128, D)), sds((128, D), LOW)), at, (*res_blocks, attended))
     out_recv = swap(out_theirs, "y")
-    qkv_mine, qkv_theirs, mixed_low, bias_sums = call(
+    out_keep, out_send = call(
+        split_kernel, (sds((256, D)), sds((256, D))), at,
+        (after(hidden, out_theirs), down_own, down_far),
+    )
+    up_pay = y_sum(after(up_mine, out_send), up_recv).reshape(TOK, D)
+    up_sum = z_reduce(up_pay)
+    down_recv = swap(lax.dynamic_index_in_dim(down_sides, 1 - y_pos, 0, keepdims=False), "y")
+    *qkv_parts, keep, send = call(
         backward_kernel,
-        (sds((4, 128, 768)), sds((4, 128, 768), LOW), sds((TOK, 768), LOW), sds((8, 256))),
+        (sds((144, 768)),) * 4 + (sds((144, 768), LOW),) * 4 + (sds((256, D)), sds((256, D))),
         at,
-        (*res_blocks, out_weight, qkv_low, seg_ids, normed1),
-        [pltpu.VMEM((D, 768), jnp.float32), pltpu.VMEM((TOK, 256), LOW)],
-    )
-    qkv_recv = swap(qkv_theirs, "y")
-    vec_mine, vec_theirs, keep, send = call(
-        vector_kernel,
-        (sds((4, 16, 128)), sds((4, 16, 128), LOW), sds((256, D)), sds((256, D))),
-        at,
-        (mixed_low, qkv_weight, x_team, row_sums, pre_sum, bias_sums),
-        [pltpu.VMEM((16, D), jnp.float32)],
-    )
-    vec_recv = swap(vec_theirs, "y")
-    up_pay = y_sum(after(up_mine, qkv_theirs), up_recv).reshape(TOK, D)
-    up_sum = z_reduce(up_pay)
-    out_sum = z_reduce(y_sum(after(out_mine, qkv_theirs), out_recv))
-    own, *pieces = call(
-        fold_kernel, (sds((144, 768)),) + (sds((144, 768), LOW),) * 3, at, (qkv_mine, qkv_recv, vec_mine, vec_recv)
-    )
-    up_back = team_exchange(after(up_sum, own).reshape(4, share, 1024))
-    turned = [
-        lax.ppermute(piece, "z", [(i, (i + hop) % 4) for i in range(4)])
-        for hop, piece in zip((1, 2, 3), pieces)
-    ]
+        (*res_blocks, out_weight, qkv_low, seg_ids, normed1, x_team, qkv_weight, row_sums, pre_sum),
+        [
+            pltpu.VMEM((TOK, 768), LOW), pltpu.VMEM((D, 768), jnp.float32),
+            pltpu.VMEM((TOK, 256), LOW), pltpu.VMEM((16, D), jnp.float32),
+        ],
+    )
+    first_recv = swap(qkv_parts[4 + 2], "y")
+    rest_recv = [swap(qkv_parts[4 + hop], "y") for hop in (1, 3, 0)]
+    qkv_recv = (rest_recv[2], rest_recv[0], first_recv, rest_recv[1])
+    down_mine = lax.dynamic_index_in_dim(down_sides, y_pos, 0, keepdims=False)
+    down_sum = down_mine.astype(jnp.float32) + after(down_recv, qkv_parts[4]).astype(jnp.float32)
+    out_sum = z_reduce(y_sum(after(out_mine, qkv_parts[4]), out_recv))
+    joined = {hop: (qkv_parts[hop] + qkv_recv[hop].astype(jnp.float32)).astype(LOW) for hop in (1, 2, 3)}
+    turned = [hop_to(joined[2], 2)]
+    turned.append(hop_to(joined[1], 1))
+    turned.append(hop_to(joined[3], 3))
 
     final_keep, final_send = keep, send
-    keep, send = call(
-        split_kernel, (sds((256, D)), sds((256, D))), at,
-        (after(hidden, vec_theirs), down_own, down_far),
-    )
-    output = residual + team_total(*team_reduce(keep, send)) + vectors[7 + FF // D]
+    output = residual + team_total(*team_reduce(out_keep, out_send)) + vectors[7 + FF // D]
     grad_normed1 = team_total(*team_reduce(final_keep, final_send))
     _, scaled1, inverse1 = normalize(x_in.astype(jnp.float32), vectors[0], vectors[1])
     grad_input = grad_residual + normalize_back(grad_normed1, scaled1, inverse1, vectors[0])
 
     state = tuple(v.reshape(-1, 128) for v in (params, first_moment, second_moment))
-    early = adam_call(early_kernel, at, (*state, up_back, down_sum), (), 2048, 9)
-    (qkv_pay,) = call(join_kernel, (sds((4, 48, 768), LOW),), at, (after(own, early[0]), *turned))
+    early = adam_call(early_kernel, at, (*state, down_sum), (), 1024, 8)
+    (qkv_pay,) = call(
+        join_kernel, (sds((4, 96, 768), LOW),), at, (qkv_parts[0], after(qkv_recv[0], early[0]), *turned, up_sum)
+    )
     qkv_back = team_exchange(qkv_pay)
-    final = adam_call(late_kernel, at, (*state, qkv_back, out_sum), early, 1032, 16)
+    final = adam_call(late_kernel, at, (*state, qkv_back, out_sum), early, 2056, 16)
     owned, new_params, new_first, new_second = (v.reshape(-1) for v in final)
     return (output, grad_input, owned, new_params, new_first, new_second)
 

time: 316 us -> 315 us (level)
  Pallas kernels: 84.1 us -> 77.1 us
  starting transfers between devices: 38.1 us -> 45.1 us
  waiting for transfers between devices: 143 us -> 138 us
  other arithmetic: 21.5 us -> 25.5 us
    ppermute x3 -> x6, waiting for transfers between devices: 0.01 us -> 21.8 us  [hop_to(): return lax.ppermute(piece, 'z', [(i, (i + hop) % 4) for i in range(4)])]
    all_gather x3 -> x2, waiting for transfers between devices: 20.4 us -> 0.04 us  [z_gather(): return lax.all_gather(shard, 'z', axis=0, tiled=True)]
    reduce_scatter x3, waiting for transfers between devices: 10.9 us -> 0.04 us  [z_reduce(): return lax.psum_scatter(values, 'z', scatter_dimension=0, tiled=True)]
    pallas_call x12 -> x10, Pallas kernels: 73.3 us -> 66.4 us  [call(): pl.pallas_call(staged, out_shape=outs, in_specs=[pl.BlockSpec(memory_spac...]
    ppermute x3 -> x6, starting transfers between devices: 5.18 us -> 12 us  [hop_to(): return lax.ppermute(piece, 'z', [(i, (i + hop) % 4) for i in range(4)])]
    ppermute x25 -> x30, waiting for transfers between devices: 96.3 us -> 102 us  [swap(): return lax.ppermute(values, axis, SWAP)]
    convert_element_type x0 -> x3, other arithmetic: none -> 4.32 us  [team_step(): (qkv_parts[hop] + qkv_recv[hop].astype(jnp.float32)).astype(LOW)]
    ppermute x25 -> x30, starting transfers between devices: 18 us -> 21.5 us  [swap(): return lax.ppermute(values, axis, SWAP)]
  transfers between devices with their start and end apart: 38 -> 44, of which waited for: 20 -> 21; matrix products, arithmetic and copies ran while one was open for 7% -> 9% of each run, Pallas kernels for 20% -> 22%
where the time goes in v3:
time: 315 us; the launch traced here: 314 us
  waiting for transfers between devices  138 us (44%)
  Pallas kernels  77.1 us (24%)
  starting transfers between devices  45.1 us (14%)
  other arithmetic  25.5 us (8%)
  between operations  14.4 us (5%)
  local copies, waits for them, and re-layouts  13.5 us (4%)
    ppermute x30, waiting for transfers between devices, swap(): return lax.ppermute(values, axis, SWAP)  102 us
    pallas_call x10, Pallas kernels, call(): pl.pallas_call(staged, out_shape=outs, in_specs=[pl.BlockSpec(memory_spac...  66.4 us
    ppermute x6, waiting for transfers between devices, hop_to(): return lax.ppermute(piece, 'z', [(i, (i + hop) % 4) for i in range(4)])  21.8 us
    ppermute x30, starting transfers between devices, swap(): return lax.ppermute(values, axis, SWAP)  21.5 us
    all_to_all x3, waiting for transfers between devices, team_exchange(): return lax.all_to_all(values, TEAM, 0, 0, tiled=True)  14.6 us
    ppermute x6, starting transfers between devices, hop_to(): return lax.ppermute(piece, 'z', [(i, (i + hop) % 4) for i in range(4)])  12 us
    all_to_all x3, starting transfers between devices, team_exchange(): return lax.all_to_all(values, TEAM, 0, 0, tiled=True)  11.1 us
    pallas_call x2, Pallas kernels, adam_call(): pl.pallas_call(kernel, out_shape=tuple((sds(arrays[0].shape) for _ in ran...  10.7 us
  transfers between devices with their start and end apart: 44, of which 21 were waited for; matrix products, arithmetic and copies ran while one was open for 9% of the time, Pallas kernels for 22%

profile of v3, /device:TPU:0, one launch (start us, length us, event | category | flops | bytes accessed | tf_op | source)
XLA Modules:
  0.0 314.1 jit_solution(10822501540051543760)
XLA Ops:
  7.2 1.5 convert_element_type.85
  9.9 4.2 %all-to-all-start = ((bf16[4,48,768]{2,1,0:T(8,128)(2,1)}), bf16[4,48,768]{2,1,0:T(8,128)(2,1)S(1)}, u32[]{:S(2)}, u32[]{:S(2)}) async-start(bf16[4,48,768]{2,1,0:T(8,128)(2,1)} %pad_maximum_fusion.2), calls=%async_computation | async-start | bytes 589824 | tf_op jit(solution)/shard_map/all_to_all | solution.py:271
  16.3 4.2 %all-to-all-done = bf16[4,48,768]{2,1,0:T(8,128)(2,1)S(1)} async-done(((bf16[4,48,768]{2,1,0:T(8,128)(2,1)}), bf16[4,48,768]{2,1,0:T(8,128)(2,1)S(1)}, u32[]{:S(2)}, u32[]{:S(2)}) %all-to-all-start) | async-done | bytes 294944 | tf_op jit(solution)/shard_map/all_to_all | solution.py:271
  20.6 3.4 %all-to-all-start.1 = ((bf16[4,32,1024]{2,1,0:T(8,128)(2,1)}), bf16[4,32,1024]{2,1,0:T(8,128)(2,1)S(1)}, u32[]{:S(2)}, u32[]{:S(2)}) async-start(bf16[4,32,1024]{2,1,0:T(8,128)(2,1)} %reshape.165), calls=%async_computation.1 | async-start | bytes 524288 | tf_op jit(solution)/shard_map/all_to_all | solution.py:271
  25.1 4.9 %all-to-all-done.1 = bf16[4,32,1024]{2,1,0:T(8,128)(2,1)S(1)} async-done(((bf16[4,32,1024]{2,1,0:T(8,128)(2,1)}), bf16[4,32,1024]{2,1,0:T(8,128)(2,1)S(1)}, u32[]{:S(2)}, u32[]{:S(2)}) %all-to-all-start.1) | async-done | bytes 262176 | tf_op jit(solution)/shard_map/all_to_all | solution.py:271
  30.4 4.3 %collective-permute-start.4 = (bf16[176,768]{1,0:T(8,128)(2,1)S(1)}, bf16[176,768]{1,0:T(8,128)(2,1)S(1)}, u32[]{:S(2)}, u32[]{:S(2)}) collective-permute-start(bf16[176,768]{1,0:T(8,128)(2,1)S(1)} %maximum_maximum_fusion.refs_2_), channel_id=1, source_target_pairs={{0,3},{1,0},{2,1},{3,2},{4,7},{5,4},{6,5},{7,6},{8,11},{9,8},{10,9... | collective-permute-start | bytes 811016 | tf_op jit(solution)/shard_map/ppermute | solution.py:255
  34.7 1.0 collective-permute-start.2
  35.7 5.9 %collective-permute-done.4.refs_5_ = bf16[176,768]{1,0:T(8,128)(2,1)S(1)} collective-permute-done((bf16[176,768]{1,0:T(8,128)(2,1)S(1)}, bf16[176,768]{1,0:T(8,128)(2,1)S(1)}, u32[]{:S(2)}, u32[]{:S(2)}) %collective-permute-start.4) | collective-permute-done | bytes 270368 | tf_op jit(solution)/shard_map/ppermute | solution.py:255
  41.6 15.9 %collective-permute-done.3.refs_4_ = bf16[176,768]{1,0:T(8,128)(2,1)S(1)} collective-permute-done((bf16[176,768]{1,0:T(8,128)(2,1)S(1)}, bf16[176,768]{1,0:T(8,128)(2,1)S(1)}, u32[]{:S(2)}, u32[]{:S(2)}) %collective-permute-start.3) | collective-permute-done | bytes 270368 | tf_op jit(solution)/shard_map/ppermute | solution.py:255
  60.0 1.5 collective-permute-start.6
  62.1 1.5 collective-permute-start.8
  64.4 1.5 fusion.22
  65.9 3.5 %collective-permute-done.6.refs_6_ = bf16[176,768]{1,0:T(8,128)(2,1)S(1)} collective-permute-done((bf16[176,768]{1,0:T(8,128)(2,1)S(1)}, bf16[176,768]{1,0:T(8,128)(2,1)S(1)}, u32[]{:S(2)}, u32[]{:S(2)}) %collective-permute-start.6) | collective-permute-done | bytes 270368 | tf_op jit(solution)/shard_map/ppermute | solution.py:251
  69.4 5.8 %collective-permute-done.9.refs_9_ = bf16[176,768]{1,0:T(8,128)(2,1)S(1)} collective-permute-done((bf16[176,768]{1,0:T(8,128)(2,1)S(1)}, bf16[176,768]{1,0:T(8,128)(2,1)S(1)}, u32[]{:S(2)}, u32[]{:S(2)}) %collective-permute-start.9) | collective-permute-done | bytes 270368 | tf_op jit(solution)/shard_map/ppermute | solution.py:251
  75.2 5.8 %collective-permute-done.8.refs_8_ = bf16[176,768]{1,0:T(8,128)(2,1)S(1)} collective-permute-done((bf16[176,768]{1,0:T(8,128)(2,1)S(1)}, bf16[176,768]{1,0:T(8,128)(2,1)S(1)}, u32[]{:S(2)}, u32[]{:S(2)}) %collective-permute-start.8) | collective-permute-done | bytes 270368 | tf_op jit(solution)/shard_map/ppermute | solution.py:251
  81.7 4.2 %collective-permute-done.7.refs_7_ = bf16[176,768]{1,0:T(8,128)(2,1)S(1)} collective-permute-done((bf16[176,768]{1,0:T(8,128)(2,1)}, bf16[176,768]{1,0:T(8,128)(2,1)S(1)}, u32[]{:S(2)}, u32[]{:S(2)}) %collective-permute-start.7) | collective-permute-done | bytes 270368 | tf_op jit(solution)/shard_map/ppermute | solution.py:251
  86.6 10.5 %shard_map.118 = (f32[16,1024]{1,0:T(8,128)}, bf16[1024,768]{1,0:T(8,128)(2,1)}, bf16[256,1024]{1,0:T(8,128)(2,1)}, bf16[512,1024]{1,0:T(8,128)(2,1)}, bf16[512,...) custom-call(s32[3]{0:T(128)} %pad_add_fusion.at_ref.at, ...), custom_call_target="tpu_custom_call" | custom-call | tf_op jit(solution)/shard_map/pallas_call | solution.py:334
  98.1 1.6 collective-permute-start.15
  100.1 1.5 fusion.17
  101.5 1.3 collective-permute-start.11
  102.9 7.1 %collective-permute-done.11.refs_3_ = bf16[128,1024]{1,0:T(8,128)(2,1)S(1)} collective-permute-done((bf16[128,1024]{1,0:T(8,128)(2,1)S(1)}, bf16[128,1024]{1,0:T(8,128)(2,1)S(1)}, u32[]{:S(2)}, u32[]{:S(2)}) %collective-permute-start.11) | collective-permute-done | bytes 262176 | tf_op jit(solution)/shard_map/ppermute | solution.py:251
  110.7 3.4 %shard_map.119 = (f32[128,1024]{1,0:T(8,128)}, bf16[128,1024]{1,0:T(8,128)(2,1)}) custom-call(s32[3]{0:T(128)} %pad_add_fusion.at_ref.at, bf16[128,1024]{1,0:T(8,128)(2,1)} %refs_0_.1, f32[256,1024]{1,0:T(8,128)} %get-tuple-element.67.refs_1_, f32[256,1024]{1,0:T(8,128)} %copy-done.4, bf16[128,1024]{1,0:T(8,128)(2,1)} %copy-done.31, ...), custom_call_target="tpu_custom_call" | custom-call | tf_op jit(solution)/shard_map/pallas_call | solution.py:334
  114.1 1.3 collective-permute-start.12
  115.4 6.4 %collective-permute-done.12.refs_1_ = bf16[128,1024]{1,0:T(8,128)(2,1)S(1)} collective-permute-done((bf16[128,1024]{1,0:T(8,128)(2,1)}, bf16[128,1024]{1,0:T(8,128)(2,1)S(1)}, u32[]{:S(2)}, u32[]{:S(2)}) %collective-permute-start.12) | collective-permute-done | bytes 262176 | tf_op jit(solution)/shard_map/ppermute | solution.py:251
  121.9 2.1 collective-permute-done.15.refs_5_
  124.0 1.0 copy-done.10
  125.1 7.9 %shard_map.120 = (bf16[512,1024]{1,0:T(8,128)(2,1)}, bf16[1024,1024]{1,0:T(8,128)(2,1)}, bf16[512,1024]{1,0:T(8,128)(2,1)}, f32[512,1024]{1,0:T(8,128)}, bf16[4,2,128,1024]{3,2,1,0:T(8,128)(2,1)}) custom-call(s32[3]{0:T(128)} %pad_add_fusion.at_ref.at, bf16[128,1024]{1,0:T(8,128)(2,1)} %get-tuple-element.71.refs_0_, bf16[128,1024]{1,0:T(8,128)(2,1)} %copy-done.27, ...), custom_call_target="tpu_custom_call" | custom-call | tf_op jit(solution)/shard_map/pallas_call | solution.py:334
  133.2 1.6 collective-permute-start.16
  134.8 23.5 %collective-permute-done.16.refs_2_ = bf16[512,1024]{1,0:T(8,128)(2,1)S(1)} collective-permute-done((bf16[512,1024]{1,0:T(8,128)(2,1)}, bf16[512,1024]{1,0:T(8,128)(2,1)S(1)}, u32[]{:S(2)}, u32[]{:S(2)}) %collective-permute-start.16) | collective-permute-done | bytes 1048608 | tf_op jit(solution)/shard_map/ppermute | solution.py:251
  158.3 1.1 copy-done.2
  159.4 8.5 %shard_map.121 = (bf16[512,1024]{1,0:T(8,128)(2,1)}, f32[8,1024]{1,0:T(8,128)}, f32[256,1024]{1,0:T(8,128)}, f32[256,1024]{1,0:T(8,128)}) custom-call(s32[3]{0:T(128)} %pad_add_fusion.at_ref.at, bf16[512,1024]{1,0:T(8,128)(2,1)} %bitcast.46, bf16[512,1024]{1,0:T(8,128)(2,1)} %all-gather.5.cloned.1.call-done.refs_1_, bf16[512,1024]{1,0:T(8,128)(2,1)} %copy-done.2, ...), custom_call_target="tpu_custom_call" | custom-call | tf_op jit(solution)/shard_map/pallas_call | solution.py:334
  168.0 5.4 %shard_map.122 = (f32[4,128,1024]{2,1,0:T(8,128)}, bf16[4,128,1024]{2,1,0:T(8,128)(2,1)}) custom-call(s32[3]{0:T(128)} %pad_add_fusion.at_ref.at, bf16[512,1024]{1,0:T(8,128)(2,1)} %get-tuple-element.80.refs_0_, bf16[512,1024]{1,0:T(8,128)(2,1)} %get-tuple-element.81.refs_1_), custom_call_target="tpu_custom_call" | custom-call | tf_op jit(solution)/shard_map/pallas_call | solution.py:334
  173.4 1.6 collective-permute-start.34
  175.1 1.3 collective-permute-start.18
  176.4 7.0 %collective-permute-done.18.refs_3_ = bf16[128,1024]{1,0:T(8,128)(2,1)S(1)} collective-permute-done((bf16[128,1024]{1,0:T(8,128)(2,1)S(1)}, bf16[128,1024]{1,0:T(8,128)(2,1)S(1)}, u32[]{:S(2)}, u32[]{:S(2)}) %collective-permute-start.18) | collective-permute-done | bytes 262176 | tf_op jit(solution)/shard_map/ppermute | solution.py:251
  184.2 4.1 %shard_map.123 = (f32[128,1024]{1,0:T(8,128)}, bf16[128,1024]{1,0:T(8,128)(2,1)}, f32[8,1024]{1,0:T(8,128)}) custom-call(s32[3]{0:T(128)} %pad_add_fusion.at_ref.at, f32[128,1024]{1,0:T(8,128)} %get-tuple-element.70.refs_0_, f32[256,1024]{1,0:T(8,128)} %get-tuple-element.78.refs_1_, f32[256,1024]{1,0:T(8,128)} %copy-done.6, bf16[128,1024]{1,0:T(8,128)(2,1)} %copy-done.30, ...), custom_call_target="tpu_custom_call" | custom-call | tf_op jit(solution)/shard_map/pallas_call | solution.py:334
  188.3 1.3 collective-permute-start.19
  189.6 6.5 %collective-permute-done.19.refs_1_ = bf16[128,1024]{1,0:T(8,128)(2,1)S(1)} collective-permute-done((bf16[128,1024]{1,0:T(8,128)(2,1)}, bf16[128,1024]{1,0:T(8,128)(2,1)S(1)}, u32[]{:S(2)}, u32[]{:S(2)}) %collective-permute-start.19) | collective-permute-done | bytes 262176 | tf_op jit(solution)/shard_map/ppermute | solution.py:251
  196.2 1.5 collective-permute-done.21.refs_3_
  198.4 3.9 %shard_map.124 = (f32[128,1024]{1,0:T(8,128)}, bf16[128,1024]{1,0:T(8,128)(2,1)}) custom-call(s32[3]{0:T(128)} %pad_add_fusion.at_ref.at, bf16[128,1024]{1,0:T(8,128)(2,1)} %get-tuple-element.84.refs_0_, bf16[128,1024]{1,0:T(8,128)(2,1)} %copy-done.11, bf16[128,1024]{1,0:T(8,128)(2,1)} %copy-done.12, bf16[128,1024]{1,0:T(8,128)(2,1)} %copy-done.13, ...), custom_call_target="tpu_custom_call" | custom-call | tf_op jit(solution)/shard_map/pallas_call | solution.py:334
  202.3 4.8 %shard_map.125 = (f32[256,1024]{1,0:T(8,128)}, f32[256,1024]{1,0:T(8,128)}) custom-call(s32[3]{0:T(128)} %pad_add_fusion.at_ref.at, bf16[512,1024]{1,0:T(8,128)(2,1)} %get-tuple-element.87.refs_0_, bf16[512,1024]{1,0:T(8,128)(2,1)} %all-gather.5.cloned.1.call-done.refs_1_, bf16[512,1024]{1,0:T(8,128)(2,1)} %copy-done.2), custom_call_target="tpu_custom_call" | custom-call | tf_op jit(solution)/shard_map/pallas_call | solution.py:334
  207.1 2.6 add_convert_fusion
  210.4 14.5 %shard_map.126 = (f32[144,768]{1,0:T(8,128)}, f32[144,768]{1,0:T(8,128)}, f32[144,768]{1,0:T(8,128)}, f32[144,768]{1,0:T(8,128)}, bf16[144,768]{1,0:T(8,128)(2,1...) custom-call(s32[3]{0:T(128)} %pad_add_fusion.at_ref.at, ...), custom_call_target="tpu_custom_call" | custom-call | tf_op jit(solution)/shard_map/pallas_call | solution.py:334
  226.4 1.6 collective-permute-start.35
  228.5 5.1 %collective-permute-done.28 = bf16[144,768]{1,0:T(8,128)(2,1)S(1)} collective-permute-done((bf16[144,768]{1,0:T(8,128)(2,1)}, bf16[144,768]{1,0:T(8,128)(2,1)S(1)}, u32[]{:S(2)}, u32[]{:S(2)}) %collective-permute-start.28) | collective-permute-done | bytes 221216 | tf_op jit(solution)/shard_map/ppermute | solution.py:251
  234.1 1.7 add_convert_fusion.4
  235.9 12.3 %collective-permute-done.30 = bf16[144,768]{1,0:T(8,128)(2,1)S(1)} collective-permute-done((bf16[144,768]{1,0:T(8,128)(2,1)}, bf16[144,768]{1,0:T(8,128)(2,1)S(1)}, u32[]{:S(2)}, u32[]{:S(2)}) %collective-permute-start.30) | collective-permute-done | bytes 221216 | tf_op jit(solution)/shard_map/ppermute | solution.py:251
  248.7 1.8 add_convert_fusion.3
  250.5 4.7 %collective-permute-done.32 = bf16[144,768]{1,0:T(8,128)(2,1)S(1)} collective-permute-done((bf16[144,768]{1,0:T(8,128)(2,1)}, bf16[144,768]{1,0:T(8,128)(2,1)S(1)}, u32[]{:S(2)}, u32[]{:S(2)}) %collective-permute-start.32) | collective-permute-done | bytes 221216 | tf_op jit(solution)/shard_map/ppermute | solution.py:251
  255.2 2.8 collective-permute-start.29
  259.6 1.3 collective-permute-start.25
  260.9 1.8 add_convert_fusion.1
  262.7 3.9 %collective-permute-start.33 = (bf16[144,768]{1,0:T(8,128)(2,1)}, bf16[144,768]{1,0:T(8,128)(2,1)}, u32[]{:S(2)}, u32[]{:S(2)}) collective-permute-start(bf16[144,768]{1,0:T(8,128)(2,1)} %add_convert_fusion.2), channel_id=1, source_target_pairs={{0,3},{1,0},{2,1},{3,2},{4,7},{5,4},{6,5},{7,6},{8,11},{9,8},{10,9... | collective-permute-start | bytes 663560 | tf_op jit(solution)/shard_map/ppermute | solution.py:255
  266.6 1.8 fusion.12
  268.4 1.2 fusion.20
  271.1 6.0 %collective-permute-done.27 = bf16[128,1024]{1,0:T(8,128)(2,1)S(1)} collective-permute-done((bf16[128,1024]{1,0:T(8,128)(2,1)S(1)}, bf16[128,1024]{1,0:T(8,128)(2,1)S(1)}, u32[]{:S(2)}, u32[]{:S(2)}) %collective-permute-start.27) | collective-permute-done | bytes 262176 | tf_op jit(solution)/shard_map/ppermute | solution.py:251
  277.7 1.8 convert_add_fusion.down_hbm
  279.5 4.2 %shard_map.127 = (f32[3075,128]{1,0:T(8,128)}, f32[3075,128]{1,0:T(8,128)}, f32[3075,128]{1,0:T(8,128)}, f32[3075,128]{1,0:T(8,128)}) custom-call(s32[3]{0:T(128)} %pad_add_fusion.at_ref.at, f32[3075,128]{1,0:T(8,128)} %bitcast.40, f32[3075,128]{1,0:T(8,128)} %bitcast.47, f32[3075,128]{1,0:T(8,128)} %bitcast.49, f32[128,1024]{1,0:T(8,128)} %convert_add_fusion.down_hbm), custom_call_target="tpu_custom_call" | custom-call | tf_op jit(solution)/shard_map/pallas_call | solution.py:725
  283.8 3.3 %shard_map.128 = bf16[4,96,768]{2,1,0:T(8,128)(2,1)} custom-call(s32[3]{0:T(128)} %pad_add_fusion.at_ref.at, f32[144,768]{1,0:T(8,128)} %get-tuple-element.99.refs_0_, bf16[144,768]{1,0:T(8,128)(2,1)} %collective-permute-done.26.refs_1_, bf16[144,768]{1,0:T(8,128)(2,1)} %collective-permute-done.29.refs_2_, bf16[144,768]{1,0:T(8,128)(2,1)} %collective-permute-done.31.refs_3_, ...), custom_call_target="tpu_custom_call" | custom-call | tf_op jit(solution)/shard_map/pallas_call | solution.py:334
  287.2 3.5 %all-to-all-start.2 = ((bf16[4,96,768]{2,1,0:T(8,128)(2,1)}), bf16[4,96,768]{2,1,0:T(8,128)(2,1)S(1)}, u32[]{:S(2)}, u32[]{:S(2)}) async-start(bf16[4,96,768]{2,1,0:T(8,128)(2,1)} %shard_map.128), calls=%async_computation.4 | async-start | bytes 1179648 | tf_op jit(solution)/shard_map/all_to_all | solution.py:271
  290.6 2.1 fusion.7
  292.7 2.0 fusion.15
  294.7 5.4 %all-to-all-done.2.qkv_hbm = bf16[4,96,768]{2,1,0:T(8,128)(2,1)S(1)} async-done(((bf16[4,96,768]{2,1,0:T(8,128)(2,1)}), bf16[4,96,768]{2,1,0:T(8,128)(2,1)S(1)}, u32[]{:S(2)}, u32[]{:S(2)}) %all-to-all-start.2) | async-done | bytes 589856 | tf_op jit(solution)/shard_map/all_to_all | solution.py:271
  301.0 6.6 %shard_map.129 = (f32[3075,128]{1,0:T(8,128)}, f32[3075,128]{1,0:T(8,128)}, f32[3075,128]{1,0:T(8,128)}, f32[3075,128]{1,0:T(8,128)}) custom-call(s32[3]{0:T(128)} %pad_add_fusion.at_ref.at, f32[3075,128]{1,0:T(8,128)} %bitcast.41, f32[3075,128]{1,0:T(8,128)} %bitcast.48, ...), custom_call_target="tpu_custom_call", output_to_operand_aliasing={{0}: (6, {}), {1}: (7, {}), {2}: (8, {}), {3}: (9, {})} | custom-call | tf_op jit(solution)/shard_map/pallas_call | solution.py:725
  (168 shorter events, 22.2 us)
Async XLA Ops:
  8.7 5.8 %copy-start.32 = (s32[128]{0:T(128)S(1)}, s32[128]{0:T(128)}, u32[]{:S(2)}) copy-start(s32[128]{0:T(128)} %param.12) | copy-start | bytes 1540
  8.7 5.8 %copy-start.33 = (s32[128]{0:T(128)S(1)}, s32[128]{0:T(128)}, u32[]{:S(2)}) copy-start(s32[128]{0:T(128)} %param.13) | copy-start | bytes 1540
  9.9 10.6 %all-to-all-start = ((bf16[4,48,768]{2,1,0:T(8,128)(2,1)}), bf16[4,48,768]{2,1,0:T(8,128)(2,1)S(1)}, u32[]{:S(2)}, u32[]{:S(2)}) async-start(bf16[4,48,768]{2,1,0:T(8,128)(2,1)} %pad_maximum_fusion.2), calls=%async_computation | async-start | bytes 589824 | tf_op jit(solution)/shard_map/all_to_all | solution.py:271
  14.2 9.9 %copy-start.18 = (f32[128,1024]{1,0:T(8,128)S(1)}, f32[128,1024]{1,0:T(8,128)}, u32[]{:S(2)}) copy-start(f32[128,1024]{1,0:T(8,128)} %param.8) | copy-start | bytes 1572868
  15.1 10.0 %copy-start = (bf16[128,1024]{1,0:T(8,128)(2,1)S(1)}, bf16[128,1024]{1,0:T(8,128)(2,1)}, u32[]{:S(2)}) copy-start(bf16[128,1024]{1,0:T(8,128)(2,1)} %refs_0_.1) | copy-start | bytes 786436
  20.6 43.7 %copy-start.9 = (bf16[176,768]{1,0:T(8,128)(2,1)}, bf16[176,768]{1,0:T(8,128)(2,1)S(1)}, u32[]{:S(2)}) copy-start(bf16[176,768]{1,0:T(8,128)(2,1)S(1)} %maximum_maximum_fusion.refs_2_) | copy-start | bytes 811012
  20.6 9.4 %all-to-all-start.1 = ((bf16[4,32,1024]{2,1,0:T(8,128)(2,1)}), bf16[4,32,1024]{2,1,0:T(8,128)(2,1)S(1)}, u32[]{:S(2)}, u32[]{:S(2)}) async-start(bf16[4,32,1024]{2,1,0:T(8,128)(2,1)} %reshape.165), calls=%async_computation.1 | async-start | bytes 524288 | tf_op jit(solution)/shard_map/all_to_all | solution.py:271
  24.1 74.1 %all-gather.3.cloned.1.call-start = ((), (), s32[]{:S(2)}) async-start(), calls=%async_computation.6 | async-start | bytes 1310720 | tf_op jit(solution)/shard_map/all_gather | solution.py:263
  30.0 27.5 %copy-start.15 = (bf16[4,32,1024]{2,1,0:T(8,128)(2,1)}, bf16[4,32,1024]{2,1,0:T(8,128)(2,1)S(1)}, u32[]{:S(2)}) copy-start(bf16[4,32,1024]{2,1,0:T(8,128)(2,1)S(1)} %all-to-all-done.1) | copy-start | bytes 786436
  30.0 28.2 %collective-permute-start = (bf16[2,128,1024]{2,1,0:T(8,128)(2,1)S(1)}, bf16[2,128,1024]{2,1,0:T(8,128)(2,1)S(1)}, u32[]{:S(2)}, u32[]{:S(2)}) collective-permute-start(bf16[2,128,1024]{2,1,0:T(8,128)(2,1)S(1)} %pad_maximum_fusion.1), channel_id=1, source_target_pairs={{0,8},{8,0},{1,9},{9,1},{2,10},{10,2},{3,11},{11,3},{4,12},{12,4},... | collective-permute-start | bytes 1572872 | tf_op jit(solution)/shard_map/ppermute | solution.py:251
  30.4 11.2 %collective-permute-start.4 = (bf16[176,768]{1,0:T(8,128)(2,1)S(1)}, bf16[176,768]{1,0:T(8,128)(2,1)S(1)}, u32[]{:S(2)}, u32[]{:S(2)}) collective-permute-start(bf16[176,768]{1,0:T(8,128)(2,1)S(1)} %maximum_maximum_fusion.refs_2_), channel_id=1, source_target_pairs={{0,3},{1,0},{2,1},{3,2},{4,7},{5,4},{6,5},{7,6},{8,11},{9,8},{10,9... | collective-permute-start | bytes 811016 | tf_op jit(solution)/shard_map/ppermute | solution.py:255
  34.7 22.8 %collective-permute-start.3 = (bf16[176,768]{1,0:T(8,128)(2,1)S(1)}, bf16[176,768]{1,0:T(8,128)(2,1)S(1)}, u32[]{:S(2)}, u32[]{:S(2)}) collective-permute-start(bf16[176,768]{1,0:T(8,128)(2,1)S(1)} %maximum_maximum_fusion.refs_2_), channel_id=1, source_target_pairs={{0,2},{1,3},{2,0},{3,1},{4,6},{5,7},{6,4},{7,5},{8,10},{9,11},{10,... | collective-permute-start | bytes 811016 | tf_op jit(solution)/shard_map/ppermute | solution.py:255
  34.7 22.8 %collective-permute-start.2 = (bf16[176,768]{1,0:T(8,128)(2,1)S(1)}, bf16[176,768]{1,0:T(8,128)(2,1)S(1)}, u32[]{:S(2)}, u32[]{:S(2)}) collective-permute-start(bf16[176,768]{1,0:T(8,128)(2,1)S(1)} %maximum_maximum_fusion.refs_2_), channel_id=1, source_target_pairs={{0,1},{1,2},{2,3},{3,0},{4,5},{5,6},{6,7},{7,4},{8,9},{9,10},{10,1... | collective-permute-start | bytes 811016 | tf_op jit(solution)/shard_map/ppermute | solution.py:255
  41.6 22.8 %copy-start.20 = (bf16[176,768]{1,0:T(8,128)(2,1)}, bf16[176,768]{1,0:T(8,128)(2,1)S(1)}, u32[]{:S(2)}) copy-start(bf16[176,768]{1,0:T(8,128)(2,1)S(1)} %collective-permute-done.4.refs_5_) | copy-start | bytes 811012
  57.5 6.9 %copy-start.21 = (bf16[176,768]{1,0:T(8,128)(2,1)}, bf16[176,768]{1,0:T(8,128)(2,1)S(1)}, u32[]{:S(2)}) copy-start(bf16[176,768]{1,0:T(8,128)(2,1)S(1)} %collective-permute-done.3.refs_4_) | copy-start | bytes 811012
  58.2 75.0 %all-gather.5.cloned.1.call-start = ((), (), s32[]{:S(2)}) async-start(), calls=%async_computation.7 | async-start | bytes 1310720 | tf_op jit(solution)/shard_map/all_gather | solution.py:263
  58.2 5.3 %collective-permute-start.1 = (bf16[2,128,1024]{2,1,0:T(8,128)(2,1)S(1)}, bf16[2,128,1024]{2,1,0:T(8,128)(2,1)S(1)}, u32[]{:S(2)}, u32[]{:S(2)}) collective-permute-start(bf16[2,128,1024]{2,1,0:T(8,128)(2,1)S(1)} %pad_maximum_fusion.1), channel_id=1, source_target_pairs={{0,4},{4,0},{1,5},{5,1},{2,6},{6,2},{3,7},{7,3},{8,12},{12,8},{9,1... | collective-permute-start | bytes 1572872 | tf_op jit(solution)/shard_map/ppermute | solution.py:251
  58.2 5.8 %collective-permute-start.5 = (bf16[2,128,1024]{2,1,0:T(8,128)(2,1)S(1)}, bf16[2,128,1024]{2,1,0:T(8,128)(2,1)S(1)}, u32[]{:S(2)}, u32[]{:S(2)}) collective-permute-start(bf16[2,128,1024]{2,1,0:T(8,128)(2,1)S(1)} %collective-permute-done), channel_id=1, source_target_pairs={{0,4},{4,0},{1,5},{5,1},{2,6},{6,2},{3,7},{7,3},{8,12},{12,8},{9,1... | collective-permute-start | bytes 1572872 | tf_op jit(solution)/shard_map/ppermute | solution.py:251
  60.0 9.4 %collective-permute-start.6 = (bf16[176,768]{1,0:T(8,128)(2,1)S(1)}, bf16[176,768]{1,0:T(8,128)(2,1)S(1)}, u32[]{:S(2)}, u32[]{:S(2)}) collective-permute-start(bf16[176,768]{1,0:T(8,128)(2,1)S(1)} %maximum_maximum_fusion.refs_2_), channel_id=1, source_target_pairs={{0,16},{16,0},{1,17},{17,1},{2,18},{18,2},{3,19},{19,3},{4,20},{20... | collective-permute-start | bytes 811016 | tf_op jit(solution)/shard_map/ppermute | solution.py:251
  61.5 13.6 %collective-permute-start.9 = (bf16[176,768]{1,0:T(8,128)(2,1)S(1)}, bf16[176,768]{1,0:T(8,128)(2,1)S(1)}, u32[]{:S(2)}, u32[]{:S(2)}) collective-permute-start(bf16[176,768]{1,0:T(8,128)(2,1)S(1)} %collective-permute-done.4.refs_5_), channel_id=1, source_target_pairs={{0,16},{16,0},{1,17},{17,1},{2,18},{18,2},{3,19},{19,3},{4,20},{20... | collective-permute-start | bytes 811016 | tf_op jit(solution)/shard_map/ppermute | solution.py:251
  62.1 18.9 %collective-permute-start.8 = (bf16[176,768]{1,0:T(8,128)(2,1)S(1)}, bf16[176,768]{1,0:T(8,128)(2,1)S(1)}, u32[]{:S(2)}, u32[]{:S(2)}) collective-permute-start(bf16[176,768]{1,0:T(8,128)(2,1)S(1)} %collective-permute-done.3.refs_4_), channel_id=1, source_target_pairs={{0,16},{16,0},{1,17},{17,1},{2,18},{18,2},{3,19},{19,3},{4,20},{20... | collective-permute-start | bytes 811016 | tf_op jit(solution)/shard_map/ppermute | solution.py:251
  63.6 22.3 %collective-permute-start.7 = (bf16[176,768]{1,0:T(8,128)(2,1)}, bf16[176,768]{1,0:T(8,128)(2,1)S(1)}, u32[]{:S(2)}, u32[]{:S(2)}) collective-permute-start(bf16[176,768]{1,0:T(8,128)(2,1)} %copy-done.22), channel_id=1, source_target_pairs={{0,16},{16,0},{1,17},{17,1},{2,18},{18,2},{3,19},{19,3},{4,20},{20... | collective-permute-start | bytes 811016 | tf_op jit(solution)/shard_map/ppermute | solution.py:251
  69.4 17.2 %copy-start.23 = (bf16[176,768]{1,0:T(8,128)(2,1)}, bf16[176,768]{1,0:T(8,128)(2,1)S(1)}, u32[]{:S(2)}) copy-start(bf16[176,768]{1,0:T(8,128)(2,1)S(1)} %collective-permute-done.6.refs_6_) | copy-start | bytes 811012
  75.2 11.4 %copy-start.24 = (bf16[176,768]{1,0:T(8,128)(2,1)}, bf16[176,768]{1,0:T(8,128)(2,1)S(1)}, u32[]{:S(2)}) copy-start(bf16[176,768]{1,0:T(8,128)(2,1)S(1)} %collective-permute-done.9.refs_9_) | copy-start | bytes 811012
  97.1 2.9 collective-permute-start.10
  98.1 171.5 %reduce-scatter.4.cloned.1.call-start = ((), (), s32[]{:S(2)}) async-start(), calls=%async_computation.8 | async-start | bytes 2621440 | tf_op jit(solution)/shard_map/reduce_scatter | solution.py:267
  98.1 25.8 %collective-permute-start.15 = (bf16[4,128,1024]{2,1,0:T(8,128)(2,1)}, bf16[4,128,1024]{2,1,0:T(8,128)(2,1)S(1)}, u32[]{:S(2)}, u32[]{:S(2)}) collective-permute-start(bf16[4,128,1024]{2,1,0:T(8,128)(2,1)} %bitcast.58), channel_id=1, source_target_pairs={{0,16},{16,0},{1,17},{17,1},{2,18},{18,2},{3,19},{19,3},{4,20},{20... | collective-permute-start | bytes 3145736 | tf_op jit(solution)/shard_map/ppermute | solution.py:251
  100.1 9.9 %copy-start.4 = (f32[256,1024]{1,0:T(8,128)}, f32[256,1024]{1,0:T(8,128)S(1)}, u32[]{:S(2)}) copy-start(f32[256,1024]{1,0:T(8,128)S(1)} %collective-permute-done.10.refs_2_) | copy-start | bytes 3145732
  101.5 8.4 %collective-permute-start.11 = (bf16[128,1024]{1,0:T(8,128)(2,1)S(1)}, bf16[128,1024]{1,0:T(8,128)(2,1)S(1)}, u32[]{:S(2)}, u32[]{:S(2)}) collective-permute-start(bf16[128,1024]{1,0:T(8,128)(2,1)S(1)} %fusion.17), channel_id=1, source_target_pairs={{0,8},{8,0},{1,9},{9,1},{2,10},{10,2},{3,11},{11,3},{4,12},{12,4},... | collective-permute-start | bytes 786440 | tf_op jit(solution)/shard_map/ppermute | solution.py:251
  114.1 7.8 %collective-permute-start.12 = (bf16[128,1024]{1,0:T(8,128)(2,1)}, bf16[128,1024]{1,0:T(8,128)(2,1)S(1)}, u32[]{:S(2)}, u32[]{:S(2)}) collective-permute-start(bf16[128,1024]{1,0:T(8,128)(2,1)} %get-tuple-element.71.refs_0_), channel_id=1, source_target_pairs={{0,8},{8,0},{1,9},{9,1},{2,10},{10,2},{3,11},{11,3},{4,12},{12,4},... | collective-permute-start | bytes 786440 | tf_op jit(solution)/shard_map/ppermute | solution.py:251
  115.4 6.4 %collective-permute-start.13 = (bf16[128,1024]{1,0:T(8,128)(2,1)}, bf16[128,1024]{1,0:T(8,128)(2,1)S(1)}, u32[]{:S(2)}, u32[]{:S(2)}) collective-permute-start(bf16[128,1024]{1,0:T(8,128)(2,1)} %get-tuple-element.71.refs_0_), channel_id=1, source_target_pairs={{0,4},{4,0},{1,5},{5,1},{2,6},{6,2},{3,7},{7,3},{8,12},{12,8},{9,1... | collective-permute-start | bytes 786440 | tf_op jit(solution)/shard_map/ppermute | solution.py:251
  121.8 2.1 collective-permute-start.14
  133.0 150.8 %reduce-scatter.6.cloned.1.call-start = ((), (), s32[]{:S(2)}) async-start(), calls=%async_computation.9 | async-start | bytes 1310720 | tf_op jit(solution)/shard_map/reduce_scatter | solution.py:267
  133.2 25.1 %collective-permute-start.16 = (bf16[512,1024]{1,0:T(8,128)(2,1)}, bf16[512,1024]{1,0:T(8,128)(2,1)S(1)}, u32[]{:S(2)}, u32[]{:S(2)}) collective-permute-start(bf16[512,1024]{1,0:T(8,128)(2,1)} %all-gather.5.cloned.1.call-done.refs_1_), channel_id=1, source_target_pairs={{0,16},{16,0},{1,17},{17,1},{2,18},{18,2},{3,19},{19,3},{4,20},{20... | collective-permute-start | bytes 3145736 | tf_op jit(solution)/shard_map/ppermute | solution.py:251
  167.9 7.1 %copy-start.5 = (f32[256,1024]{1,0:T(8,128)S(1)}, f32[256,1024]{1,0:T(8,128)}, u32[]{:S(2)}) copy-start(f32[256,1024]{1,0:T(8,128)} %get-tuple-element.78.refs_1_) | copy-start | bytes 3145732
  167.9 7.1 %collective-permute-start.17 = (f32[256,1024]{1,0:T(8,128)}, f32[256,1024]{1,0:T(8,128)S(1)}, u32[]{:S(2)}, u32[]{:S(2)}) collective-permute-start(f32[256,1024]{1,0:T(8,128)} %get-tuple-element.79), channel_id=1, source_target_pairs={{0,4},{4,0},{1,5},{5,1},{2,6},{6,2},{3,7},{7,3},{8,12},{12,8},{9,1... | collective-permute-start | bytes 3145736 | tf_op jit(solution)/shard_map/ppermute | solution.py:251
  173.4 33.7 %collective-permute-start.34 = (bf16[4,128,1024]{2,1,0:T(8,128)(2,1)}, bf16[4,128,1024]{2,1,0:T(8,128)(2,1)}, u32[]{:S(2)}, u32[]{:S(2)}) collective-permute-start(bf16[4,128,1024]{2,1,0:T(8,128)(2,1)} %get-tuple-element.82), channel_id=1, source_target_pairs={{0,16},{16,0},{1,17},{17,1},{2,18},{18,2},{3,19},{19,3},{4,20},{20... | collective-permute-start | bytes 3145736 | tf_op jit(solution)/shard_map/ppermute | solution.py:251
  175.0 8.5 %copy-start.6 = (f32[256,1024]{1,0:T(8,128)}, f32[256,1024]{1,0:T(8,128)S(1)}, u32[]{:S(2)}) copy-start(f32[256,1024]{1,0:T(8,128)S(1)} %collective-permute-done.17.refs_2_) | copy-start | bytes 3145732
  175.1 8.4 %collective-permute-start.18 = (bf16[128,1024]{1,0:T(8,128)(2,1)S(1)}, bf16[128,1024]{1,0:T(8,128)(2,1)S(1)}, u32[]{:S(2)}, u32[]{:S(2)}) collective-permute-start(bf16[128,1024]{1,0:T(8,128)(2,1)S(1)} %fusion.16), channel_id=1, source_target_pairs={{0,8},{8,0},{1,9},{9,1},{2,10},{10,2},{3,11},{11,3},{4,12},{12,4},... | collective-permute-start | bytes 786440 | tf_op jit(solution)/shard_map/ppermute | solution.py:251
  188.3 7.8 %collective-permute-start.19 = (bf16[128,1024]{1,0:T(8,128)(2,1)}, bf16[128,1024]{1,0:T(8,128)(2,1)S(1)}, u32[]{:S(2)}, u32[]{:S(2)}) collective-permute-start(bf16[128,1024]{1,0:T(8,128)(2,1)} %get-tuple-element.84.refs_0_), channel_id=1, source_target_pairs={{0,8},{8,0},{1,9},{9,1},{2,10},{10,2},{3,11},{11,3},{4,12},{12,4},... | collective-permute-start | bytes 786440 | tf_op jit(solution)/shard_map/ppermute | solution.py:251
  189.6 6.5 %collective-permute-start.20 = (bf16[128,1024]{1,0:T(8,128)(2,1)}, bf16[128,1024]{1,0:T(8,128)(2,1)S(1)}, u32[]{:S(2)}, u32[]{:S(2)}) collective-permute-start(bf16[128,1024]{1,0:T(8,128)(2,1)} %get-tuple-element.84.refs_0_), channel_id=1, source_target_pairs={{0,4},{4,0},{1,5},{5,1},{2,6},{6,2},{3,7},{7,3},{8,12},{12,8},{9,1... | collective-permute-start | bytes 786440 | tf_op jit(solution)/shard_map/ppermute | solution.py:251
  196.1 1.5 collective-permute-start.21
  198.4 8.8 %copy-start.7 = (f32[4,128,1024]{2,1,0:T(8,128)S(1)}, f32[4,128,1024]{2,1,0:T(8,128)}, u32[]{:S(2)}) copy-start(f32[4,128,1024]{2,1,0:T(8,128)} %get-tuple-element.112) | copy-start | bytes 6291460
  207.1 3.0 copy-start.1
  209.8 84.9 %reduce-scatter.8.cloned.1.call-start = ((), (), s32[]{:S(2)}) async-start(), calls=%async_computation.10 | async-start | bytes 327680 | tf_op jit(solution)/shard_map/reduce_scatter | solution.py:267
  224.9 33.9 %copy-start.14 = (f32[256,1024]{1,0:T(8,128)S(1)}, f32[256,1024]{1,0:T(8,128)}, u32[]{:S(2)}) copy-start(f32[256,1024]{1,0:T(8,128)} %get-tuple-element.97) | copy-start | bytes 3145732
  224.9 33.8 %collective-permute-start.24 = (f32[256,1024]{1,0:T(8,128)}, f32[256,1024]{1,0:T(8,128)S(1)}, u32[]{:S(2)}, u32[]{:S(2)}) collective-permute-start(f32[256,1024]{1,0:T(8,128)} %get-tuple-element.98), channel_id=1, source_target_pairs={{0,4},{4,0},{1,5},{5,1},{2,6},{6,2},{3,7},{7,3},{8,12},{12,8},{9,1... | collective-permute-start | bytes 3145736 | tf_op jit(solution)/shard_map/ppermute | solution.py:251
  225.1 32.9 %copy-start.19 = (f32[144,768]{1,0:T(8,128)S(1)}, f32[144,768]{1,0:T(8,128)}, u32[]{:S(2)}) copy-start(f32[144,768]{1,0:T(8,128)} %get-tuple-element.109) | copy-start | bytes 1327108
  225.1 8.5 %collective-permute-start.28 = (bf16[144,768]{1,0:T(8,128)(2,1)}, bf16[144,768]{1,0:T(8,128)(2,1)S(1)}, u32[]{:S(2)}, u32[]{:S(2)}) collective-permute-start(bf16[144,768]{1,0:T(8,128)(2,1)} %get-tuple-element.106), channel_id=1, source_target_pairs={{0,16},{16,0},{1,17},{17,1},{2,18},{18,2},{3,19},{19,3},{4,20},{20... | collective-permute-start | bytes 663560 | tf_op jit(solution)/shard_map/ppermute | solution.py:251
  226.4 33.1 %collective-permute-start.35 = (bf16[128,1024]{1,0:T(8,128)(2,1)}, bf16[128,1024]{1,0:T(8,128)(2,1)S(1)}, u32[]{:S(2)}, u32[]{:S(2)}) collective-permute-start(bf16[128,1024]{1,0:T(8,128)(2,1)} %get-tuple-element.86), channel_id=1, source_target_pairs={{0,16},{16,0},{1,17},{17,1},{2,18},{18,2},{3,19},{19,3},{4,20},{20... | collective-permute-start | bytes 786440 | tf_op jit(solution)/shard_map/ppermute | solution.py:251
  228.0 34.7 %collective-permute-start.22 = (f32[256,1024]{1,0:T(8,128)}, f32[256,1024]{1,0:T(8,128)}, u32[]{:S(2)}, u32[]{:S(2)}) collective-permute-start(f32[256,1024]{1,0:T(8,128)} %get-tuple-element.89), channel_id=1, source_target_pairs={{0,4},{4,0},{1,5},{5,1},{2,6},{6,2},{3,7},{7,3},{8,12},{12,8},{9,1... | collective-permute-start | bytes 3145736 | tf_op jit(solution)/shard_map/ppermute | solution.py:251
  228.0 55.7 %collective-permute-start.26 = (bf16[144,768]{1,0:T(8,128)(2,1)}, bf16[144,768]{1,0:T(8,128)(2,1)}, u32[]{:S(2)}, u32[]{:S(2)}) collective-permute-start(bf16[144,768]{1,0:T(8,128)(2,1)} %get-tuple-element.100), channel_id=1, source_target_pairs={{0,16},{16,0},{1,17},{17,1},{2,18},{18,2},{3,19},{19,3},{4,20},{20... | collective-permute-start | bytes 663560 | tf_op jit(solution)/shard_map/ppermute | solution.py:251
  233.6 14.5 %collective-permute-start.30 = (bf16[144,768]{1,0:T(8,128)(2,1)}, bf16[144,768]{1,0:T(8,128)(2,1)S(1)}, u32[]{:S(2)}, u32[]{:S(2)}) collective-permute-start(bf16[144,768]{1,0:T(8,128)(2,1)} %get-tuple-element.108), channel_id=1, source_target_pairs={{0,16},{16,0},{1,17},{17,1},{2,18},{18,2},{3,19},{19,3},{4,20},{20... | collective-permute-start | bytes 663560 | tf_op jit(solution)/shard_map/ppermute | solution.py:251
  248.2 7.1 %collective-permute-start.32 = (bf16[144,768]{1,0:T(8,128)(2,1)}, bf16[144,768]{1,0:T(8,128)(2,1)S(1)}, u32[]{:S(2)}, u32[]{:S(2)}) collective-permute-start(bf16[144,768]{1,0:T(8,128)(2,1)} %get-tuple-element.110), channel_id=1, source_target_pairs={{0,16},{16,0},{1,17},{17,1},{2,18},{18,2},{3,19},{19,3},{4,20},{20... | collective-permute-start | bytes 663560 | tf_op jit(solution)/shard_map/ppermute | solution.py:251
  248.7 17.9 %copy-start.16 = (f32[256,1024]{1,0:T(8,128)S(1)}, f32[256,1024]{1,0:T(8,128)}, u32[]{:S(2)}) copy-start(f32[256,1024]{1,0:T(8,128)} %get-tuple-element.88) | copy-start | bytes 3145732
  255.2 28.5 %collective-permute-start.29 = (bf16[144,768]{1,0:T(8,128)(2,1)}, bf16[144,768]{1,0:T(8,128)(2,1)}, u32[]{:S(2)}, u32[]{:S(2)}) collective-permute-start(bf16[144,768]{1,0:T(8,128)(2,1)} %add_convert_fusion.4), channel_id=1, source_target_pairs={{0,2},{1,3},{2,0},{3,1},{4,6},{5,7},{6,4},{7,5},{8,10},{9,11},{10,... | collective-permute-start | bytes 663560 | tf_op jit(solution)/shard_map/ppermute | solution.py:255
  258.8 25.0 %collective-permute-start.31 = (bf16[144,768]{1,0:T(8,128)(2,1)}, bf16[144,768]{1,0:T(8,128)(2,1)}, u32[]{:S(2)}, u32[]{:S(2)}) collective-permute-start(bf16[144,768]{1,0:T(8,128)(2,1)} %add_convert_fusion.3), channel_id=1, source_target_pairs={{0,1},{1,2},{2,3},{3,0},{4,5},{5,6},{6,7},{7,4},{8,9},{9,10},{10,1... | collective-permute-start | bytes 663560 | tf_op jit(solution)/shard_map/ppermute | solution.py:255
  259.6 8.8 %collective-permute-start.25 = (bf16[128,1024]{1,0:T(8,128)(2,1)}, bf16[128,1024]{1,0:T(8,128)(2,1)}, u32[]{:S(2)}, u32[]{:S(2)}) collective-permute-start(bf16[128,1024]{1,0:T(8,128)(2,1)} %fusion.9), channel_id=1, source_target_pairs={{0,8},{8,0},{1,9},{9,1},{2,10},{10,2},{3,11},{11,3},{4,12},{12,4},... | collective-permute-start | bytes 786440 | tf_op jit(solution)/shard_map/ppermute | solution.py:251
  262.7 21.1 %collective-permute-start.33 = (bf16[144,768]{1,0:T(8,128)(2,1)}, bf16[144,768]{1,0:T(8,128)(2,1)}, u32[]{:S(2)}, u32[]{:S(2)}) collective-permute-start(bf16[144,768]{1,0:T(8,128)(2,1)} %add_convert_fusion.2), channel_id=1, source_target_pairs={{0,3},{1,0},{2,1},{3,2},{4,7},{5,4},{6,5},{7,6},{8,11},{9,8},{10,9... | collective-permute-start | bytes 663560 | tf_op jit(solution)/shard_map/ppermute | solution.py:255
  270.6 6.4 %collective-permute-start.27 = (bf16[128,1024]{1,0:T(8,128)(2,1)S(1)}, bf16[128,1024]{1,0:T(8,128)(2,1)S(1)}, u32[]{:S(2)}, u32[]{:S(2)}) collective-permute-start(bf16[128,1024]{1,0:T(8,128)(2,1)S(1)} %dynamic-slice_bitcast_fusion), channel_id=1, source_target_pairs={{0,16},{16,0},{1,17},{17,1},{2,18},{18,2},{3,19},{19,3},{4,20},{20... | collective-permute-start | bytes 786440 | tf_op jit(solution)/shard_map/ppermute | solution.py:251
  277.0 15.7 %collective-permute-start.23 = (bf16[128,1024]{1,0:T(8,128)(2,1)}, bf16[128,1024]{1,0:T(8,128)(2,1)S(1)}, u32[]{:S(2)}, u32[]{:S(2)}) collective-permute-start(bf16[128,1024]{1,0:T(8,128)(2,1)} %fusion.12), channel_id=1, source_target_pairs={{0,8},{8,0},{1,9},{9,1},{2,10},{10,2},{3,11},{11,3},{4,12},{12,4},... | collective-permute-start | bytes 786440 | tf_op jit(solution)/shard_map/ppermute | solution.py:251
  283.8 8.9 %copy-start.8 = (f32[128,1024]{1,0:T(8,128)S(1)}, f32[128,1024]{1,0:T(8,128)}, u32[]{:S(2)}) copy-start(f32[128,1024]{1,0:T(8,128)} %get-tuple-element.70.refs_0_) | copy-start | bytes 1572868
  283.8 8.9 %copy-start.17 = (f32[256,1024]{1,0:T(8,128)S(1)}, f32[256,1024]{1,0:T(8,128)}, u32[]{:S(2)}) copy-start(f32[256,1024]{1,0:T(8,128)} %get-tuple-element.88) | copy-start | bytes 3145732
  287.2 13.0 %all-to-all-start.2 = ((bf16[4,96,768]{2,1,0:T(8,128)(2,1)}), bf16[4,96,768]{2,1,0:T(8,128)(2,1)S(1)}, u32[]{:S(2)}, u32[]{:S(2)}) async-start(bf16[4,96,768]{2,1,0:T(8,128)(2,1)} %shard_map.128), calls=%async_computation.4 | async-start | bytes 1179648 | tf_op jit(solution)/shard_map/all_to_all | solution.py:271
  (14 other events, 15.7 us)
Sparse Core Ops, SparseCore 0:
  57.7 28.1 all-gather.2
  98.2 28.3 all-gather.4
  133.1 43.8 reduce-scatter.3
  209.9 26.6 reduce-scatter.5
  262.8 19.8 reduce-scatter.7
